TPU v7x, 32 devices: a whole 2x2x4 slice. The times are simulated.
32 devices in a mesh: dp: 4 (over y, core), row: 4 (over z), view: 2 (over x).
Axes of the slice: x: 2, y: 2, z: 4, core: 2. Of those that a mesh axis runs over, the one named last changes fastest.
Arguments:
- frames_in: float32 [2, 4, 64, 16, 480], P('view', 'dp', None, 'row'), may hold values from -13 to 13
- cotangent: float32 [2, 4, 64, 16, 480], P('view', 'dp', None, 'row'), may hold values from -36 to 36
- expand_in: float32 [128, 64], replicated, may hold values from -0.75 to 0.75
- conv_kernel: float32 [128, 3, 3], replicated, may hold values from -2 to 2
- pool_proj: float32 [64, 64], replicated, may hold values from -1.5 to 1.5
- pool_bias: float32 [64], replicated, may hold values from 0.5 to 1.5
- squeeze_out: float32 [64, 64], replicated, may hold values from -0.75 to 0.75
- branch_scale: float32 [64], replicated, may hold values from 0.3 to 1
- ffn_expand: float32 [128, 64], replicated, may hold values from -0.75 to 0.75
- ffn_shrink: float32 [64, 64], replicated, may hold values from -0.75 to 0.75
- ffn_scale: float32 [64], replicated, may hold values from 0.3 to 1
- query_proj: float32 [2, 64, 64], P('view'), may hold values from -1.5 to 1.5
- value_proj: float32 [2, 64, 64], P('view'), may hold values from -0.75 to 0.75
- cross_scale: float32 [2, 64], P('view'), may hold values from 0.3 to 1
Outputs:
- block_out: float32 [2, 4, 64, 16, 480], P('view', 'dp', None, 'row')
- grad_in: float32 [2, 4, 64, 16, 480], P('view', 'dp', None, 'row')
- grad_expand: float32 [128, 64], replicated
- grad_kernel: float32 [128, 3, 3], replicated
- grad_pool: float32 [64, 64], replicated
- grad_bias: float32 [64], replicated
- grad_squeeze: float32 [64, 64], replicated
- grad_branch: float32 [64], replicated
- grad_ffn_up: float32 [128, 64], replicated
- grad_ffn_down: float32 [64, 64], replicated
- grad_ffn_scale: float32 [64], replicated
- grad_query: float32 [2, 64, 64], P('view')
- grad_value: float32 [2, 64, 64], P('view')
- grad_cross: float32 [2, 64], P('view')
All inputs are finite; a program needn't handle non-finite values.
Results may differ from a plain program's by a relative error of at most 0.0003.
Values sent between devices are 32-bit elements; how exact they have to be, the bound alone decides.
No kernel may reach another device: no remote copies, remote signals or barrier semaphores. Data moves between devices by JAX's collectives and lax.ppermute only.
A program may use at most 64 MiB of HBM per device.

v0:
```python
import jax
import jax.numpy as jnp
from jax import lax
from jax.sharding import PartitionSpec as P

epsilon = 1e-06
highest = lax.Precision.HIGHEST


def extended(value, sides, width):
    for axis, dim in sides:
        count, length = (lax.axis_size(axis), value.shape[dim])
        up = [(i, (i + 1) % count) for i in range(count - 1)]
        down = [(j, i) for i, j in up]
        last = lax.slice_in_dim(value, length - width, length, axis=dim)
        first = lax.slice_in_dim(value, 0, width, axis=dim)
        before = lax.ppermute(last, axis, up)
        after = lax.ppermute(first, axis, down)
        value = jnp.concatenate([before, value, after], axis=dim)
    return value


def partner(value, axis, distance):
    mask = 2**distance
    pairs = [(source, source ^ mask) for source in range(lax.axis_size(axis))]
    return lax.ppermute(value, axis, pairs)


def channel_norm(fields):
    center = fields - jnp.mean(fields, axis=-3, keepdims=True)
    spread = jnp.mean(center * center, axis=-3, keepdims=True)
    return center / jnp.sqrt(spread + epsilon)


def mixing(weight, fields):
    return jnp.einsum("oc,...chw->...ohw", weight, fields, precision=highest)


def depthwise(padded, kernel, height, breadth):
    summed = kernel[:, 0, 0][:, None, None] * padded[..., 0:height, 0:breadth]
    for offset in range(1, 9):
        row_off = offset // 3
        col_off = offset % 3
        summed = (
            summed
            + kernel[:, row_off, col_off][:, None, None]
            * padded[..., row_off : row_off + height, col_off : col_off + breadth]
        )
    return summed


def simple_gate(doubled):
    halves = doubled.shape[-3] // 2
    return doubled[..., :halves, :, :] * doubled[..., halves:, :, :]


def attend(hidden, queries, query_other, value_other, scales):
    scores = jnp.einsum(
        "...chi,...chj->...hij", queries, query_other, precision=highest
    ) * queries.shape[-3] ** (-0.5)
    weights = jnp.exp(scores)
    weights = weights / jnp.sum(weights, axis=-1, keepdims=True)
    carried = jnp.einsum("...hij,...chj->...chi", weights, value_other, precision=highest)
    return hidden + scales[:, None, None] * carried


def block_tail(
    frames,
    gating,
    pooled,
    pool_proj,
    pool_bias,
    squeeze_out,
    branch_scale,
    ffn_expand,
    ffn_shrink,
    ffn_scale,
):
    attention = jnp.einsum("oc,...c->...o", pool_proj, pooled, precision=highest) + pool_bias
    scaled = gating * attention[..., :, None, None]
    residual_one = frames + branch_scale[:, None, None] * mixing(squeeze_out, scaled)
    expanded = mixing(ffn_expand, channel_norm(residual_one))
    return residual_one + ffn_scale[:, None, None] * mixing(ffn_shrink, simple_gate(expanded))


def front_piece(frames, expand_in):
    return mixing(expand_in, channel_norm(frames))


def conv_piece(banded, conv_kernel):
    padded = jnp.pad(banded, ((0, 0), (0, 0), (0, 0), (1, 1)))
    return simple_gate(depthwise(padded, conv_kernel, banded.shape[2] - 2, banded.shape[3]))


def query_piece(hidden, query_proj):
    return mixing(query_proj, channel_norm(hidden))


def value_piece(hidden, value_proj):
    return mixing(value_proj, hidden)


def per_device(
    frames_in,
    cotangent,
    expand_in,
    conv_kernel,
    pool_proj,
    pool_bias,
    squeeze_out,
    branch_scale,
    ffn_expand,
    ffn_shrink,
    ffn_scale,
    query_proj,
    value_proj,
    cross_scale,
):
    frames = frames_in[0]
    upstream = cotangent[0]
    own_query = query_proj[0]
    own_value = value_proj[0]
    own_scale = cross_scale[0]
    height = frames.shape[2] * lax.axis_size("row")
    breadth = frames.shape[3]
    factor = (2 * frames.shape[0] * lax.axis_size("dp") * height * breadth) ** (-0.5)
    doubled, back_front = jax.vjp(front_piece, frames, expand_in)
    banded = extended(doubled, (("row", 2),), 1)
    gating, back_conv = jax.vjp(conv_piece, banded, conv_kernel)
    pooled = lax.psum(jnp.sum(gating, axis=(2, 3)), "row") / (height * breadth)
    hidden, back_tail = jax.vjp(
        block_tail,
        frames,
        gating,
        pooled,
        pool_proj,
        pool_bias,
        squeeze_out,
        branch_scale,
        ffn_expand,
        ffn_shrink,
        ffn_scale,
    )
    queries, back_query = jax.vjp(query_piece, hidden, own_query)
    values, back_value = jax.vjp(value_piece, hidden, own_value)
    query_other, value_other = partner((queries, values), "view", 0)
    output, back_attend = jax.vjp(attend, hidden, queries, query_other, value_other, own_scale)
    hidden_grad, query_grad, other_query_grad, other_value_grad, scale_grad = back_attend(upstream)
    query_back, value_back = partner((other_query_grad, other_value_grad), "view", 0)
    hidden_from_query, query_weight_grad = back_query(query_grad + query_back)
    hidden_from_value, value_weight_grad = back_value(value_back)
    hidden_total = hidden_grad + hidden_from_query + hidden_from_value
    tail_grads = back_tail(hidden_total)
    frames_grad_tail = tail_grads[0]
    gating_grad = tail_grads[1]
    pooled_grad = lax.psum(tail_grads[2], "row")
    gating_total = gating_grad + (pooled_grad / (height * breadth))[:, :, None, None]
    banded_grad, kernel_grad = back_conv(gating_total)
    border_rows = jnp.concatenate([banded_grad[:, :, :1], banded_grad[:, :, -1:]], axis=2)
    received = extended(border_rows, (("row", 2),), 1)
    doubled_grad = banded_grad[:, :, 1:-1]
    doubled_grad = doubled_grad.at[:, :, :1].add(received[:, :, :1])
    doubled_grad = doubled_grad.at[:, :, -1:].add(received[:, :, 3:])
    frames_grad_front, expand_grad = back_front(doubled_grad)
    frames_grad = frames_grad_tail + frames_grad_front
    shared = (
        expand_grad,
        kernel_grad,
        tail_grads[3],
        tail_grads[4],
        tail_grads[5],
        tail_grads[6],
        tail_grads[7],
        tail_grads[8],
        tail_grads[9],
    )
    owned = (query_weight_grad, value_weight_grad, scale_grad)
    slot_index = lax.axis_index("view")
    picks = (jnp.arange(2) == slot_index).astype(jnp.float32)
    widened = tuple(
        (picks.reshape((2,) + (1,) * grad_item.ndim) * grad_item[None] for grad_item in owned)
    )
    summed = lax.psum(shared + widened, ("dp", "row", "view"))
    shared = summed[:9]
    owned = tuple(
        (
            lax.dynamic_index_in_dim(grad_item, slot_index, 0, keepdims=False)
            for grad_item in summed[9:]
        )
    )
    shared_out = [grad_item * factor for grad_item in shared]
    owned_out = [grad_item[None] * factor for grad_item in owned]
    return (
        output[None],
        frames_grad[None],
        shared_out[0],
        shared_out[1],
        shared_out[2],
        shared_out[3],
        shared_out[4],
        shared_out[5],
        shared_out[6],
        shared_out[7],
        shared_out[8],
        owned_out[0],
        owned_out[1],
        owned_out[2],
    )


def solution(mesh):
    placed = (
        P("view", "dp", None, "row", None),
        P("view", "dp", None, "row", None),
        P(),
        P(),
        P(),
        P(),
        P(),
        P(),
        P(),
        P(),
        P(),
        P("view", None, None),
        P("view", None, None),
        P("view", None),
    )
    return jax.shard_map(
        per_device,
        mesh=mesh,
        in_specs=placed,
        out_specs=(
            P("view", "dp", None, "row", None),
            P("view", "dp", None, "row", None),
            P(),
            P(),
            P(),
            P(),
            P(),
            P(),
            P(),
            P(),
            P(),
            P("view", None, None),
            P("view", None, None),
            P("view", None),
        ),
        check_vma=False,
    )
```

profile of v0, /device:TPU:0, one launch (start us, length us, event | category | flops | bytes accessed | tf_op | source)
XLA Modules:
  0.0 308.0 jit_solution(11862306679924161565)
XLA Ops:
  7.2 1.2 reduce_sum.247
  8.4 1.2 multiply_reduce_fusion.15
  10.3 1.1 fusion.46
  11.4 2.5 convolution_bitcast_fusion.3
  13.9 1.3 collective-permute-start.1
  15.2 5.6 %collective-permute-start = (f32[1,128,1,480]{1,3,2,0:T(8,128)S(1)}, f32[1,128,1,480]{1,3,2,0:T(8,128)S(1)}, u32[]{:S(2)}, u32[]{:S(2)}) collective-permute-start(f32[1,128,1,480]{1,3,2,0:T(8,128)S(1)} %get-tuple-element.100), channel_id=1, source_target_pairs={{0,2},{2,4},{4,6},{1,3},{3,5},{5,7},{8,10},{10,12},{12,14},{9,11},... | collective-permute-start | bytes 737288 | tf_op jit(solution)/shard_map/ppermute | solution.py:17
  21.0 3.9 %collective-permute-done.1 = f32[1,128,1,480]{1,3,2,0:T(8,128)S(1)} collective-permute-done((f32[1,128,1,480]{1,3,2,0:T(8,128)S(1)}, f32[1,128,1,480]{1,3,2,0:T(8,128)S(1)}, u32[]{:S(2)}, u32[]{:S(2)}) %collective-permute-start.1) | collective-permute-done | bytes 245792 | tf_op jit(solution)/shard_map/ppermute | solution.py:18
  24.9 1.2 collective-permute-done
  27.0 1.8 fusion.96
  28.8 13.6 %psum.98 = f32[1,64]{1,0:T(1,128)} all-reduce(f32[1,64]{1,0:T(1,128)} %bitcast.369), channel_id=1, replica_groups=mesh['dp'=4,'row'=4,'view'=2] {'row'}, use_global_device_ids=true, to_apply=%region_3.4 | all-reduce | flops 64 | bytes 512 | tf_op jit(solution)/shard_map/psum | solution.py:130
  42.4 0.9 fusion.8
  43.4 3.4 %fusion.95 = (f32[4,480]{1,0:T(4,128)S(1)}, f32[1,64,4,480]{3,1,2,0:T(8,128)S(1)}, f32[1,64,4,480]{3,1,2,0:T(8,128)}) fusion(f32[64]{0:T(128)S(1)} %copy-done.48, f32[1,1,64,4,480]{4,3,2,1,0:T(4,128)S(1)} %copy-done.1, f32[64,64]{1,0:T(8,128)} %param.24, f32[1,64,4,480]{1,3,2,0:T(8,128)} %get-tuple-element.84, f32[64]{0:T(128)S(1)} %fusion.8), kind=kOutput, calls=%fused_computation.225 | convolution fusion | flops 94861440 | bytes 1990656 | tf_op jit(solution)/shard_map/jvp(oc,...chw->...ohw)/dot_general | solution.py:36
  46.9 0.7 multiply_divide_fusion.1
  48.2 2.5 convolution_bitcast_fusion.2
  50.7 3.0 fusion.94
  54.5 1.5 fusion.38
  56.0 1.6 collective-permute-start.3
  57.5 0.9 divide_bitcast_fusion
  59.0 1.7 convolution_bitcast_fusion.10
  61.2 1.2 multiply_bitcast_fusion.1
  62.5 8.7 %collective-permute-done.3 = f32[1,64,4,480]{3,1,2,0:T(8,128)} collective-permute-done((f32[1,64,4,480]{3,1,2,0:T(8,128)}, f32[1,64,4,480]{3,1,2,0:T(8,128)}, u32[]{:S(2)}, u32[]{:S(2)}) %collective-permute-start.3) | collective-permute-done | bytes 491552 | tf_op jit(solution)/shard_map/ppermute | solution.py:26
  71.1 4.9 %fusion.1 = (f32[4,480]{1,0:T(4,128)S(1)}, f32[4,480,480]{1,2,0:T(8,128)S(1)}) fusion(f32[1,64,4,480]{3,1,2,0:T(8,128)} %collective-permute-done.3, f32[4,480,64]{1,2,0:T(8,128)} %fusion.38), kind=kOutput, calls=%fused_computation.4 | convolution fusion | flops 709630080 | bytes 4677120 | tf_op jit(solution)/shard_map/jvp(...chi,...chj->...hij)/dot_general | solution.py:58
  76.0 2.0 collective-permute-done.2
  78.0 4.2 %multiply_reduce_fusion = (f32[4,480]{1,0:T(4,128)S(1)}, f32[4,480,480]{1,2,0:T(8,128)S(1)}) fusion(f32[4,480,480]{1,2,0:T(8,128)S(1)} %get-tuple-element.126, f32[4,480]{1,0:T(4,128)S(1)} %multiply_divide_fusion.3, f32[1,64,4,480]{3,1,2,0:T(8,128)S(1)} %collective-permute-done.2, f32[1,1,64,4,480]{4,3,2,1,0:T(4,128)S(1)} %copy-done.18, f32[64]{0:T(128)S(1)} %bitcast.366), kind=kOutput, calls=%fused_computation.1 | convolution fusion | flops 711596160 | bytes 8371456 | tf_op jit(solution)/shard_map/transpose(jvp(...hij,...chj->...chi))/dot_general | solution.py:63
  82.2 5.7 %convolution_bitcast_fusion.7 = f32[1,64,4,480]{3,1,2,0:T(8,128)S(1)} fusion(f32[4,480,64]{1,2,0:T(8,128)} %fusion.38, f32[4,480,480]{1,2,0:T(8,128)S(1)} %get-tuple-element.128, f32[4,480,480]{1,2,0:T(8,128)S(1)} %get-tuple-element.126, f32[4,480]{1,0:T(4,128)S(1)} %neg.37, f32[4,480]{1,0:T(4,128)S(1)} %get-tuple-element.125), kind=kOutput, calls=%fused_computation.18 | convolution fusion | flops 712396800 | bytes 8371200 | tf_op jit(solution)/shard_map/transpose(jvp(...chi,...chj->...hij))/dot_general | solution.py:58
  87.9 1.6 collective-permute-start.4
  89.5 4.1 %convolution_bitcast_fusion.5 = f32[1,64,4,480]{3,1,2,0:T(8,128)S(1)} fusion(f32[4,480,480]{1,2,0:T(8,128)S(1)} %get-tuple-element.126, f32[4,480]{1,0:T(4,128)S(1)} %get-tuple-element.125, f32[1,1,64,4,480]{4,3,2,1,0:T(4,128)S(1)} %copy-done.18, f32[64]{0:T(128)S(1)} %bitcast.367), kind=kOutput, calls=%fused_computation.16 | convolution fusion | flops 709754880 | bytes 4677376 | tf_op jit(solution)/shard_map/transpose(jvp(...hij,...chj->...chi))/dot_general | solution.py:63
  94.3 8.5 %collective-permute-done.4 = f32[1,64,4,480]{3,1,2,0:T(8,128)S(1)} collective-permute-done((f32[1,64,4,480]{3,1,2,0:T(8,128)S(1)}, f32[1,64,4,480]{3,1,2,0:T(8,128)S(1)}, u32[]{:S(2)}, u32[]{:S(2)}) %collective-permute-start.4) | collective-permute-done | bytes 491552 | tf_op jit(solution)/shard_map/ppermute | solution.py:26
  102.8 4.7 %fusion.4 = f32[4,480,64]{1,2,0:T(8,128)S(1)} fusion(f32[1,64,4,480]{3,1,2,0:T(8,128)S(1)} %collective-permute-done.4, f32[1,64,4,480]{3,1,2,0:T(8,128)} %collective-permute-done.3, f32[4,480,480]{1,2,0:T(8,128)S(1)} %get-tuple-element.128, f32[4,480,480]{1,2,0:T(8,128)S(1)} %get-tuple-element.126, f32[4,480]{1,0:T(4,128)S(1)} %neg.37, ...), kind=kOutput, calls=%fused_computation.27 | convolution fusion | flops 712519680 | bytes 8862720 | tf_op jit(solution)/shard_map/transpose(jvp(...chi,...chj->...hij))/dot_general | solution.py:58
  107.6 0.7 fusion.30
  108.4 4.6 %fusion.34 = (f32[64]{0:T(128)}, f32[1,1,64,4,480]{4,2,3,1,0:T(8,128)}, f32[4,480]{1,0:T(4,128)S(1)}) fusion(f32[1,1,64,4,480]{4,3,2,1,0:T(4,128)S(1)} %copy-done.18, f32[1,64,4,480]{3,1,2,0:T(8,128)S(1)} %copy-done.9, f32[64]{0:T(128)S(1)} %bitcast.368, f32[4,480]{1,0:T(4,128)S(1)} %multiply_multiply_fusion.3, f32[4,480]{1,0:T(4,128)S(1)} %copy-done.28, ...), kind=kOutput, calls=%fused_computation.93 | convolution fusion | flops 710858816 | bytes 6182912 | tf_op jit(solution)/shard_map/jvp(...hij,...chj->...chi)/dot_general | solution.py:63
  113.0 0.8 fusion.5
  113.8 2.0 slice_multiply_fusion.2
  115.8 1.7 convolution_bitcast_fusion.15
  117.5 1.2 convolution_bitcast_fusion.20
  118.7 1.8 convolution_bitcast_fusion.16
  120.6 1.6 fusion.26
  122.4 0.9 multiply_reduce_fusion.12
  123.3 3.0 multiply_reduce_fusion.10
  126.4 8.9 %psum.99 = f32[1,64]{1,0:T(1,128)} all-reduce(f32[1,64]{1,0:T(1,128)S(1)} %fusion.81), channel_id=1, replica_groups=mesh['dp'=4,'row'=4,'view'=2] {'row'}, use_global_device_ids=true, to_apply=%region_15.16 | all-reduce | flops 64 | bytes 512 | tf_op jit(solution)/shard_map/psum | solution.py:156
  135.3 0.7 multiply_bitcast_fusion
  136.1 1.5 slice_multiply_fusion.5
  137.7 0.9 multiply_reduce_fusion.9
  138.7 1.0 broadcast_multiply_fusion
  139.8 0.7 pad_add_fusion
  140.6 4.0 %collective-permute-start.6 = (f32[1,128,1,480]{1,3,2,0:T(8,128)S(1)}, f32[1,128,1,480]{1,3,2,0:T(8,128)S(1)}, u32[]{:S(2)}, u32[]{:S(2)}) collective-permute-start(f32[1,128,1,480]{1,3,2,0:T(8,128)S(1)} %get-tuple-element.90), channel_id=1, source_target_pairs={{0,2},{2,4},{4,6},{1,3},{3,5},{5,7},{8,10},{10,12},{12,14},{9,11},... | collective-permute-start | bytes 737288 | tf_op jit(solution)/shard_map/ppermute | solution.py:17
  144.6 1.3 collective-permute-start.7
  145.9 0.7 broadcast_multiply_fusion.14
  147.9 0.7 broadcast_multiply_fusion.9
  148.6 1.6 convolution_bitcast_fusion.17
  150.9 1.1 copy.46
  152.0 0.7 collective-permute-done.7
  152.8 1.4 fusion.25
  154.5 1.7 convolution_bitcast_fusion.18
  156.5 1.1 copy.47
  157.6 132.7 %all-reduce.26.cloned.1.call-done = (f32[128,64]{0,1:T(8,128)}, f32[128,3,3]{0,2,1:T(4,128)}, f32[64,64]{1,0:T(8,128)}, f32[64]{0:T(128)}, f32[64,64]{1,0:T(8,12...) async-done(((f32[128,64]{0,1:T(8,128)}, ...) | async-done | bytes 186128 | tf_op jit(solution)/shard_map/psum | solution.py:183
  290.4 1.3 broadcast_multiply_fusion.20
  291.6 1.4 broadcast_multiply_fusion.13
  293.0 1.1 broadcast_multiply_fusion.24
  294.1 1.4 broadcast_multiply_fusion.15
  295.6 1.4 broadcast_multiply_fusion.11
  297.0 1.2 broadcast_multiply_fusion.22
  298.1 1.2 fusion.80
  299.3 1.4 dynamic-slice_multiply_fusion
  (187 shorter events, 7.9 us)
Async XLA Ops:
  7.2 43.5 %copy-start = (f32[64,64]{1,0:T(8,128)S(1)}, f32[64,64]{1,0:T(8,128)}, u32[]{:S(2)}) copy-start(f32[64,64]{1,0:T(8,128)} %param.27) | copy-start | bytes 49156
  7.2 13.7 %copy-start.70 = (f32[128,3,3]{0,2,1:T(4,128)S(1)}, f32[128,3,3]{0,2,1:T(4,128)}, u32[]{:S(2)}) copy-start(f32[128,3,3]{0,2,1:T(4,128)} %param.21) | copy-start | bytes 13828
  7.2 283.1 %all-reduce.26.cloned.1.call-start = ((), (), s32[]{:S(2)}) async-start(), calls=%async_computation | async-start | bytes 607232 | tf_op jit(solution)/shard_map/psum | solution.py:183
  13.9 13.0 %copy-start.2 = (f32[1,128,4,480]{1,3,2,0:T(8,128)}, f32[1,128,4,480]{1,3,2,0:T(8,128)S(1)}, u32[]{:S(2)}) copy-start(f32[1,128,4,480]{1,3,2,0:T(8,128)S(1)} %convolution_bitcast_fusion.3) | copy-start | bytes 2949124
  13.9 10.9 %collective-permute-start.1 = (f32[1,128,1,480]{1,3,2,0:T(8,128)S(1)}, f32[1,128,1,480]{1,3,2,0:T(8,128)S(1)}, u32[]{:S(2)}, u32[]{:S(2)}) collective-permute-start(f32[1,128,1,480]{1,3,2,0:T(8,128)S(1)} %get-tuple-element.101), channel_id=1, source_target_pairs={{2,0},{4,2},{6,4},{3,1},{5,3},{7,5},{10,8},{12,10},{14,12},{11,9},... | collective-permute-start | bytes 737288 | tf_op jit(solution)/shard_map/ppermute | solution.py:18
  15.2 10.8 %collective-permute-start = (f32[1,128,1,480]{1,3,2,0:T(8,128)S(1)}, f32[1,128,1,480]{1,3,2,0:T(8,128)S(1)}, u32[]{:S(2)}, u32[]{:S(2)}) collective-permute-start(f32[1,128,1,480]{1,3,2,0:T(8,128)S(1)} %get-tuple-element.100), channel_id=1, source_target_pairs={{0,2},{2,4},{4,6},{1,3},{3,5},{5,7},{8,10},{10,12},{12,14},{9,11},... | collective-permute-start | bytes 737288 | tf_op jit(solution)/shard_map/ppermute | solution.py:17
  20.9 6.0 %copy-start.51 = (f32[128]{0:T(128)}, f32[128]{0:T(128)S(1)}, u32[]{:S(2)}) copy-start(f32[128]{0:T(128)S(1)} %get-tuple-element.112) | copy-start | bytes 1540
  20.9 6.0 %copy-start.53 = (f32[128]{0:T(128)}, f32[128]{0:T(128)S(1)}, u32[]{:S(2)}) copy-start(f32[128]{0:T(128)S(1)} %get-tuple-element.113) | copy-start | bytes 1540
  20.9 6.0 %copy-start.55 = (f32[128]{0:T(128)}, f32[128]{0:T(128)S(1)}, u32[]{:S(2)}) copy-start(f32[128]{0:T(128)S(1)} %get-tuple-element.114) | copy-start | bytes 1540
  20.9 6.0 %copy-start.57 = (f32[128]{0:T(128)}, f32[128]{0:T(128)S(1)}, u32[]{:S(2)}) copy-start(f32[128]{0:T(128)S(1)} %get-tuple-element.115) | copy-start | bytes 1540
  20.9 6.0 %copy-start.59 = (f32[128]{0:T(128)}, f32[128]{0:T(128)S(1)}, u32[]{:S(2)}) copy-start(f32[128]{0:T(128)S(1)} %get-tuple-element.116) | copy-start | bytes 1540
  20.9 6.0 %copy-start.61 = (f32[128]{0:T(128)}, f32[128]{0:T(128)S(1)}, u32[]{:S(2)}) copy-start(f32[128]{0:T(128)S(1)} %get-tuple-element.117) | copy-start | bytes 1540
  20.9 6.0 %copy-start.63 = (f32[128]{0:T(128)}, f32[128]{0:T(128)S(1)}, u32[]{:S(2)}) copy-start(f32[128]{0:T(128)S(1)} %get-tuple-element.118) | copy-start | bytes 1540
  21.0 6.0 %copy-start.65 = (f32[128]{0:T(128)}, f32[128]{0:T(128)S(1)}, u32[]{:S(2)}) copy-start(f32[128]{0:T(128)S(1)} %get-tuple-element.119) | copy-start | bytes 1540
  21.0 6.0 %copy-start.67 = (f32[128]{0:T(128)}, f32[128]{0:T(128)S(1)}, u32[]{:S(2)}) copy-start(f32[128]{0:T(128)S(1)} %get-tuple-element.120) | copy-start | bytes 1540
  26.2 17.1 %copy-start.1 = (f32[1,1,64,4,480]{4,3,2,1,0:T(4,128)S(1)}, f32[1,1,64,4,480]{4,3,2,1,0:T(4,128)}, u32[]{:S(2)}) copy-start(f32[1,1,64,4,480]{4,3,2,1,0:T(4,128)} %param.18) | copy-start | bytes 1474564
  26.2 17.1 %copy-start.48 = (f32[64]{0:T(128)S(1)}, f32[64]{0:T(128)}, u32[]{:S(2)}) copy-start(f32[64]{0:T(128)} %param.25) | copy-start | bytes 772
  43.3 3.5 %copy-start.46 = (f32[64]{0:T(128)}, f32[64]{0:T(128)S(1)}, u32[]{:S(2)}) copy-start(f32[64]{0:T(128)S(1)} %fusion.8) | copy-start | bytes 772
  43.3 11.1 %copy-start.39 = (f32[1,64,64]{2,1,0:T(8,128)S(1)}, f32[1,64,64]{2,1,0:T(8,128)}, u32[]{:S(2)}) copy-start(f32[1,64,64]{2,1,0:T(8,128)} %param.29) | copy-start | bytes 49156
  46.8 11.6 %copy-start.4 = (f32[1,64,4,480]{3,1,2,0:T(8,128)}, f32[1,64,4,480]{3,1,2,0:T(8,128)S(1)}, u32[]{:S(2)}) copy-start(f32[1,64,4,480]{3,1,2,0:T(8,128)S(1)} %get-tuple-element.82) | copy-start | bytes 1474564
  50.7 5.3 %copy-start.11 = (f32[1,128,4,480]{1,3,2,0:T(8,128)}, f32[1,128,4,480]{1,3,2,0:T(8,128)S(1)}, u32[]{:S(2)}) copy-start(f32[1,128,4,480]{1,3,2,0:T(8,128)S(1)} %convolution_bitcast_fusion.2) | copy-start | bytes 2949124
  54.5 3.1 copy-start.44
  56.0 15.2 %collective-permute-start.3 = (f32[1,64,4,480]{3,1,2,0:T(8,128)}, f32[1,64,4,480]{3,1,2,0:T(8,128)}, u32[]{:S(2)}, u32[]{:S(2)}) collective-permute-start(f32[1,64,4,480]{3,1,2,0:T(8,128)} %bitcast.43), channel_id=1, source_target_pairs={{0,1},{1,0},{2,3},{3,2},{4,5},{5,4},{6,7},{7,6},{8,9},{9,8},{10,11... | collective-permute-start | bytes 1474568 | tf_op jit(solution)/shard_map/ppermute | solution.py:26
  58.4 19.6 %copy-start.18 = (f32[1,1,64,4,480]{4,3,2,1,0:T(4,128)S(1)}, f32[1,1,64,4,480]{4,3,2,1,0:T(4,128)}, u32[]{:S(2)}) copy-start(f32[1,1,64,4,480]{4,3,2,1,0:T(4,128)} %param.19) | copy-start | bytes 1474564
  58.4 19.6 %copy-start.72 = (f32[1,64]{1,0:T(1,128)S(1)}, f32[1,64]{1,0:T(1,128)}, u32[]{:S(2)}) copy-start(f32[1,64]{1,0:T(1,128)} %param.31) | copy-start | bytes 772
  60.6 17.3 %collective-permute-start.2 = (f32[1,64,4,480]{3,1,2,0:T(8,128)S(1)}, f32[1,64,4,480]{3,1,2,0:T(8,128)S(1)}, u32[]{:S(2)}, u32[]{:S(2)}) collective-permute-start(f32[1,64,4,480]{3,1,2,0:T(8,128)S(1)} %convolution_bitcast_fusion.10), channel_id=1, source_target_pairs={{0,1},{1,0},{2,3},{3,2},{4,5},{5,4},{6,7},{7,6},{8,9},{9,8},{10,11... | collective-permute-start | bytes 1474568 | tf_op jit(solution)/shard_map/ppermute | solution.py:26
  87.9 14.9 %collective-permute-start.4 = (f32[1,64,4,480]{3,1,2,0:T(8,128)S(1)}, f32[1,64,4,480]{3,1,2,0:T(8,128)S(1)}, u32[]{:S(2)}, u32[]{:S(2)}) collective-permute-start(f32[1,64,4,480]{3,1,2,0:T(8,128)S(1)} %convolution_bitcast_fusion.7), channel_id=1, source_target_pairs={{0,1},{1,0},{2,3},{3,2},{4,5},{5,4},{6,7},{7,6},{8,9},{9,8},{10,11... | collective-permute-start | bytes 1474568 | tf_op jit(solution)/shard_map/ppermute | solution.py:26
  93.6 13.9 %copy-start.9 = (f32[1,64,4,480]{3,1,2,0:T(8,128)S(1)}, f32[1,64,4,480]{3,1,2,0:T(8,128)}, u32[]{:S(2)}) copy-start(f32[1,64,4,480]{3,1,2,0:T(8,128)} %copy-done.8) | copy-start | bytes 1474564
  93.6 13.9 %copy-start.28 = (f32[4,480]{1,0:T(4,128)S(1)}, f32[4,480]{1,0:T(4,128)}, u32[]{:S(2)}) copy-start(f32[4,480]{1,0:T(4,128)} %copy-done.27) | copy-start | bytes 23044
  93.6 13.9 %copy-start.38 = (f32[4,480]{1,0:T(4,128)S(1)}, f32[4,480]{1,0:T(4,128)}, u32[]{:S(2)}) copy-start(f32[4,480]{1,0:T(4,128)} %get-tuple-element.110) | copy-start | bytes 23044
  93.6 13.9 %copy-start.40 = (f32[1,64,64]{2,1,0:T(8,128)S(1)}, f32[1,64,64]{2,1,0:T(8,128)}, u32[]{:S(2)}) copy-start(f32[1,64,64]{2,1,0:T(8,128)} %param.29) | copy-start | bytes 49156
  93.7 14.6 %copy-start.34 = (f32[4,480]{1,0:T(4,128)S(1)}, f32[4,480]{1,0:T(4,128)}, u32[]{:S(2)}) copy-start(f32[4,480]{1,0:T(4,128)} %copy-done.33) | copy-start | bytes 23044
  93.7 14.7 %copy-start.45 = (f32[4,480]{1,0:T(4,128)S(1)}, f32[4,480]{1,0:T(4,128)}, u32[]{:S(2)}) copy-start(f32[4,480]{1,0:T(4,128)} %copy-done.44) | copy-start | bytes 23044
  93.7 19.3 %collective-permute-start.5 = (f32[1,64,4,480]{3,1,2,0:T(8,128)S(1)}, f32[1,64,4,480]{3,1,2,0:T(8,128)S(1)}, u32[]{:S(2)}, u32[]{:S(2)}) collective-permute-start(f32[1,64,4,480]{3,1,2,0:T(8,128)S(1)} %convolution_bitcast_fusion.5), channel_id=1, source_target_pairs={{0,1},{1,0},{2,3},{3,2},{4,5},{5,4},{6,7},{7,6},{8,9},{9,8},{10,11... | collective-permute-start | bytes 1474568 | tf_op jit(solution)/shard_map/ppermute | solution.py:26
  108.3 4.6 %copy-start.41 = (f32[1,64,64]{2,1,0:T(8,128)S(1)}, f32[1,64,64]{2,1,0:T(8,128)}, u32[]{:S(2)}) copy-start(f32[1,64,64]{2,1,0:T(8,128)} %param.30) | copy-start | bytes 49156
  108.3 5.5 %copy-start.12 = (f32[1,128,4,480]{1,3,2,0:T(8,128)S(1)}, f32[1,128,4,480]{1,3,2,0:T(8,128)}, u32[]{:S(2)}) copy-start(f32[1,128,4,480]{1,3,2,0:T(8,128)} %copy-done.11) | copy-start | bytes 2949124
  108.4 5.5 %copy-start.69 = (f32[64]{0:T(128)S(1)}, f32[64]{0:T(128)}, u32[]{:S(2)}) copy-start(f32[64]{0:T(128)} %param.28) | copy-start | bytes 772
  112.9 5.8 %copy-start.20 = (f32[1,64,4,480]{3,1,2,0:T(8,128)}, f32[1,64,4,480]{3,1,2,0:T(8,128)S(1)}, u32[]{:S(2)}) copy-start(f32[1,64,4,480]{3,1,2,0:T(8,128)S(1)} %collective-permute-done.5) | copy-start | bytes 1474564
  113.8 4.9 %copy-start.5 = (f32[1,64,4,480]{3,1,2,0:T(8,128)S(1)}, f32[1,64,4,480]{3,1,2,0:T(8,128)}, u32[]{:S(2)}) copy-start(f32[1,64,4,480]{3,1,2,0:T(8,128)} %copy-done.4) | copy-start | bytes 1474564
  113.8 4.9 %copy-start.26 = (f32[4,480]{1,0:T(4,128)S(1)}, f32[4,480]{1,0:T(4,128)}, u32[]{:S(2)}) copy-start(f32[4,480]{1,0:T(4,128)} %copy-done.25) | copy-start | bytes 23044
  115.8 4.7 %copy-start.35 = (f32[128,64]{0,1:T(8,128)S(1)}, f32[128,64]{0,1:T(8,128)}, u32[]{:S(2)}) copy-start(f32[128,64]{0,1:T(8,128)} %param.26) | copy-start | bytes 98308
  115.8 4.7 %copy-start.37 = (f32[4,480]{1,0:T(4,128)S(1)}, f32[4,480]{1,0:T(4,128)}, u32[]{:S(2)}) copy-start(f32[4,480]{1,0:T(4,128)} %get-tuple-element.108) | copy-start | bytes 23044
  117.5 4.7 %copy-start.32 = (f32[4,480]{1,0:T(4,128)S(1)}, f32[4,480]{1,0:T(4,128)}, u32[]{:S(2)}) copy-start(f32[4,480]{1,0:T(4,128)} %copy-done.31) | copy-start | bytes 23044
  118.7 3.6 %copy-start.16 = (f32[1,64,4,480]{3,1,2,0:T(8,128)S(1)}, f32[1,64,4,480]{3,1,2,0:T(8,128)}, u32[]{:S(2)}) copy-start(f32[1,64,4,480]{3,1,2,0:T(8,128)} %get-tuple-element.123) | copy-start | bytes 1474564
  118.7 3.7 %copy-start.17 = (f32[1,64,4,480]{3,1,2,0:T(8,128)S(1)}, f32[1,64,4,480]{3,1,2,0:T(8,128)}, u32[]{:S(2)}) copy-start(f32[1,64,4,480]{3,1,2,0:T(8,128)} %get-tuple-element.124) | copy-start | bytes 1474564
  122.2 4.2 %copy-start.24 = (f32[64,64]{1,0:T(8,128)S(1)}, f32[64,64]{1,0:T(8,128)}, u32[]{:S(2)}) copy-start(f32[64,64]{1,0:T(8,128)} %param.22) | copy-start | bytes 49156
  126.3 19.6 %copy-start.43 = (f32[64]{0:T(128)}, f32[64]{0:T(128)S(1)}, u32[]{:S(2)}) copy-start(f32[64]{0:T(128)S(1)} %get-tuple-element.133) | copy-start | bytes 772
  139.7 6.2 %copy-start.73 = (f32[64]{0:T(128)S(1)}, f32[64]{0:T(128)}, u32[]{:S(2)}) copy-start(f32[64]{0:T(128)} %multiply_bitcast_fusion.1) | copy-start | bytes 772
  139.7 6.9 %copy-start.71 = (f32[2]{0:T(128)S(1)}, f32[2]{0:T(128)}, u32[]{:S(2)}) copy-start(f32[2]{0:T(128)} %compare_convert_fusion) | copy-start | bytes 28
  139.8 6.9 %copy-start.74 = (f32[64]{0:T(128)S(1)}, f32[64]{0:T(128)}, u32[]{:S(2)}) copy-start(f32[64]{0:T(128)} %get-tuple-element.102) | copy-start | bytes 772
  139.8 7.5 %copy-start.10 = (f32[1,64,4,480]{3,1,2,0:T(8,128)S(1)}, f32[1,64,4,480]{3,1,2,0:T(8,128)}, u32[]{:S(2)}) copy-start(f32[1,64,4,480]{3,1,2,0:T(8,128)} %copy-done.8) | copy-start | bytes 1474564
  139.8 7.5 %copy-start.21 = (f32[1,64,4,480]{3,1,2,0:T(8,128)S(1)}, f32[1,64,4,480]{3,1,2,0:T(8,128)}, u32[]{:S(2)}) copy-start(f32[1,64,4,480]{3,1,2,0:T(8,128)} %copy-done.20) | copy-start | bytes 1474564
  139.8 8.1 %copy-start.42 = (f32[64,64]{1,0:T(8,128)S(1)}, f32[64,64]{1,0:T(8,128)}, u32[]{:S(2)}) copy-start(f32[64,64]{1,0:T(8,128)} %convolution_bitcast_fusion.20) | copy-start | bytes 49156
  139.8 8.8 %copy-start.7 = (f32[1,64,4,480]{1,3,2,0:T(8,128)S(1)}, f32[1,64,4,480]{1,3,2,0:T(8,128)}, u32[]{:S(2)}) copy-start(f32[1,64,4,480]{1,3,2,0:T(8,128)} %get-tuple-element.84) | copy-start | bytes 1474564
  139.8 8.8 %copy-start.14 = (f32[1,64,4,480]{3,1,2,0:T(8,128)S(1)}, f32[1,64,4,480]{3,1,2,0:T(8,128)}, u32[]{:S(2)}) copy-start(f32[1,64,4,480]{3,1,2,0:T(8,128)} %copy-done.13) | copy-start | bytes 1474564
  139.8 8.8 %copy-start.47 = (f32[64]{0:T(128)S(1)}, f32[64]{0:T(128)}, u32[]{:S(2)}) copy-start(f32[64]{0:T(128)} %copy-done.46) | copy-start | bytes 772
  139.8 8.8 %copy-start.50 = (f32[64]{0:T(128)S(1)}, f32[64]{0:T(128)}, u32[]{:S(2)}) copy-start(f32[64]{0:T(128)} %param.25) | copy-start | bytes 772
  140.5 10.3 %copy-start.19 = (f32[1,1,64,4,480]{4,2,3,1,0:T(8,128)S(1)}, f32[1,1,64,4,480]{4,2,3,1,0:T(8,128)}, u32[]{:S(2)}) copy-start(f32[1,1,64,4,480]{4,2,3,1,0:T(8,128)} %get-tuple-element.103) | copy-start | bytes 1474564
  140.6 12.2 %copy-start.23 = (f32[128,64]{0,1:T(8,128)S(1)}, f32[128,64]{0,1:T(8,128)}, u32[]{:S(2)}) copy-start(f32[128,64]{0,1:T(8,128)} %param.20) | copy-start | bytes 98308
  140.6 12.2 %copy-start.36 = (f32[4,480]{1,0:T(4,128)S(1)}, f32[4,480]{1,0:T(4,128)}, u32[]{:S(2)}) copy-start(f32[4,480]{1,0:T(4,128)} %get-tuple-element.106) | copy-start | bytes 23044
  140.6 11.4 %collective-permute-start.6 = (f32[1,128,1,480]{1,3,2,0:T(8,128)S(1)}, f32[1,128,1,480]{1,3,2,0:T(8,128)S(1)}, u32[]{:S(2)}, u32[]{:S(2)}) collective-permute-start(f32[1,128,1,480]{1,3,2,0:T(8,128)S(1)} %get-tuple-element.90), channel_id=1, source_target_pairs={{0,2},{2,4},{4,6},{1,3},{3,5},{5,7},{8,10},{10,12},{12,14},{9,11},... | collective-permute-start | bytes 737288 | tf_op jit(solution)/shard_map/ppermute | solution.py:17
  144.6 8.1 %collective-permute-start.7 = (f32[1,128,1,480]{1,3,2,0:T(8,128)S(1)}, f32[1,128,1,480]{1,3,2,0:T(8,128)S(1)}, u32[]{:S(2)}, u32[]{:S(2)}) collective-permute-start(f32[1,128,1,480]{1,3,2,0:T(8,128)S(1)} %get-tuple-element.89), channel_id=1, source_target_pairs={{2,0},{4,2},{6,4},{3,1},{5,3},{7,5},{10,8},{12,10},{14,12},{11,9},... | collective-permute-start | bytes 737288 | tf_op jit(solution)/shard_map/ppermute | solution.py:18
  148.6 5.6 %copy-start.30 = (f32[4,480]{1,0:T(4,128)S(1)}, f32[4,480]{1,0:T(4,128)}, u32[]{:S(2)}) copy-start(f32[4,480]{1,0:T(4,128)} %copy-done.29) | copy-start | bytes 23044
  150.2 4.3 %copy-start.15 = (f32[64,4,480]{2,1,0:T(4,128)S(1)}, f32[64,4,480]{2,1,0:T(4,128)}, u32[]{:S(2)}) copy-start(f32[64,4,480]{2,1,0:T(4,128)} %divide_bitcast_fusion) | copy-start | bytes 1474564
  (20 other events, 29.4 us)
Sparse Core Ops, SparseCore 0:
  156.3 133.9 all-reduce.25
where the time goes:
time: 312 us; the launch traced here: 308 us
  waiting for transfers between devices  158 us (51%)
  matrix products  61.9 us (20%)
  other arithmetic  30.4 us (10%)
  blocking collectives  22.5 us (7%)
  starting transfers between devices  16.5 us (5%)
  between operations  15.6 us (5%)
  local copies, waits for them, and re-layouts  3.39 us (1%)
    psum x1, waiting for transfers between devices, per_device(): summed = lax.psum(shared + widened, ('dp', 'row', 'view'))  133 us
    dot_general x18, matrix products, mixing(): return jnp.einsum('oc,...chw->...ohw', weight, fields, precision=highest)  32.6 us
    ppermute x4, waiting for transfers between devices, partner(): return lax.ppermute(value, axis, pairs)  19.1 us
    dot_general x3, matrix products, attend(): jnp.einsum('...chi,...chj->...hij', queries, query_other, precision=highest)  15.3 us
    psum x1, blocking collectives, per_device(): pooled = lax.psum(jnp.sum(gating, axis=(2, 3)), 'row') / (height * breadth)  13.6 us
    dot_general x3, matrix products, attend(): jnp.einsum('...hij,...chj->...chi', weights, value_other, precision=highest)  13 us
    ppermute x2, starting transfers between devices, extended(): before = lax.ppermute(last, axis, up)  9.63 us
    psum x1, blocking collectives, per_device(): pooled_grad = lax.psum(tail_grads[2], 'row')  8.89 us
  transfers between devices with their start and end apart: 9, of which 7 were waited for; matrix products, arithmetic and copies ran while one was open for 10% of the time, Pallas kernels for 0%

commit v1 on v0

v1 whole, which is shorter than its diff:
```python
import functools

import jax
import jax.numpy as jnp
from jax import lax
from jax.experimental import pallas as pl
from jax.experimental.pallas import tpu as pltpu
from jax.sharding import PartitionSpec as P

epsilon = 1e-06
F32 = jnp.float32
BF16 = jnp.bfloat16
MIB = 1 << 20


def split(x):
    high = x.astype(BF16)
    return high, (x - high.astype(F32)).astype(BF16)


def stack_rows(*parts):
    return jnp.concatenate(parts, axis=0)


def left_rows(w):
    h, l = split(w)
    return stack_rows(h, h, l)


def right_rows(x):
    h, l = split(x)
    return stack_rows(h, l, h)


def left_lanes(w):
    h, l = split(w)
    return jnp.concatenate([h, h, l], axis=1)


def dot_nn(a, b):
    return lax.dot_general(a, b, (((1,), (0,)), ((), ())), preferred_element_type=F32)


def dot_tn(a, b):
    return lax.dot_general(a, b, (((0,), (0,)), ((), ())), preferred_element_type=F32)


def dot_nt(a, b):
    return lax.dot_general(a, b, (((1,), (1,)), ((), ())), preferred_element_type=F32)


def outer_pixels(a, b):
    return dot_nt(stack_rows(*split(a)), stack_rows(*split(b)))


def fold(acc):
    m, n = acc.shape[0] // 2, acc.shape[1] // 2
    return acc[:m, :n] + acc[:m, n:] + acc[m:, :n]


def channel_mean(x):
    return jnp.sum(x, axis=0, keepdims=True) * (1.0 / x.shape[0])


def normed_of(x):
    center = x - channel_mean(x)
    scale = 1.0 / jnp.sqrt(channel_mean(center * center) + epsilon)
    return center * scale, scale


def norm_back(grad, normed, scale):
    return scale * (grad - channel_mean(grad) - normed * channel_mean(grad * normed))


def eye(n):
    rows = lax.broadcasted_iota(jnp.int32, (n, n), 0)
    return (rows == lax.broadcasted_iota(jnp.int32, (n, n), 1)).astype(F32)


def to_column(row):
    return jnp.sum(eye(row.shape[1]) * row, axis=1, keepdims=True)


def to_row(column):
    return jnp.sum(eye(column.shape[0]) * column, axis=0, keepdims=True)


def lane_mask(shape, width):
    return lax.broadcasted_iota(jnp.int32, shape, len(shape) - 1) < width


def relayout(x_ref, o_ref):
    rows, width = o_ref.shape[0], x_ref.shape[2]
    padded = o_ref.shape[2]
    for h in range(rows):
        o_ref[h, :, 0:width] = x_ref[:, h, :]
        if padded > width:
            o_ref[h, :, width:padded] = jnp.zeros((o_ref.shape[1], padded - width), F32)


def start_kernel(x_ref, q_ref, v_ref, s_ref, band_ref, first_ref, last_ref, pack_ref):
    ch = q_ref.shape[0]
    relayout(x_ref, band_ref)
    first_ref[...] = band_ref[0]
    last_ref[...] = band_ref[band_ref.shape[0] - 1]
    pack_ref[0:ch, 0:ch] = q_ref[...]
    pack_ref[0:ch, ch : 2 * ch] = v_ref[...]
    pack_ref[ch : ch + 8, 0:ch] = jnp.broadcast_to(s_ref[...], (8, ch))


def kernel_columns(k_ref, kt_ref):
    tall = k_ref.shape[2]
    rows = lax.broadcasted_iota(jnp.int32, (tall, tall), 0)
    mat = jnp.zeros((tall, tall), F32)
    for i in range(3):
        for j in range(3):
            mat = jnp.where(rows == 3 * i + j, k_ref[i, j : j + 1, :], mat)
    kt_ref[...] = mat.T


def shifted(x):
    n = x.shape[1]
    return pltpu.roll(x, 1, 1), x, pltpu.roll(x, n - 1, 1)


def conv_own_kernel(
    view_ref, band_ref, exp_ref, k_ref, cot_ref, doubled_ref, conv_ref, send_ref, keep_ref, kt_ref, cband_ref
):
    rows, ch, padded = band_ref.shape
    half = rows // 2
    wide = doubled_ref.shape[1]
    kernel_columns(k_ref, kt_ref)
    weight = left_rows(exp_ref[...])
    for h in range(rows):
        doubled_ref[h] = dot_tn(weight, right_rows(normed_of(band_ref[h])[0]))

    def group(g, carry):
        at = pl.ds(pl.multiple_of(g * 8, 8), 8)
        taps = kt_ref[at, :]
        moved = [shifted(doubled_ref[h, at, :]) for h in range(rows)]
        for h in range(rows):
            total = None
            for i in range(3):
                src = h + i - 1
                if 0 <= src < rows:
                    for j in range(3):
                        term = taps[:, 3 * i + j : 3 * i + j + 1] * moved[src][j]
                        total = term if total is None else total + term
            conv_ref[h, at, :] = total
        return carry

    lax.fori_loop(0, wide // 8, group, 0)
    relayout(cot_ref, cband_ref)
    view = view_ref[0]
    for k in range(half):
        keep_ref[k] = cband_ref[half * view + k]
        send_ref[k] = cband_ref[half * (1 - view) + k]


def conv_edge_kernel(
    width, part_ref, doubled_ref, up_ref, down_ref, exp_ref, k_ref, conv_ref, edge_ref, gating_ref, pool_ref, kt_ref
):
    rows, wide, padded = part_ref.shape
    ch = wide // 2
    kernel_columns(k_ref, kt_ref)
    weight = left_rows(exp_ref[...])
    edge_ref[0] = dot_tn(weight, right_rows(normed_of(up_ref[...])[0]))
    edge_ref[1] = dot_tn(weight, right_rows(normed_of(down_ref[...])[0]))
    keep = lane_mask((8, padded), width)

    def group(g, carry):
        lower = pl.multiple_of(g * 8, 8)
        halves = []
        for offset in (0, ch):
            at = pl.ds(pl.multiple_of(lower + offset, 8), 8)
            taps = kt_ref[at, :]
            above, below = shifted(edge_ref[0, at, :]), shifted(edge_ref[1, at, :])
            out = []
            for h in range(rows):
                total = part_ref[h, at, :]
                for j in range(3):
                    if h == 0:
                        total = total + taps[:, j : j + 1] * above[j]
                    if h == rows - 1:
                        total = total + taps[:, 6 + j : 7 + j] * below[j]
                total = jnp.where(keep, total, 0.0)
                conv_ref[h, at, :] = total
                out.append(total)
            halves.append(out)
        pooled = jnp.zeros((8, padded), F32)
        at = pl.ds(lower, 8)
        for h in range(rows):
            gate = halves[0][h] * halves[1][h]
            gating_ref[h, at, :] = gate
            pooled = pooled + gate
        kt_ref[at, :] = jnp.broadcast_to(jnp.sum(pooled, axis=1, keepdims=True), (8, kt_ref.shape[1]))
        return carry

    lax.fori_loop(0, ch // 8, group, 0)
    sums = to_row(kt_ref[0:ch, 0:1])
    pool_ref[...] = jnp.zeros(pool_ref.shape, F32)
    pool_ref[:, 0:ch] = jnp.broadcast_to(sums, (8, ch))


def attention_of(pool_ref, proj_ref, bias_ref, area):
    ch = proj_ref.shape[0]
    pooled = pool_ref[:, 0:ch] * (1.0 / area)
    ph, plow = split(pooled)
    wh, wl = split(proj_ref[...])
    product = dot_nt(ph, wh) + dot_nt(ph, wl) + dot_nt(plow, wh)
    return pooled[0:1], product[0:1] + bias_ref[...]


def tail_kernel(
    area,
    base_ref,
    band_ref,
    gating_ref,
    pool_ref,
    proj_ref,
    bias_ref,
    squeeze_ref,
    branch_ref,
    up_ref,
    down_ref,
    scale_ref,
    hidden_ref,
    one_ref,
    expanded_ref,
):
    half, ch, _ = hidden_ref.shape
    _, attention = attention_of(pool_ref, proj_ref, bias_ref, area)
    squeeze = left_lanes(to_column(branch_ref[...]) * squeeze_ref[...] * attention)
    up = left_rows(up_ref[...])
    down = left_lanes(to_column(scale_ref[...]) * down_ref[...])
    base = base_ref[0]
    for k in range(half):
        one = band_ref[base + k] + dot_nn(squeeze, right_rows(gating_ref[base + k]))
        one_ref[k] = one
        expanded = dot_tn(up, right_rows(normed_of(one)[0]))
        expanded_ref[k] = expanded
        hidden_ref[k] = one + dot_nn(down, right_rows(expanded[:ch] * expanded[ch:]))


def attend_kernel(
    width,
    hid0_ref,
    hid1_ref,
    cot0_ref,
    cot1_ref,
    pack0_ref,
    pack1_ref,
    out0_ref,
    out1_ref,
    dh0_ref,
    dh1_ref,
    grad0_ref,
    grad1_ref,
    e_ref,
    eh_ref,
    el_ref,
):
    half, ch, padded = hid0_ref.shape
    block = 128
    inv = ch ** (-0.5)
    mask = lane_mask((1, padded), width)
    hids, cots = (hid0_ref, hid1_ref), (cot0_ref, cot1_ref)
    wq = [ref[0:ch, 0:ch] for ref in (pack0_ref, pack1_ref)]
    wv = [ref[0:ch, ch : 2 * ch] for ref in (pack0_ref, pack1_ref)]
    scale = [to_column(ref[ch : ch + 1, 0:ch]) for ref in (pack0_ref, pack1_ref)]
    lq, lv = [left_lanes(w) for w in wq], [left_lanes(w) for w in wv]
    lqt, lvt = [left_rows(w) for w in wq], [left_rows(w) for w in wv]
    acc_q, acc_v, acc_s = [None, None], [None, None], [None, None]

    def add(acc, s, value):
        acc[s] = value if acc[s] is None else acc[s] + value

    for k in range(half):
        h = [ref[k] for ref in hids]
        u = [ref[k] for ref in cots]
        norms = [normed_of(x) for x in h]
        q = [dot_nn(lq[s], right_rows(norms[s][0])) for s in range(2)]
        v = [dot_nn(lv[s], right_rows(h[s])) for s in range(2)]
        qh, ql = zip(*[split(q[0] * inv), split(q[1])])
        vh, vl = zip(*[split(x) for x in v])
        left = stack_rows(qh[0], qh[0], ql[0])
        right = stack_rows(qh[1], ql[1], qh[1])
        col_sum = jnp.zeros((1, padded), F32)
        for b in range(0, padded, block):
            scores = dot_tn(left[:, b : b + block], right)
            weights = jnp.where(mask, jnp.exp(scores), 0.0)
            if b + block > width:
                rows_at = lax.broadcasted_iota(jnp.int32, (block, 1), 0) + b
                weights = jnp.where(rows_at < width, weights, 0.0)
            eh, el = split(weights)
            e_ref[b : b + block, :] = weights
            eh_ref[b : b + block, :] = eh
            el_ref[b : b + block, :] = el
            col_sum = col_sum + jnp.sum(weights, axis=0, keepdims=True)
        b_inv = jnp.where(mask, 1.0 / jnp.where(mask, col_sum, 1.0), 0.0)
        g = [scale[s] * u[s] for s in range(2)]
        bg = g[1] * b_inv
        bgh, bgl = split(bg)
        ones = jnp.ones((16, padded), BF16)
        first = dot_nt(stack_rows(vh[1], vl[1], bgh, bgl, ones), eh_ref[...])
        second = dot_nt(stack_rows(vh[1], bgh, ones), el_ref[...])
        row_sum = first[4 * ch : 4 * ch + 1] + second[2 * ch : 2 * ch + 1]
        a_inv = jnp.where(mask, 1.0 / jnp.where(mask, row_sum, 1.0), 0.0)
        carried0 = (first[0:ch] + first[ch : 2 * ch] + second[0:ch]) * a_inv
        dv0 = first[2 * ch : 3 * ch] + first[3 * ch : 4 * ch] + second[ch : 2 * ch]
        ag = g[0] * a_inv
        agh, agl = split(ag)
        first = dot_nn(stack_rows(vh[0], vl[0], agh, agl), eh_ref[...])
        second = dot_nn(stack_rows(vh[0], agh), el_ref[...])
        carried1 = (first[0:ch] + first[ch : 2 * ch] + second[0:ch]) * b_inv
        dv1 = first[2 * ch : 3 * ch] + first[3 * ch : 4 * ch] + second[ch : 2 * ch]
        out0_ref[k] = h[0] + scale[0] * carried0
        out1_ref[k] = h[1] + scale[1] * carried1
        d0 = jnp.sum(ag * carried0, axis=0, keepdims=True)
        d1 = jnp.sum(bg * carried1, axis=0, keepdims=True)
        d0h, d0l = split(d0)
        row_at = lax.broadcasted_iota(jnp.int32, (16, padded), 0)
        extra = jnp.where(row_at == 0, d0h.astype(F32), jnp.where(row_at == 1, d0l.astype(F32), 0.0)).astype(BF16)
        left = stack_rows(agh, vh[0], agh, vh[0], agl, vl[0], extra)
        right = stack_rows(vh[1], bgh, vl[1], bgl, vh[1], bgh, -ones)
        for b in range(0, padded, block):
            inner = dot_tn(left[:, b : b + block], right) - d1
            dsh, dsl = split(e_ref[b : b + block, :] * inner)
            eh_ref[b : b + block, :] = dsh
            el_ref[b : b + block, :] = dsl
        first = dot_nt(stack_rows(qh[1], ql[1]), eh_ref[...])
        dq0 = (first[0:ch] + first[ch : 2 * ch] + dot_nt(qh[1], el_ref[...])) * inv
        first = dot_nn(stack_rows(qh[0], ql[0]), eh_ref[...])
        dq1 = first[0:ch] + first[ch : 2 * ch] + dot_nn(qh[0], el_ref[...])
        dq, dv, carried = (dq0, dq1), (dv0, dv1), (carried0, carried1)
        for s, ref in enumerate((dh0_ref, dh1_ref)):
            normed, spread = norms[s]
            dn = dot_tn(lqt[s], right_rows(dq[s]))
            ref[k] = u[s] + norm_back(dn, normed, spread) + dot_tn(lvt[s], right_rows(dv[s]))
            add(acc_q, s, outer_pixels(dq[s], normed))
            add(acc_v, s, outer_pixels(dv[s], h[s]))
            add(acc_s, s, u[s] * carried[s])
    for s, ref in enumerate((grad0_ref, grad1_ref)):
        ref[0:ch, 0:ch] = fold(acc_q[s])
        ref[0:ch, ch : 2 * ch] = fold(acc_v[s])
        row = to_row(jnp.sum(acc_s[s], axis=1, keepdims=True))
        ref[ch : ch + 8, 0:ch] = jnp.broadcast_to(row, (8, ch))
        ref[ch : ch + 8, ch : 2 * ch] = jnp.zeros((8, ch), F32)


def tail_back_kernel(
    area,
    final,
    base_ref,
    dh_ref,
    one_ref,
    expanded_ref,
    gating_ref,
    pool_ref,
    proj_ref,
    bias_ref,
    squeeze_ref,
    branch_ref,
    up_ref,
    down_ref,
    scale_ref,
    *refs,
):
    half, ch, _ = dh_ref.shape
    base = base_ref[0]
    pooled, attention = attention_of(pool_ref, proj_ref, bias_ref, area)
    branch, scale = to_column(branch_ref[...]), to_column(scale_ref[...])
    mixed = branch * squeeze_ref[...]
    squeeze = left_rows(mixed * attention)
    up = left_lanes(up_ref[...])
    down = left_rows(scale * down_ref[...])
    if final:
        acc_in, dgate_in, done_in, (dgate_ref, done_ref, pg_ref, grad_ref) = refs[0], refs[1], refs[2], refs[3:]
    else:
        dgate_ref, done_ref, acc_ref = refs
    acc1 = acc2 = acc3 = None
    for k in range(half):
        dh, one, expanded = dh_ref[k], one_ref[k], expanded_ref[k]
        lower, upper = expanded[:ch], expanded[ch:]
        normed, spread = normed_of(one)
        term1 = outer_pixels(dh, lower * upper)
        dprod = dot_tn(down, right_rows(dh))
        dexp = stack_rows(dprod * upper, dprod * lower)
        term2 = outer_pixels(normed, dexp)
        dn = dot_nn(up, right_rows(dexp))
        done = dh + norm_back(dn, normed, spread)
        done_ref[k] = done
        term3 = outer_pixels(done, gating_ref[base + k])
        dgate_ref[k] = dot_tn(squeeze, right_rows(done))
        acc1 = term1 if acc1 is None else acc1 + term1
        acc2 = term2 if acc2 is None else acc2 + term2
        acc3 = term3 if acc3 is None else acc3 + term3
    if not final:
        acc_ref[:, 0 : 2 * ch] = acc1
        acc_ref[:, 2 * ch : 6 * ch] = acc2
        acc_ref[:, 6 * ch : 8 * ch] = acc3
        return
    m1 = fold(acc1 + acc_in[:, 0 : 2 * ch])
    m2 = fold(acc2 + acc_in[:, 2 * ch : 6 * ch])
    m3 = fold(acc3 + acc_in[:, 6 * ch : 8 * ch])
    datt = jnp.sum(mixed * m3, axis=0, keepdims=True)
    dcol = to_column(datt)
    dh8, dl8 = split(jnp.broadcast_to(datt, (8, ch)))
    ph, plow = split(proj_ref[...])
    pg_ref[...] = jnp.zeros(pg_ref.shape, F32)
    pg_ref[:, 0:ch] = (dot_nn(dh8, ph) + dot_nn(dh8, plow) + dot_nn(dl8, ph)) * (1.0 / area)
    grad_ref[0:ch, :] = m2
    grad_ref[ch : 2 * ch, 0:ch] = scale * m1
    grad_ref[ch : 2 * ch, ch : 2 * ch] = branch * m3 * attention
    grad_ref[2 * ch : 3 * ch, 0:ch] = dcol * pooled
    dscale = jnp.sum(down_ref[...] * m1, axis=1, keepdims=True)
    dbranch = jnp.sum(squeeze_ref[...] * attention * m3, axis=1, keepdims=True)
    row_at = lax.broadcasted_iota(jnp.int32, (ch, ch), 0)
    vectors = jnp.where(row_at == 0, datt, jnp.where(row_at == 1, to_row(dbranch), jnp.where(row_at == 2, to_row(dscale), 0.0)))
    grad_ref[2 * ch : 3 * ch, ch : 2 * ch] = vectors


def conv_back_kernel(
    width,
    view_ref,
    dkeep_ref,
    dsend_ref,
    pg_ref,
    conv_ref,
    doubled_ref,
    edge_ref,
    band_ref,
    up_ref,
    down_ref,
    exp_ref,
    k_ref,
    dn_ref,
    dnup_ref,
    dndown_ref,
    grad_ref,
    kt_ref,
    dgate_ref,
    bg_ref,
    gk_ref,
    pgcol_ref,
):
    rows, wide, padded = conv_ref.shape
    ch = wide // 2
    half = rows // 2
    view = view_ref[0]
    kernel_columns(k_ref, kt_ref)
    pgcol_ref[...] = jnp.broadcast_to(to_column(pg_ref[0:1, 0:ch]), pgcol_ref.shape)
    for k in range(half):
        dgate_ref[half * view + k] = dkeep_ref[k]
        dgate_ref[half * (1 - view) + k] = dsend_ref[k]
    keep = lane_mask((8, padded), width)
    lanes = lax.broadcasted_iota(jnp.int32, (8, 128), 1)

    def fold_lanes(x):
        total = x[:, 0:128]
        for t in range(128, padded, 128):
            total = total + x[:, t : t + 128]
        return total

    def group(g, carry):
        lower = pl.multiple_of(g * 8, 8)
        at = pl.ds(lower, 8)
        other = pl.ds(pl.multiple_of(lower + ch, 8), 8)
        shift = pgcol_ref[at, 0:1]
        total = [dgate_ref[h, at, :] + shift for h in range(rows)]
        for own, partner in ((at, other), (other, at)):
            taps = kt_ref[own, :]
            moved = []
            for h in range(rows):
                minus, same, plus = shifted(total[h] * conv_ref[h, partner, :])
                moved.append((plus, same, minus))
            sums = [[None] * 3 for _ in range(3)]
            for r in range(-1, rows + 1):
                if r < 0:
                    feature = edge_ref[0, own, :]
                elif r == rows:
                    feature = edge_ref[1, own, :]
                else:
                    feature = doubled_ref[r, own, :]
                back = None
                for i in range(3):
                    src = r - i + 1
                    if 0 <= src < rows:
                        for j in range(3):
                            term = taps[:, 3 * i + j : 3 * i + j + 1] * moved[src][j]
                            back = term if back is None else back + term
                            part = fold_lanes(feature * moved[src][j])
                            sums[i][j] = part if sums[i][j] is None else sums[i][j] + part
                bg_ref[r + 1, own, :] = jnp.where(keep, back, 0.0)
            packed = jnp.zeros((8, 128), F32)
            for i in range(3):
                for j in range(3):
                    packed = jnp.where(lanes == 3 * i + j, jnp.sum(sums[i][j], axis=1, keepdims=True), packed)
            gk_ref[own, :] = packed
        return carry

    lax.fori_loop(0, ch // 8, group, 0)
    weight = left_lanes(exp_ref[...])
    acc = None
    for r in range(rows + 2):
        source = up_ref[...] if r == 0 else down_ref[...] if r == rows + 1 else band_ref[r - 1]
        back = bg_ref[r]
        term = outer_pixels(normed_of(source)[0], back)
        acc = term if acc is None else acc + term
        value = dot_nn(weight, right_rows(back))
        if r == 0:
            dnup_ref[...] = value
        elif r == rows + 1:
            dndown_ref[...] = value
        else:
            dn_ref[r - 1] = value
    grad_ref[0:ch, :] = fold(acc)
    grad_ref[ch : ch + 16, :] = gk_ref[...].T[0:16, :]


def place_rows(o_ref, row, value):
    o_ref[:, row, :] = value[:, 0 : o_ref.shape[2]]


def front_back_kernel(view_ref, dn_ref, above_ref, below_ref, band_ref, keep_ref, send_ref, o_ref, scratch_ref):
    rows = dn_ref.shape[0]
    half = rows // 2
    view = view_ref[0]
    for k in range(half):
        scratch_ref[half * view + k] = keep_ref[k]
        scratch_ref[half * (1 - view) + k] = send_ref[k]
    for h in range(rows):
        dn = dn_ref[h]
        if h == 0:
            dn = dn + above_ref[...]
        if h == rows - 1:
            dn = dn + below_ref[...]
        normed, spread = normed_of(band_ref[h])
        place_rows(o_ref, h, scratch_ref[h] + norm_back(dn, normed, spread))


def assemble_kernel(view_ref, keep_ref, send_ref, o_ref, scratch_ref):
    half = keep_ref.shape[0]
    view = view_ref[0]
    for k in range(half):
        scratch_ref[half * view + k] = keep_ref[k]
        scratch_ref[half * (1 - view) + k] = send_ref[k]
    for h in range(2 * half):
        place_rows(o_ref, h, scratch_ref[h])


def finish_kernel(factor, a_ref, b_ref, c_ref, up_ref, down_ref, squeeze_ref, pool_ref, bias_ref, branch_ref, scale_ref, q_ref, v_ref, s_ref, exp_ref, k_ref):
    ch = q_ref.shape[0]
    q_ref[...] = a_ref[0:ch, 0:ch] * factor
    v_ref[...] = a_ref[0:ch, ch : 2 * ch] * factor
    s_ref[...] = a_ref[ch : ch + 1, 0:ch] * factor
    up_ref[...] = b_ref[0:ch, :] * factor
    down_ref[...] = b_ref[ch : 2 * ch, 0:ch] * factor
    squeeze_ref[...] = b_ref[ch : 2 * ch, ch : 2 * ch] * factor
    pool_ref[...] = b_ref[2 * ch : 3 * ch, 0:ch] * factor
    bias_ref[...] = b_ref[2 * ch : 2 * ch + 1, ch : 2 * ch] * factor
    branch_ref[...] = b_ref[2 * ch + 1 : 2 * ch + 2, ch : 2 * ch] * factor
    scale_ref[...] = b_ref[2 * ch + 2 : 2 * ch + 3, ch : 2 * ch] * factor
    exp_ref[...] = c_ref[0:ch, :] * factor
    for i in range(3):
        k_ref[i] = c_ref[ch + 3 * i : ch + 3 * i + 3, :] * factor


def call(kernel, outs, *args, scalars=0, scratch=(), name=None, cost=None):
    smem = pl.BlockSpec(memory_space=pltpu.SMEM)
    vmem = pl.BlockSpec(memory_space=pltpu.VMEM)
    shapes = tuple(jax.ShapeDtypeStruct(s, F32) for s in outs)
    return pl.pallas_call(
        kernel,
        out_shape=shapes,
        in_specs=[smem] * scalars + [vmem] * (len(args) - scalars),
        out_specs=(vmem,) * len(shapes),
        scratch_shapes=list(scratch),
        compiler_params=pltpu.CompilerParams(vmem_limit_bytes=28 * MIB),
        name=name,
        cost_estimate=cost,
    )(*args)


def swap(x, axis, mask):
    return lax.ppermute(x, axis, [(i, i ^ mask) for i in range(lax.axis_size(axis))])


def sum_over(x, *axes):
    for axis in axes:
        size = lax.axis_size(axis)
        if size & (size - 1):
            x = lax.psum(x, axis)
            continue
        mask = 1
        while mask < size:
            x = x + swap(x, axis, mask)
            mask *= 2
    return x


def per_device(
    frames_in,
    cotangent,
    expand_in,
    conv_kernel,
    pool_proj,
    pool_bias,
    squeeze_out,
    branch_scale,
    ffn_expand,
    ffn_shrink,
    ffn_scale,
    query_proj,
    value_proj,
    cross_scale,
):
    _, frames, ch, rows, width = frames_in.shape
    assert frames == 1 and rows % 2 == 0
    half = rows // 2
    wide = 2 * ch
    padded = -(-width // 128) * 128
    bands = lax.axis_size("row")
    area = rows * bands * width
    factor = (2 * frames * lax.axis_size("dp") * area) ** (-0.5)
    view = lax.axis_index("view").astype(jnp.int32).reshape(1)
    keep_base, send_base = half * view, half * (1 - view)
    part, full = (half, ch, padded), (rows, ch, padded)
    row = (ch, padded)
    exp_t, up_t = expand_in.T, ffn_expand.T
    k_rows = jnp.transpose(conv_kernel, (1, 2, 0))
    bias, branch, scale = (x.reshape(1, ch) for x in (pool_bias, branch_scale, ffn_scale))
    vm = lambda *shape: pltpu.VMEM(shape, F32)

    band, first, last, pack = call(
        start_kernel,
        [full, row, row, (ch + 8, wide)],
        frames_in[0, 0],
        query_proj[0],
        value_proj[0],
        cross_scale,
        name="start",
    )
    up_pairs = [(i, i + 1) for i in range(bands - 1)]
    down_pairs = [(i + 1, i) for i in range(bands - 1)]
    above = lax.ppermute(last, "row", up_pairs)
    below = lax.ppermute(first, "row", down_pairs)
    pack_other = swap(pack, "view", 1)
    doubled, conv_part, cot_send, cot_keep = call(
        conv_own_kernel,
        [(rows, wide, padded)] * 2 + [part] * 2,
        view,
        band,
        exp_t,
        k_rows,
        cotangent[0, 0],
        scalars=1,
        scratch=[vm(wide, wide), vm(rows, ch, padded)],
        name="conv_own",
    )
    cot_other = swap(cot_send, "view", 1)
    conv, edge, gating, pool = call(
        functools.partial(conv_edge_kernel, width),
        [(rows, wide, padded), (2, wide, padded), full, (8, wide)],
        conv_part,
        doubled,
        above,
        below,
        exp_t,
        k_rows,
        scratch=[vm(wide, wide)],
        name="conv_edge",
    )
    pool = sum_over(pool, "row")
    weights = (pool, pool_proj, bias, squeeze_out, branch, up_t, ffn_shrink, scale)

    def tail(base, name):
        return call(
            functools.partial(tail_kernel, area),
            [part, part, (half, wide, padded)],
            base,
            band,
            gating,
            *weights,
            scalars=1,
            name=name,
        )

    hid_send, one_send, expanded_send = tail(send_base, "tail_send")
    hid_other = swap(hid_send, "view", 1)
    hid_keep, one_keep, expanded_keep = tail(keep_base, "tail_keep")
    out_keep, out_send, dh_keep, dh_send, grad_own, grad_other = call(
        functools.partial(attend_kernel, width),
        [part] * 4 + [(ch + 8, wide)] * 2,
        hid_keep,
        hid_other,
        cot_keep,
        cot_other,
        pack,
        pack_other,
        scratch=[vm(padded, padded), pltpu.VMEM((padded, padded), BF16), pltpu.VMEM((padded, padded), BF16)],
        name="attend",
    )
    dh_back = swap(dh_send, "view", 1)
    out_back = swap(out_send, "view", 1)
    grad_a = grad_own + swap(grad_other, "view", 1)
    dgate_keep, done_keep, acc = call(
        functools.partial(tail_back_kernel, area, False),
        [part, part, (wide, 8 * ch)],
        keep_base,
        dh_keep,
        one_keep,
        expanded_keep,
        gating,
        *weights,
        scalars=1,
        name="tail_back_keep",
    )
    dgate_send, done_send, pool_grad, grad_b = call(
        lambda base, dh, one, ex, gate, w0, w1, w2, w3, w4, w5, w6, w7, acc, dg, dn, pg, gr: tail_back_kernel(
            area, True, base, dh, one, ex, gate, w0, w1, w2, w3, w4, w5, w6, w7, acc, None, None, dg, dn, pg, gr
        ),
        [part, part, (8, wide), (3 * ch, wide)],
        send_base,
        dh_back,
        one_send,
        expanded_send,
        gating,
        *weights,
        acc,
        scalars=1,
        name="tail_back_send",
    )
    pool_grad = sum_over(pool_grad, "row")
    grad_a = sum_over(grad_a, "dp", "row")
    grad_b = sum_over(grad_b, "dp", "view", "row")
    (output,) = call(
        assemble_kernel,
        [(ch, rows, width)],
        view,
        out_keep,
        out_back,
        scalars=1,
        scratch=[vm(rows, ch, padded)],
        name="assemble",
    )
    dn, dn_up, dn_down, grad_c = call(
        functools.partial(conv_back_kernel, width),
        [full, row, row, (ch + 16, wide)],
        view,
        dgate_keep,
        dgate_send,
        pool_grad,
        conv,
        doubled,
        edge,
        band,
        above,
        below,
        exp_t,
        k_rows,
        scalars=1,
        scratch=[vm(wide, wide), vm(rows, ch, padded), vm(rows + 2, wide, padded), vm(wide, wide), vm(ch, wide)],
        name="conv_back",
    )
    from_above = lax.ppermute(dn_down, "row", up_pairs)
    from_below = lax.ppermute(dn_up, "row", down_pairs)
    grad_c = sum_over(grad_c, "dp", "view", "row")
    (frames_grad,) = call(
        front_back_kernel,
        [(ch, rows, width)],
        view,
        dn,
        from_above,
        from_below,
        band,
        done_keep,
        done_send,
        scalars=1,
        scratch=[vm(rows, ch, padded)],
        name="front_back",
    )
    g_up, g_down, g_squeeze, g_pool, g_bias, g_branch, g_scale, g_q, g_v, g_s, g_exp, g_k = call(
        functools.partial(finish_kernel, factor),
        [(ch, wide), (ch, ch), (ch, ch), (ch, ch), (1, ch), (1, ch), (1, ch), (ch, ch), (ch, ch), (1, ch), (ch, wide), (3, 3, wide)],
        grad_a,
        grad_b,
        grad_c,
        name="finish",
    )
    return (
        output[None, None],
        frames_grad[None, None],
        g_exp.T,
        jnp.transpose(g_k, (2, 0, 1)),
        g_pool,
        g_bias.reshape(ch),
        g_squeeze,
        g_branch.reshape(ch),
        g_up.T,
        g_down,
        g_scale.reshape(ch),
        g_q[None],
        g_v[None],
        g_s,
    )


def solution(mesh):
    image = P("view", "dp", None, "row", None)
    owned = (P("view", None, None), P("view", None, None), P("view", None))
    return jax.shard_map(
        per_device,
        mesh=mesh,
        in_specs=(image, image) + (P(),) * 9 + owned,
        out_specs=(image, image) + (P(),) * 9 + owned,
        check_vma=False,
    )
```

time: 312 us -> 104 us (0.33); the launches traced: 308 us -> 104 us
  waiting for transfers between devices: 158 us -> 36.4 us
  matrix products: 61.9 us -> 0 us
  other arithmetic: 30.4 us -> 0.14 us
  starting transfers between devices: 16.5 us -> 39.9 us
  blocking collectives: 22.5 us -> 0 us
  Pallas kernels: 0 us -> 21.7 us
  between operations: 15.6 us -> 0.92 us
    psum x1 -> x0, waiting for transfers between devices: 133 us -> none  [per_device(): summed = lax.psum(shared + widened, ('dp', 'row', 'view'))]
    dot_general x26 -> x0, matrix products: 61.9 us -> none  [the longest x18 32.6 us: mixing(): return jnp.einsum('oc,...chw->...ohw', weight, fields, precision=highest)]
    ppermute x8 -> x28, starting transfers between devices: 16.5 us -> 39.9 us  [the longest x24 28.9 us: swap(): lax.ppermute(x, axis, [(i, i ^ mask) for i in range(lax.axis_size(axis))])]
    psum x2 -> x0, blocking collectives: 22.5 us -> none  [the longest x1 13.6 us: per_device(): pooled = lax.psum(jnp.sum(gating, axis=(2, 3)), 'row') / (height * breadth)]
    pallas_call x0 -> x12, Pallas kernels: none -> 21.7 us  [call(): pl.pallas_call(kernel, out_shape=shapes, in_specs=[smem] * scalars + [vme...]
    mul x12 -> x0, other arithmetic: 14.3 us -> none  [the longest x6 7.76 us: per_device(): shared_out = [grad_item * factor for grad_item in shared]]
    ppermute x8 -> x28, waiting for transfers between devices: 24.9 us -> 36.4 us  [the longest x24 34.1 us: swap(): lax.ppermute(x, axis, [(i, i ^ mask) for i in range(lax.axis_size(axis))])]
    reduce_sum x9 -> x0, other arithmetic: 6.49 us -> none  [the longest x1 1.8 us: per_device(): pooled = lax.psum(jnp.sum(gating, axis=(2, 3)), 'row') / (height * breadth)]
  transfers between devices with their start and end apart: 9 -> 28, of which waited for: 7 -> 15; matrix products, arithmetic and copies ran while one was open for 10% -> 0% of each run, Pallas kernels for 0% -> 12%
where the time goes in v1:
time: 104 us
  starting transfers between devices  39.9 us (38%)
  waiting for transfers between devices  36.4 us (35%)
  Pallas kernels  21.7 us (21%)
  local copies, waits for them, and re-layouts  4.54 us (4%)
    ppermute x24, waiting for transfers between devices, swap(): lax.ppermute(x, axis, [(i, i ^ mask) for i in range(lax.axis_size(axis))])  34.1 us
    ppermute x24, starting transfers between devices, swap(): lax.ppermute(x, axis, [(i, i ^ mask) for i in range(lax.axis_size(axis))])  28.9 us
    pallas_call x12, Pallas kernels, call(): pl.pallas_call(kernel, out_shape=shapes, in_specs=[smem] * scalars + [vme...  21.7 us
    ppermute x1, starting transfers between devices, per_device(): above = lax.ppermute(last, 'row', up_pairs)  5.1 us
    unnamed x28, local copies, waits for them, and re-layouts  4.54 us
    ppermute x1, starting transfers between devices, per_device(): from_above = lax.ppermute(dn_down, 'row', up_pairs)  3.32 us
    ppermute x1, waiting for transfers between devices, per_device(): below = lax.ppermute(first, 'row', down_pairs)  2.28 us
  transfers between devices with their start and end apart: 28, of which 15 were waited for; matrix products, arithmetic and copies ran while one was open for 0% of the time, Pallas kernels for 12%

profile of v1, /device:TPU:0, one launch (start us, length us, event | category | flops | bytes accessed | tf_op | source)
XLA Modules:
  0.0 103.6 jit_solution(14967731270225666157)
XLA Ops:
  0.7 0.6 copy-done.13
  1.3 1.0 %copy-done.4 = f32[1,1,64,4,480]{4,3,2,1,0:T(4,128)S(1)} copy-done((f32[1,1,64,4,480]{4,3,2,1,0:T(4,128)S(1)}, f32[1,1,64,4,480]{4,3,2,1,0:T(4,128)}, u32[]{:S(2)}) %copy-start.4) | copy-done | bytes 491544
  2.3 0.8 copy-done.8
  3.1 0.8 copy-done.9
  3.9 0.1 start.1
  4.0 5.1 %collective-permute-start = (f32[64,512]{1,0:T(8,128)S(1)}, f32[64,512]{1,0:T(8,128)S(1)}, u32[]{:S(2)}, u32[]{:S(2)}) collective-permute-start(f32[64,512]{1,0:T(8,128)S(1)} %get-tuple-element.64), channel_id=1, source_target_pairs={{0,2},{2,4},{4,6},{1,3},{3,5},{5,7},{8,10},{10,12},{12,14},{9,11},... | collective-permute-start | bytes 393224 | tf_op jit(solution)/shard_map/ppermute | solution.py:646
  9.1 1.3 %collective-permute-start.1 = (f32[64,512]{1,0:T(8,128)S(1)}, f32[64,512]{1,0:T(8,128)S(1)}, u32[]{:S(2)}, u32[]{:S(2)}) collective-permute-start(f32[64,512]{1,0:T(8,128)S(1)} %get-tuple-element.65), channel_id=1, source_target_pairs={{2,0},{4,2},{6,4},{3,1},{5,3},{7,5},{10,8},{12,10},{14,12},{11,9},... | collective-permute-start | bytes 393224 | tf_op jit(solution)/shard_map/ppermute | solution.py:647
  10.4 0.0 copy-start.7
  10.4 0.7 copy-done.7
  11.1 2.6 %conv_own.1 = (f32[4,128,512]{2,1,0:T(8,128)S(1)}, f32[4,128,512]{2,1,0:T(8,128)S(1)}, f32[2,64,512]{2,1,0:T(8,128)S(1)}, f32[2,64,512]{2,1,0:T(8,128)S(1)}) custom-call(s32[1]{0:T(128)} %bitcast.view_ref, f32[4,64,512]{2,1,0:T(8,128)S(1)} %get-tuple-element.61.band_ref, f32[64,128]{1,0:T(8,128)S(1)} %bitcast.27, f32[3,3,128]{2,1,0:T(4,128)S(1)} %bitcast.30, ...), custom_call_target="tpu_custom_call" | custom-call | tf_op jit(solution)/shard_map/conv_own/pallas_call | solution.py:573
  13.7 2.3 %collective-permute-done.1.down_ref = f32[64,512]{1,0:T(8,128)S(1)} collective-permute-done((f32[64,512]{1,0:T(8,128)S(1)}, f32[64,512]{1,0:T(8,128)S(1)}, u32[]{:S(2)}, u32[]{:S(2)}) %collective-permute-start.1) | collective-permute-done | bytes 131104 | tf_op jit(solution)/shard_map/ppermute | solution.py:647
  16.0 2.0 %conv_edge.1 = (f32[4,128,512]{2,1,0:T(8,128)S(1)}, f32[2,128,512]{2,1,0:T(8,128)S(1)}, f32[4,64,512]{2,1,0:T(8,128)S(1)}, f32[8,128]{1,0:T(8,128)S(1)}) custom-call(f32[4,128,512]{2,1,0:T(8,128)S(1)} %get-tuple-element.62.part_ref, f32[4,128,512]{2,1,0:T(8,128)S(1)} %get-tuple-element.63.doubled_ref, f32[64,512]{1,0:T(8,128)S(1)} %collective-permute-done.up_ref, ...), custom_call_target="tpu_custom_call" | custom-call | tf_op jit(solution)/shard_map/conv_edge/pallas_call | solution.py:573
  18.0 0.0 copy-start
  18.0 1.6 %collective-permute-start.2 = (f32[8,128]{1,0:T(8,128)S(1)}, f32[8,128]{1,0:T(8,128)S(1)}, u32[]{:S(2)}, u32[]{:S(2)}) collective-permute-start(f32[8,128]{1,0:T(8,128)S(1)} %get-tuple-element.67), channel_id=1, source_target_pairs={{0,2},{2,0},{4,6},{6,4},{1,3},{3,1},{5,7},{7,5},{8,10},{10,8},{12,... | collective-permute-start | bytes 12296 | tf_op jit(solution)/shard_map/ppermute | solution.py:586
  19.7 2.0 %collective-permute-done.2 = f32[8,128]{1,0:T(8,128)S(1)} collective-permute-done((f32[8,128]{1,0:T(8,128)S(1)}, f32[8,128]{1,0:T(8,128)S(1)}, u32[]{:S(2)}, u32[]{:S(2)}) %collective-permute-start.2) | collective-permute-done | bytes 4128 | tf_op jit(solution)/shard_map/ppermute | solution.py:586
  21.7 2.6 %collective-permute-start.3 = (f32[8,128]{1,0:T(8,128)S(1)}, f32[8,128]{1,0:T(8,128)S(1)}, u32[]{:S(2)}, u32[]{:S(2)}) collective-permute-start(f32[8,128]{1,0:T(8,128)S(1)} %add.57), channel_id=1, source_target_pairs={{0,4},{2,6},{4,0},{6,2},{1,5},{3,7},{5,1},{7,3},{8,12},{10,14},{12... | collective-permute-start | bytes 12296 | tf_op jit(solution)/shard_map/ppermute | solution.py:586
  24.3 1.5 %collective-permute-start.5 = (f32[2,64,512]{2,1,0:T(8,128)S(1)}, f32[2,64,512]{2,1,0:T(8,128)S(1)}, u32[]{:S(2)}, u32[]{:S(2)}) collective-permute-start(f32[2,64,512]{2,1,0:T(8,128)S(1)} %get-tuple-element.71), channel_id=1, source_target_pairs={{0,1},{1,0},{2,3},{3,2},{4,5},{5,4},{6,7},{7,6},{8,9},{9,8},{10,11... | collective-permute-start | bytes 786440 | tf_op jit(solution)/shard_map/ppermute | solution.py:586
  25.8 0.4 collective-permute-done.3
  26.3 0.6 copy-done.10
  26.9 0.0 copy-done.11
  26.9 0.0 copy-done.12
  26.9 1.2 %tail_send.1 = (f32[2,64,512]{2,1,0:T(8,128)S(1)}, f32[2,64,512]{2,1,0:T(8,128)S(1)}, f32[2,128,512]{2,1,0:T(8,128)S(1)}) custom-call(s32[1]{0:T(128)S(6)} %mul.7.base_ref.base, f32[4,64,512]{2,1,0:T(8,128)S(1)} %get-tuple-element.61.band_ref, f32[4,64,512]{2,1,0:T(8,128)S(1)} %get-tuple-element.66.gating_ref.gate, f32[8,128]{1,0:T(8,128)S(1)} %add.58.pool_ref.w0, ...), custom_call_target="tpu_custom_call" | custom-call | tf_op jit(solution)/shard_map/tail_send/pallas_call | solution.py:573
  28.1 1.5 %collective-permute-start.4 = (f32[2,64,512]{2,1,0:T(8,128)S(1)}, f32[2,64,512]{2,1,0:T(8,128)S(1)}, u32[]{:S(2)}, u32[]{:S(2)}) collective-permute-start(f32[2,64,512]{2,1,0:T(8,128)S(1)} %get-tuple-element.69), channel_id=1, source_target_pairs={{0,1},{1,0},{2,3},{3,2},{4,5},{5,4},{6,7},{7,6},{8,9},{9,8},{10,11... | collective-permute-start | bytes 786440 | tf_op jit(solution)/shard_map/ppermute | solution.py:586
  29.6 0.5 collective-permute-start.6
  30.1 1.2 %tail_keep.1 = (f32[2,64,512]{2,1,0:T(8,128)S(1)}, f32[2,64,512]{2,1,0:T(8,128)S(1)}, f32[2,128,512]{2,1,0:T(8,128)S(1)}) custom-call(s32[1]{0:T(128)S(6)} %mul.6.base_ref, f32[4,64,512]{2,1,0:T(8,128)S(1)} %get-tuple-element.61.band_ref, f32[4,64,512]{2,1,0:T(8,128)S(1)} %get-tuple-element.66.gating_ref.gate, f32[8,128]{1,0:T(8,128)S(1)} %add.58.pool_ref.w0, ...), custom_call_target="tpu_custom_call" | custom-call | tf_op jit(solution)/shard_map/tail_keep/pallas_call | solution.py:573
  31.3 4.9 %collective-permute-done.6.pack1_ref = f32[72,128]{1,0:T(8,128)S(1)} collective-permute-done((f32[72,128]{1,0:T(8,128)S(1)}, f32[72,128]{1,0:T(8,128)S(1)}, u32[]{:S(2)}, u32[]{:S(2)}) %collective-permute-start.6) | collective-permute-done | bytes 36896 | tf_op jit(solution)/shard_map/ppermute | solution.py:586
  36.2 4.7 %attend.1 = (f32[2,64,512]{2,1,0:T(8,128)S(1)}, f32[2,64,512]{2,1,0:T(8,128)S(1)}, f32[2,64,512]{2,1,0:T(8,128)S(1)}, f32[2,64,512]{2,1,0:T(8,128)S(1)}, f32[72,128]{1,0:T(8,128)S(1)}, /*index=5*/f32[72,128]{1,0:T(8,128)S(1)}) custom-call(f32[2,64,512]{2,1,0:T(8,128)S(1)} %get-tuple-element.68.hid0_ref, f32[2,64,512]{2,1,0:T(8,128)S(1)} %collective-permute-done.4.hid1_ref, ...), custom_call_target="tpu_custom_call" | custom-call | tf_op jit(solution)/shard_map/attend/pallas_call | solution.py:573
  40.9 1.4 %collective-permute-start.8 = (f32[2,64,512]{2,1,0:T(8,128)S(1)}, f32[2,64,512]{2,1,0:T(8,128)S(1)}, u32[]{:S(2)}, u32[]{:S(2)}) collective-permute-start(f32[2,64,512]{2,1,0:T(8,128)S(1)} %get-tuple-element.79), channel_id=1, source_target_pairs={{0,1},{1,0},{2,3},{3,2},{4,5},{5,4},{6,7},{7,6},{8,9},{9,8},{10,11... | collective-permute-start | bytes 786440 | tf_op jit(solution)/shard_map/ppermute | solution.py:586
  42.3 1.3 %tail_back_keep.1 = (f32[2,64,512]{2,1,0:T(8,128)S(1)}, f32[2,64,512]{2,1,0:T(8,128)S(1)}, f32[128,512]{1,0:T(8,128)S(1)}) custom-call(s32[1]{0:T(128)S(6)} %mul.6.base_ref, f32[2,64,512]{2,1,0:T(8,128)S(1)} %get-tuple-element.75.dh_ref, f32[2,64,512]{2,1,0:T(8,128)S(1)} %get-tuple-element.76.one_ref, f32[2,128,512]{2,1,0:T(8,128)S(1)} %get-tuple-element.77.expanded_ref, ...), custom_call_target="tpu_custom_call" | custom-call | tf_op jit(solution)/shard_map/tail_back_keep/pallas_call | solution.py:573
  43.6 3.8 %collective-permute-done.8.dh = f32[2,64,512]{2,1,0:T(8,128)S(1)} collective-permute-done((f32[2,64,512]{2,1,0:T(8,128)S(1)}, f32[2,64,512]{2,1,0:T(8,128)S(1)}, u32[]{:S(2)}, u32[]{:S(2)}) %collective-permute-start.8) | collective-permute-done | bytes 262176 | tf_op jit(solution)/shard_map/ppermute | solution.py:586
  47.3 1.6 %tail_back_send.1 = (f32[2,64,512]{2,1,0:T(8,128)S(1)}, f32[2,64,512]{2,1,0:T(8,128)S(1)}, f32[8,128]{1,0:T(8,128)S(1)}, f32[192,128]{1,0:T(8,128)S(1)}) custom-call(s32[1]{0:T(128)S(6)} %mul.7.base_ref.base, f32[2,64,512]{2,1,0:T(8,128)S(1)} %collective-permute-done.8.dh, f32[2,64,512]{2,1,0:T(8,128)S(1)} %get-tuple-element.80.one, ...), custom_call_target="tpu_custom_call" | custom-call | tf_op jit(solution)/shard_map/tail_back_send/pallas_call | solution.py:573
  48.9 0.0 collective-permute-start.18
  49.0 1.3 %collective-permute-done.18 = f32[192,128]{1,0:T(8,128)S(1)} collective-permute-done((f32[192,128]{1,0:T(8,128)S(1)}, f32[192,128]{1,0:T(8,128)S(1)}, u32[]{:S(2)}, u32[]{:S(2)}) %collective-permute-start.18) | collective-permute-done | bytes 98336 | tf_op jit(solution)/shard_map/ppermute | solution.py:586
  50.3 1.6 %collective-permute-start.19 = (f32[192,128]{1,0:T(8,128)S(1)}, f32[192,128]{1,0:T(8,128)S(1)}, u32[]{:S(2)}, u32[]{:S(2)}) collective-permute-start(f32[192,128]{1,0:T(8,128)S(1)} %add.66), channel_id=1, source_target_pairs={{0,16},{8,24},{16,0},{24,8},{1,17},{9,25},{17,1},{25,9},{2,18},{10... | collective-permute-start | bytes 294920 | tf_op jit(solution)/shard_map/ppermute | solution.py:586
  51.9 3.3 %collective-permute-done.19 = f32[192,128]{1,0:T(8,128)S(1)} collective-permute-done((f32[192,128]{1,0:T(8,128)S(1)}, f32[192,128]{1,0:T(8,128)S(1)}, u32[]{:S(2)}, u32[]{:S(2)}) %collective-permute-start.19) | collective-permute-done | bytes 98336 | tf_op jit(solution)/shard_map/ppermute | solution.py:586
  55.2 1.4 %collective-permute-start.20 = (f32[192,128]{1,0:T(8,128)S(1)}, f32[192,128]{1,0:T(8,128)S(1)}, u32[]{:S(2)}, u32[]{:S(2)}) collective-permute-start(f32[192,128]{1,0:T(8,128)S(1)} %add.67), channel_id=1, source_target_pairs={{0,1},{1,0},{2,3},{3,2},{4,5},{5,4},{6,7},{7,6},{8,9},{9,8},{10,11... | collective-permute-start | bytes 294920 | tf_op jit(solution)/shard_map/ppermute | solution.py:586
  56.6 1.4 %collective-permute-start.9 = (f32[8,128]{1,0:T(8,128)S(1)}, f32[8,128]{1,0:T(8,128)S(1)}, u32[]{:S(2)}, u32[]{:S(2)}) collective-permute-start(f32[8,128]{1,0:T(8,128)S(1)} %get-tuple-element.84), channel_id=1, source_target_pairs={{0,2},{2,0},{4,6},{6,4},{1,3},{3,1},{5,7},{7,5},{8,10},{10,8},{12,... | collective-permute-start | bytes 12296 | tf_op jit(solution)/shard_map/ppermute | solution.py:586
  58.0 0.5 collective-permute-start.7
  58.6 1.6 %collective-permute-done.9 = f32[8,128]{1,0:T(8,128)S(1)} collective-permute-done((f32[8,128]{1,0:T(8,128)S(1)}, f32[8,128]{1,0:T(8,128)S(1)}, u32[]{:S(2)}, u32[]{:S(2)}) %collective-permute-start.9) | collective-permute-done | bytes 4128 | tf_op jit(solution)/shard_map/ppermute | solution.py:586
  60.2 1.4 %collective-permute-start.10 = (f32[8,128]{1,0:T(8,128)S(1)}, f32[8,128]{1,0:T(8,128)S(1)}, u32[]{:S(2)}, u32[]{:S(2)}) collective-permute-start(f32[8,128]{1,0:T(8,128)S(1)} %add.59), channel_id=1, source_target_pairs={{0,4},{2,6},{4,0},{6,2},{1,5},{3,7},{5,1},{7,3},{8,12},{10,14},{12... | collective-permute-start | bytes 12296 | tf_op jit(solution)/shard_map/ppermute | solution.py:586
  61.6 3.1 %collective-permute-done.10 = f32[8,128]{1,0:T(8,128)S(1)} collective-permute-done((f32[8,128]{1,0:T(8,128)S(1)}, f32[8,128]{1,0:T(8,128)S(1)}, u32[]{:S(2)}, u32[]{:S(2)}) %collective-permute-start.10) | collective-permute-done | bytes 4128 | tf_op jit(solution)/shard_map/ppermute | solution.py:586
  64.7 4.2 %conv_back.1 = (f32[4,64,512]{2,1,0:T(8,128)S(1)}, f32[64,512]{1,0:T(8,128)S(1)}, f32[64,512]{1,0:T(8,128)S(1)}, f32[80,128]{1,0:T(8,128)S(1)}) custom-call(s32[1]{0:T(128)} %bitcast.view_ref, f32[2,64,512]{2,1,0:T(8,128)S(1)} %get-tuple-element.78.dkeep_ref, f32[2,64,512]{2,1,0:T(8,128)S(1)} %get-tuple-element.83.dsend_ref, f32[8,128]{1,0:T(8,128)S(1)} %add.60.pg_ref, ...), custom_call_target="tpu_custom_call" | custom-call | tf_op jit(solution)/shard_map/conv_back/pallas_call | solution.py:573
  68.9 0.1 collective-permute-start.23
  69.0 0.8 collective-permute-start.13
  69.8 1.3 %collective-permute-start.21 = (f32[192,128]{1,0:T(8,128)S(1)}, f32[192,128]{1,0:T(8,128)S(1)}, u32[]{:S(2)}, u32[]{:S(2)}) collective-permute-start(f32[192,128]{1,0:T(8,128)S(1)} %add.68), channel_id=1, source_target_pairs={{0,2},{2,0},{4,6},{6,4},{1,3},{3,1},{5,7},{7,5},{8,10},{10,8},{12,... | collective-permute-start | bytes 294920 | tf_op jit(solution)/shard_map/ppermute | solution.py:586
  71.1 1.6 %collective-permute-start.24 = (f32[80,128]{1,0:T(8,128)S(1)}, f32[80,128]{1,0:T(8,128)S(1)}, u32[]{:S(2)}, u32[]{:S(2)}) collective-permute-start(f32[80,128]{1,0:T(8,128)S(1)} %add.71), channel_id=1, source_target_pairs={{0,16},{8,24},{16,0},{24,8},{1,17},{9,25},{17,1},{25,9},{2,18},{10... | collective-permute-start | bytes 122888 | tf_op jit(solution)/shard_map/ppermute | solution.py:586
  72.7 0.3 collective-permute-done.13
  73.0 2.2 %collective-permute-done.24 = f32[80,128]{1,0:T(8,128)S(1)} collective-permute-done((f32[80,128]{1,0:T(8,128)S(1)}, f32[80,128]{1,0:T(8,128)S(1)}, u32[]{:S(2)}, u32[]{:S(2)}) %collective-permute-start.24) | collective-permute-done | bytes 40992 | tf_op jit(solution)/shard_map/ppermute | solution.py:586
  75.2 1.5 %collective-permute-start.25 = (f32[80,128]{1,0:T(8,128)S(1)}, f32[80,128]{1,0:T(8,128)S(1)}, u32[]{:S(2)}, u32[]{:S(2)}) collective-permute-start(f32[80,128]{1,0:T(8,128)S(1)} %add.72), channel_id=1, source_target_pairs={{0,1},{1,0},{2,3},{3,2},{4,5},{5,4},{6,7},{7,6},{8,9},{9,8},{10,11... | collective-permute-start | bytes 122888 | tf_op jit(solution)/shard_map/ppermute | solution.py:586
  76.7 1.6 %collective-permute-start.15 = (f32[72,128]{1,0:T(8,128)S(1)}, f32[72,128]{1,0:T(8,128)S(1)}, u32[]{:S(2)}, u32[]{:S(2)}) collective-permute-start(f32[72,128]{1,0:T(8,128)S(1)} %add.62), channel_id=1, source_target_pairs={{0,16},{8,24},{16,0},{24,8},{1,17},{9,25},{17,1},{25,9},{2,18},{10... | collective-permute-start | bytes 110600 | tf_op jit(solution)/shard_map/ppermute | solution.py:586
  78.3 2.4 %collective-permute-done.15 = f32[72,128]{1,0:T(8,128)S(1)} collective-permute-done((f32[72,128]{1,0:T(8,128)S(1)}, f32[72,128]{1,0:T(8,128)S(1)}, u32[]{:S(2)}, u32[]{:S(2)}) %collective-permute-start.15) | collective-permute-done | bytes 36896 | tf_op jit(solution)/shard_map/ppermute | solution.py:586
  80.7 0.6 collective-permute-start.16
  81.3 3.3 %collective-permute-start.11 = (f32[64,512]{1,0:T(8,128)S(1)}, f32[64,512]{1,0:T(8,128)S(1)}, u32[]{:S(2)}, u32[]{:S(2)}) collective-permute-start(f32[64,512]{1,0:T(8,128)S(1)} %get-tuple-element.88), channel_id=1, source_target_pairs={{0,2},{2,4},{4,6},{1,3},{3,5},{5,7},{8,10},{10,12},{12,14},{9,11},... | collective-permute-start | bytes 393224 | tf_op jit(solution)/shard_map/ppermute | solution.py:766
  84.7 1.3 %collective-permute-start.12 = (f32[64,512]{1,0:T(8,128)S(1)}, f32[64,512]{1,0:T(8,128)S(1)}, u32[]{:S(2)}, u32[]{:S(2)}) collective-permute-start(f32[64,512]{1,0:T(8,128)S(1)} %get-tuple-element.89), channel_id=1, source_target_pairs={{2,0},{4,2},{6,4},{3,1},{5,3},{7,5},{10,8},{12,10},{14,12},{11,9},... | collective-permute-start | bytes 393224 | tf_op jit(solution)/shard_map/ppermute | solution.py:767
  86.0 2.7 %collective-permute-start.26 = (f32[80,128]{1,0:T(8,128)S(1)}, f32[80,128]{1,0:T(8,128)S(1)}, u32[]{:S(2)}, u32[]{:S(2)}) collective-permute-start(f32[80,128]{1,0:T(8,128)S(1)} %add.73), channel_id=1, source_target_pairs={{0,2},{2,0},{4,6},{6,4},{1,3},{3,1},{5,7},{7,5},{8,10},{10,8},{12,... | collective-permute-start | bytes 122888 | tf_op jit(solution)/shard_map/ppermute | solution.py:586
  88.7 1.6 %collective-permute-start.22 = (f32[192,128]{1,0:T(8,128)S(1)}, f32[192,128]{1,0:T(8,128)S(1)}, u32[]{:S(2)}, u32[]{:S(2)}) collective-permute-start(f32[192,128]{1,0:T(8,128)S(1)} %add.69), channel_id=1, source_target_pairs={{0,4},{2,6},{4,0},{6,2},{1,5},{3,7},{5,1},{7,3},{8,12},{10,14},{12... | collective-permute-start | bytes 294920 | tf_op jit(solution)/shard_map/ppermute | solution.py:586
  90.3 2.8 %collective-permute-done.26 = f32[80,128]{1,0:T(8,128)S(1)} collective-permute-done((f32[80,128]{1,0:T(8,128)S(1)}, f32[80,128]{1,0:T(8,128)S(1)}, u32[]{:S(2)}, u32[]{:S(2)}) %collective-permute-start.26) | collective-permute-done | bytes 40992 | tf_op jit(solution)/shard_map/ppermute | solution.py:586
  93.1 0.8 collective-permute-start.17
  93.9 4.1 %collective-permute-done.17 = f32[72,128]{1,0:T(8,128)S(1)} collective-permute-done((f32[72,128]{1,0:T(8,128)S(1)}, f32[72,128]{1,0:T(8,128)S(1)}, u32[]{:S(2)}, u32[]{:S(2)}) %collective-permute-start.17) | collective-permute-done | bytes 36896 | tf_op jit(solution)/shard_map/ppermute | solution.py:586
  97.9 0.8 collective-permute-start.27
  98.8 0.9 assemble.1
  99.7 1.3 %front_back.1 = f32[64,4,480]{2,1,0:T(4,128)} custom-call(s32[1]{0:T(128)} %bitcast.view_ref, f32[4,64,512]{2,1,0:T(8,128)S(1)} %get-tuple-element.87.dn_ref, f32[64,512]{1,0:T(8,128)S(1)} %collective-permute-done.11.above_ref, f32[64,512]{1,0:T(8,128)S(1)} %collective-permute-done.12.below_ref, f32[4,64,512]{2,1,0:T(8,128)S(1)} %get-tuple-element.61.band_ref, ...), custom_call_target="tpu_custom_call" | custom-call | tf_op jit(solution)/shard_map/front_back/pallas_call | solution.py:573
  101.0 1.9 %collective-permute-done.27 = f32[80,128]{1,0:T(8,128)S(1)} collective-permute-done((f32[80,128]{1,0:T(8,128)S(1)}, f32[80,128]{1,0:T(8,128)S(1)}, u32[]{:S(2)}, u32[]{:S(2)}) %collective-permute-start.27) | collective-permute-done | bytes 40992 | tf_op jit(solution)/shard_map/ppermute | solution.py:586
  102.9 0.7 finish.1
  (51 shorter events, 0.2 us)
Async XLA Ops:
  0.6 0.7 copy-start.13
  1.3 1.0 %copy-start.4 = (f32[1,1,64,4,480]{4,3,2,1,0:T(4,128)S(1)}, f32[1,1,64,4,480]{4,3,2,1,0:T(4,128)}, u32[]{:S(2)}) copy-start(f32[1,1,64,4,480]{4,3,2,1,0:T(4,128)} %param.14) | copy-start | bytes 1474564
  2.3 0.8 copy-start.8
  3.1 0.8 copy-start.9
  3.9 6.6 %copy-start.5 = (f32[1,1,64,4,480]{4,3,2,1,0:T(4,128)S(1)}, f32[1,1,64,4,480]{4,3,2,1,0:T(4,128)}, u32[]{:S(2)}) copy-start(f32[1,1,64,4,480]{4,3,2,1,0:T(4,128)} %param.15) | copy-start | bytes 1474564
  3.9 6.6 %copy-start.6 = (f32[128,64]{0,1:T(8,128)S(1)}, f32[128,64]{0,1:T(8,128)}, u32[]{:S(2)}) copy-start(f32[128,64]{0,1:T(8,128)} %param.16) | copy-start | bytes 98308
  4.0 9.7 %collective-permute-start = (f32[64,512]{1,0:T(8,128)S(1)}, f32[64,512]{1,0:T(8,128)S(1)}, u32[]{:S(2)}, u32[]{:S(2)}) collective-permute-start(f32[64,512]{1,0:T(8,128)S(1)} %get-tuple-element.64), channel_id=1, source_target_pairs={{0,2},{2,4},{4,6},{1,3},{3,5},{5,7},{8,10},{10,12},{12,14},{9,11},... | collective-permute-start | bytes 393224 | tf_op jit(solution)/shard_map/ppermute | solution.py:646
  9.1 6.9 %collective-permute-start.1 = (f32[64,512]{1,0:T(8,128)S(1)}, f32[64,512]{1,0:T(8,128)S(1)}, u32[]{:S(2)}, u32[]{:S(2)}) collective-permute-start(f32[64,512]{1,0:T(8,128)S(1)} %get-tuple-element.65), channel_id=1, source_target_pairs={{2,0},{4,2},{6,4},{3,1},{5,3},{7,5},{10,8},{12,10},{14,12},{11,9},... | collective-permute-start | bytes 393224 | tf_op jit(solution)/shard_map/ppermute | solution.py:647
  10.4 0.7 copy-start.7
  16.0 10.3 %copy-start.1 = (f32[64,64]{1,0:T(8,128)S(1)}, f32[64,64]{1,0:T(8,128)}, u32[]{:S(2)}) copy-start(f32[64,64]{1,0:T(8,128)} %w3.1) | copy-start | bytes 49156
  16.0 10.3 %copy-start.2 = (f32[128,64]{0,1:T(8,128)S(1)}, f32[128,64]{0,1:T(8,128)}, u32[]{:S(2)}) copy-start(f32[128,64]{0,1:T(8,128)} %param.22) | copy-start | bytes 98308
  16.0 10.3 %copy-start.3 = (f32[64,64]{1,0:T(8,128)S(1)}, f32[64,64]{1,0:T(8,128)}, u32[]{:S(2)}) copy-start(f32[64,64]{1,0:T(8,128)} %w6.1) | copy-start | bytes 49156
  18.0 8.2 %copy-start = (f32[64,64]{1,0:T(8,128)S(1)}, f32[64,64]{1,0:T(8,128)}, u32[]{:S(2)}) copy-start(f32[64,64]{1,0:T(8,128)} %w1.1) | copy-start | bytes 49156
  18.0 3.7 %collective-permute-start.2 = (f32[8,128]{1,0:T(8,128)S(1)}, f32[8,128]{1,0:T(8,128)S(1)}, u32[]{:S(2)}, u32[]{:S(2)}) collective-permute-start(f32[8,128]{1,0:T(8,128)S(1)} %get-tuple-element.67), channel_id=1, source_target_pairs={{0,2},{2,0},{4,6},{6,4},{1,3},{3,1},{5,7},{7,5},{8,10},{10,8},{12,... | collective-permute-start | bytes 12296 | tf_op jit(solution)/shard_map/ppermute | solution.py:586
  21.7 4.5 %collective-permute-start.3 = (f32[8,128]{1,0:T(8,128)S(1)}, f32[8,128]{1,0:T(8,128)S(1)}, u32[]{:S(2)}, u32[]{:S(2)}) collective-permute-start(f32[8,128]{1,0:T(8,128)S(1)} %add.57), channel_id=1, source_target_pairs={{0,4},{2,6},{4,0},{6,2},{1,5},{3,7},{5,1},{7,3},{8,12},{10,14},{12... | collective-permute-start | bytes 12296 | tf_op jit(solution)/shard_map/ppermute | solution.py:586
  24.3 11.9 %collective-permute-start.5 = (f32[2,64,512]{2,1,0:T(8,128)S(1)}, f32[2,64,512]{2,1,0:T(8,128)S(1)}, u32[]{:S(2)}, u32[]{:S(2)}) collective-permute-start(f32[2,64,512]{2,1,0:T(8,128)S(1)} %get-tuple-element.71), channel_id=1, source_target_pairs={{0,1},{1,0},{2,3},{3,2},{4,5},{5,4},{6,7},{7,6},{8,9},{9,8},{10,11... | collective-permute-start | bytes 786440 | tf_op jit(solution)/shard_map/ppermute | solution.py:586
  26.2 0.7 copy-start.10
  26.2 0.7 copy-start.11
  26.2 0.7 copy-start.12
  28.1 8.1 %collective-permute-start.4 = (f32[2,64,512]{2,1,0:T(8,128)S(1)}, f32[2,64,512]{2,1,0:T(8,128)S(1)}, u32[]{:S(2)}, u32[]{:S(2)}) collective-permute-start(f32[2,64,512]{2,1,0:T(8,128)S(1)} %get-tuple-element.69), channel_id=1, source_target_pairs={{0,1},{1,0},{2,3},{3,2},{4,5},{5,4},{6,7},{7,6},{8,9},{9,8},{10,11... | collective-permute-start | bytes 786440 | tf_op jit(solution)/shard_map/ppermute | solution.py:586
  29.6 6.6 %collective-permute-start.6 = (f32[72,128]{1,0:T(8,128)S(1)}, f32[72,128]{1,0:T(8,128)S(1)}, u32[]{:S(2)}, u32[]{:S(2)}) collective-permute-start(f32[72,128]{1,0:T(8,128)S(1)} %get-tuple-element.72.pack0_ref), channel_id=1, source_target_pairs={{0,1},{1,0},{2,3},{3,2},{4,5},{5,4},{6,7},{7,6},{8,9},{9,8},{10,11... | collective-permute-start | bytes 110600 | tf_op jit(solution)/shard_map/ppermute | solution.py:586
  40.9 6.4 %collective-permute-start.8 = (f32[2,64,512]{2,1,0:T(8,128)S(1)}, f32[2,64,512]{2,1,0:T(8,128)S(1)}, u32[]{:S(2)}, u32[]{:S(2)}) collective-permute-start(f32[2,64,512]{2,1,0:T(8,128)S(1)} %get-tuple-element.79), channel_id=1, source_target_pairs={{0,1},{1,0},{2,3},{3,2},{4,5},{5,4},{6,7},{7,6},{8,9},{9,8},{10,11... | collective-permute-start | bytes 786440 | tf_op jit(solution)/shard_map/ppermute | solution.py:586
  48.9 1.3 %collective-permute-start.18 = (f32[192,128]{1,0:T(8,128)S(1)}, f32[192,128]{1,0:T(8,128)S(1)}, u32[]{:S(2)}, u32[]{:S(2)}) collective-permute-start(f32[192,128]{1,0:T(8,128)S(1)} %get-tuple-element.94), channel_id=1, source_target_pairs={{0,8},{8,0},{16,24},{24,16},{1,9},{9,1},{17,25},{25,17},{2,10},{10... | collective-permute-start | bytes 294920 | tf_op jit(solution)/shard_map/ppermute | solution.py:586
  50.3 4.9 %collective-permute-start.19 = (f32[192,128]{1,0:T(8,128)S(1)}, f32[192,128]{1,0:T(8,128)S(1)}, u32[]{:S(2)}, u32[]{:S(2)}) collective-permute-start(f32[192,128]{1,0:T(8,128)S(1)} %add.66), channel_id=1, source_target_pairs={{0,16},{8,24},{16,0},{24,8},{1,17},{9,25},{17,1},{25,9},{2,18},{10... | collective-permute-start | bytes 294920 | tf_op jit(solution)/shard_map/ppermute | solution.py:586
  55.2 14.6 %collective-permute-start.20 = (f32[192,128]{1,0:T(8,128)S(1)}, f32[192,128]{1,0:T(8,128)S(1)}, u32[]{:S(2)}, u32[]{:S(2)}) collective-permute-start(f32[192,128]{1,0:T(8,128)S(1)} %add.67), channel_id=1, source_target_pairs={{0,1},{1,0},{2,3},{3,2},{4,5},{5,4},{6,7},{7,6},{8,9},{9,8},{10,11... | collective-permute-start | bytes 294920 | tf_op jit(solution)/shard_map/ppermute | solution.py:586
  56.6 3.6 %collective-permute-start.9 = (f32[8,128]{1,0:T(8,128)S(1)}, f32[8,128]{1,0:T(8,128)S(1)}, u32[]{:S(2)}, u32[]{:S(2)}) collective-permute-start(f32[8,128]{1,0:T(8,128)S(1)} %get-tuple-element.84), channel_id=1, source_target_pairs={{0,2},{2,0},{4,6},{6,4},{1,3},{3,1},{5,7},{7,5},{8,10},{10,8},{12,... | collective-permute-start | bytes 12296 | tf_op jit(solution)/shard_map/ppermute | solution.py:586
  58.0 40.7 %collective-permute-start.7 = (f32[2,64,512]{2,1,0:T(8,128)S(1)}, f32[2,64,512]{2,1,0:T(8,128)S(1)}, u32[]{:S(2)}, u32[]{:S(2)}) collective-permute-start(f32[2,64,512]{2,1,0:T(8,128)S(1)} %get-tuple-element.74), channel_id=1, source_target_pairs={{0,1},{1,0},{2,3},{3,2},{4,5},{5,4},{6,7},{7,6},{8,9},{9,8},{10,11... | collective-permute-start | bytes 786440 | tf_op jit(solution)/shard_map/ppermute | solution.py:586
  60.2 4.5 %collective-permute-start.10 = (f32[8,128]{1,0:T(8,128)S(1)}, f32[8,128]{1,0:T(8,128)S(1)}, u32[]{:S(2)}, u32[]{:S(2)}) collective-permute-start(f32[8,128]{1,0:T(8,128)S(1)} %add.59), channel_id=1, source_target_pairs={{0,4},{2,6},{4,0},{6,2},{1,5},{3,7},{5,1},{7,3},{8,12},{10,14},{12... | collective-permute-start | bytes 12296 | tf_op jit(solution)/shard_map/ppermute | solution.py:586
  68.9 2.2 %collective-permute-start.23 = (f32[80,128]{1,0:T(8,128)S(1)}, f32[80,128]{1,0:T(8,128)S(1)}, u32[]{:S(2)}, u32[]{:S(2)}) collective-permute-start(f32[80,128]{1,0:T(8,128)S(1)} %get-tuple-element.95), channel_id=1, source_target_pairs={{0,8},{8,0},{16,24},{24,16},{1,9},{9,1},{17,25},{25,17},{2,10},{10... | collective-permute-start | bytes 122888 | tf_op jit(solution)/shard_map/ppermute | solution.py:586
  69.0 4.0 %collective-permute-start.13 = (f32[72,128]{1,0:T(8,128)S(1)}, f32[72,128]{1,0:T(8,128)S(1)}, u32[]{:S(2)}, u32[]{:S(2)}) collective-permute-start(f32[72,128]{1,0:T(8,128)S(1)} %get-tuple-element.93), channel_id=1, source_target_pairs={{0,1},{1,0},{2,3},{3,2},{4,5},{5,4},{6,7},{7,6},{8,9},{9,8},{10,11... | collective-permute-start | bytes 110600 | tf_op jit(solution)/shard_map/ppermute | solution.py:586
  69.8 16.2 %collective-permute-start.21 = (f32[192,128]{1,0:T(8,128)S(1)}, f32[192,128]{1,0:T(8,128)S(1)}, u32[]{:S(2)}, u32[]{:S(2)}) collective-permute-start(f32[192,128]{1,0:T(8,128)S(1)} %add.68), channel_id=1, source_target_pairs={{0,2},{2,0},{4,6},{6,4},{1,3},{3,1},{5,7},{7,5},{8,10},{10,8},{12,... | collective-permute-start | bytes 294920 | tf_op jit(solution)/shard_map/ppermute | solution.py:586
  71.1 4.1 %collective-permute-start.24 = (f32[80,128]{1,0:T(8,128)S(1)}, f32[80,128]{1,0:T(8,128)S(1)}, u32[]{:S(2)}, u32[]{:S(2)}) collective-permute-start(f32[80,128]{1,0:T(8,128)S(1)} %add.71), channel_id=1, source_target_pairs={{0,16},{8,24},{16,0},{24,8},{1,17},{9,25},{17,1},{25,9},{2,18},{10... | collective-permute-start | bytes 122888 | tf_op jit(solution)/shard_map/ppermute | solution.py:586
  73.0 3.7 %collective-permute-start.14 = (f32[72,128]{1,0:T(8,128)S(1)}, f32[72,128]{1,0:T(8,128)S(1)}, u32[]{:S(2)}, u32[]{:S(2)}) collective-permute-start(f32[72,128]{1,0:T(8,128)S(1)} %add.61), channel_id=1, source_target_pairs={{0,8},{8,0},{16,24},{24,16},{1,9},{9,1},{17,25},{25,17},{2,10},{10... | collective-permute-start | bytes 110600 | tf_op jit(solution)/shard_map/ppermute | solution.py:586
  75.2 9.5 %collective-permute-start.25 = (f32[80,128]{1,0:T(8,128)S(1)}, f32[80,128]{1,0:T(8,128)S(1)}, u32[]{:S(2)}, u32[]{:S(2)}) collective-permute-start(f32[80,128]{1,0:T(8,128)S(1)} %add.72), channel_id=1, source_target_pairs={{0,1},{1,0},{2,3},{3,2},{4,5},{5,4},{6,7},{7,6},{8,9},{9,8},{10,11... | collective-permute-start | bytes 122888 | tf_op jit(solution)/shard_map/ppermute | solution.py:586
  76.7 4.0 %collective-permute-start.15 = (f32[72,128]{1,0:T(8,128)S(1)}, f32[72,128]{1,0:T(8,128)S(1)}, u32[]{:S(2)}, u32[]{:S(2)}) collective-permute-start(f32[72,128]{1,0:T(8,128)S(1)} %add.62), channel_id=1, source_target_pairs={{0,16},{8,24},{16,0},{24,8},{1,17},{9,25},{17,1},{25,9},{2,18},{10... | collective-permute-start | bytes 110600 | tf_op jit(solution)/shard_map/ppermute | solution.py:586
  80.7 8.0 %collective-permute-start.16 = (f32[72,128]{1,0:T(8,128)S(1)}, f32[72,128]{1,0:T(8,128)S(1)}, u32[]{:S(2)}, u32[]{:S(2)}) collective-permute-start(f32[72,128]{1,0:T(8,128)S(1)} %add.63), channel_id=1, source_target_pairs={{0,2},{2,0},{4,6},{6,4},{1,3},{3,1},{5,7},{7,5},{8,10},{10,8},{12,... | collective-permute-start | bytes 110600 | tf_op jit(solution)/shard_map/ppermute | solution.py:586
  81.3 18.3 %collective-permute-start.11 = (f32[64,512]{1,0:T(8,128)S(1)}, f32[64,512]{1,0:T(8,128)S(1)}, u32[]{:S(2)}, u32[]{:S(2)}) collective-permute-start(f32[64,512]{1,0:T(8,128)S(1)} %get-tuple-element.88), channel_id=1, source_target_pairs={{0,2},{2,4},{4,6},{1,3},{3,5},{5,7},{8,10},{10,12},{12,14},{9,11},... | collective-permute-start | bytes 393224 | tf_op jit(solution)/shard_map/ppermute | solution.py:766
  84.7 15.0 %collective-permute-start.12 = (f32[64,512]{1,0:T(8,128)S(1)}, f32[64,512]{1,0:T(8,128)S(1)}, u32[]{:S(2)}, u32[]{:S(2)}) collective-permute-start(f32[64,512]{1,0:T(8,128)S(1)} %get-tuple-element.89), channel_id=1, source_target_pairs={{2,0},{4,2},{6,4},{3,1},{5,3},{7,5},{10,8},{12,10},{14,12},{11,9},... | collective-permute-start | bytes 393224 | tf_op jit(solution)/shard_map/ppermute | solution.py:767
  86.0 7.1 %collective-permute-start.26 = (f32[80,128]{1,0:T(8,128)S(1)}, f32[80,128]{1,0:T(8,128)S(1)}, u32[]{:S(2)}, u32[]{:S(2)}) collective-permute-start(f32[80,128]{1,0:T(8,128)S(1)} %add.73), channel_id=1, source_target_pairs={{0,2},{2,0},{4,6},{6,4},{1,3},{3,1},{5,7},{7,5},{8,10},{10,8},{12,... | collective-permute-start | bytes 122888 | tf_op jit(solution)/shard_map/ppermute | solution.py:586
  88.7 14.1 %collective-permute-start.22 = (f32[192,128]{1,0:T(8,128)S(1)}, f32[192,128]{1,0:T(8,128)S(1)}, u32[]{:S(2)}, u32[]{:S(2)}) collective-permute-start(f32[192,128]{1,0:T(8,128)S(1)} %add.69), channel_id=1, source_target_pairs={{0,4},{2,6},{4,0},{6,2},{1,5},{3,7},{5,1},{7,3},{8,12},{10,14},{12... | collective-permute-start | bytes 294920 | tf_op jit(solution)/shard_map/ppermute | solution.py:586
  93.1 4.9 %collective-permute-start.17 = (f32[72,128]{1,0:T(8,128)S(1)}, f32[72,128]{1,0:T(8,128)S(1)}, u32[]{:S(2)}, u32[]{:S(2)}) collective-permute-start(f32[72,128]{1,0:T(8,128)S(1)} %add.64), channel_id=1, source_target_pairs={{0,4},{2,6},{4,0},{6,2},{1,5},{3,7},{5,1},{7,3},{8,12},{10,14},{12... | collective-permute-start | bytes 110600 | tf_op jit(solution)/shard_map/ppermute | solution.py:586
  97.9 4.9 %collective-permute-start.27 = (f32[80,128]{1,0:T(8,128)S(1)}, f32[80,128]{1,0:T(8,128)S(1)}, u32[]{:S(2)}, u32[]{:S(2)}) collective-permute-start(f32[80,128]{1,0:T(8,128)S(1)} %add.74), channel_id=1, source_target_pairs={{0,4},{2,6},{4,0},{6,2},{1,5},{3,7},{5,1},{7,3},{8,12},{10,14},{12... | collective-permute-start | bytes 122888 | tf_op jit(solution)/shard_map/ppermute | solution.py:586

commit v2 on v1

--- a/solution.py
+++ b/solution.py
@@ -7,10 +7,12 @@
 from jax.experimental.pallas import tpu as pltpu
 from jax.sharding import PartitionSpec as P
 
+
 epsilon = 1e-06
 F32 = jnp.float32
 BF16 = jnp.bfloat16
 MIB = 1 << 20
+UNROLL = 2
 
 
 def split(x):
@@ -98,14 +100,63 @@
             o_ref[h, :, width:padded] = jnp.zeros((o_ref.shape[1], padded - width), F32)
 
 
-def start_kernel(x_ref, q_ref, v_ref, s_ref, band_ref, first_ref, last_ref, pack_ref):
-    ch = q_ref.shape[0]
+def pack_square(o_ref, base, left, right, row):
+    ch = left.shape[0]
+    lines = 2 * ch * ch // o_ref.shape[1]
+    span = 2 * ch
+    o_ref[base : base + lines + 8, :] = jnp.zeros((lines + 8, o_ref.shape[1]), F32)
+    for t in range(ch // lines):
+        at = slice(t * lines, (t + 1) * lines)
+        o_ref[base : base + lines, t * span : t * span + ch] = left[at]
+        o_ref[base : base + lines, t * span + ch : (t + 1) * span] = right[at]
+    o_ref[base + lines : base + lines + 8, 0:ch] = jnp.broadcast_to(row, (8, ch))
+
+
+def unpack_square(x_ref, base, ch):
+    lines = 2 * ch * ch // x_ref.shape[1]
+    span = 2 * ch
+    wide = jnp.concatenate([x_ref[base : base + lines, t * span : (t + 1) * span] for t in range(ch // lines)], axis=0)
+    return wide[:, :ch], wide[:, ch:], x_ref[base + lines : base + lines + 1, 0:ch]
+
+
+def start_kernel(
+    view_ref,
+    core_ref,
+    x_hbm,
+    cot_hbm,
+    q_hbm,
+    v_hbm,
+    s_hbm,
+    band_ref,
+    first_ref,
+    last_ref,
+    keep_ref,
+    send_ref,
+    x_ref,
+    cot_ref,
+    q_ref,
+    v_ref,
+    s_ref,
+    scratch_ref,
+    sems,
+):
+    pairs = ((x_hbm, x_ref), (cot_hbm, cot_ref), (q_hbm, q_ref), (v_hbm, v_ref), (s_hbm, s_ref))
+    copies = [pltpu.make_async_copy(src, dst, sems.at[i]) for i, (src, dst) in enumerate(pairs)]
+    for copy in copies:
+        copy.start()
+    half, ch, _ = keep_ref.shape
+    view = view_ref[0]
+    copies[0].wait()
     relayout(x_ref, band_ref)
     first_ref[...] = band_ref[0]
-    last_ref[...] = band_ref[band_ref.shape[0] - 1]
-    pack_ref[0:ch, 0:ch] = q_ref[...]
-    pack_ref[0:ch, ch : 2 * ch] = v_ref[...]
-    pack_ref[ch : ch + 8, 0:ch] = jnp.broadcast_to(s_ref[...], (8, ch))
+    last_ref[...] = band_ref[2 * half - 1]
+    for copy in copies[1:]:
+        copy.wait()
+    relayout(cot_ref, scratch_ref)
+    for k in range(half):
+        keep_ref[k] = scratch_ref[half * view + k]
+        send_ref[k * ch : (k + 1) * ch, :] = scratch_ref[half * (1 - view) + k]
+    pack_square(send_ref, half * ch, q_ref[...], v_ref[...], s_ref[...])
 
 
 def kernel_columns(k_ref, kt_ref):
@@ -123,49 +174,12 @@
     return pltpu.roll(x, 1, 1), x, pltpu.roll(x, n - 1, 1)
 
 
-def conv_own_kernel(
-    view_ref, band_ref, exp_ref, k_ref, cot_ref, doubled_ref, conv_ref, send_ref, keep_ref, kt_ref, cband_ref
-):
+def conv_own_kernel(width, band_ref, exp_ref, k_ref, doubled_ref, conv_ref, gating_ref, pool_ref, taps_ref):
     rows, ch, padded = band_ref.shape
-    half = rows // 2
-    wide = doubled_ref.shape[1]
-    kernel_columns(k_ref, kt_ref)
+    kernel_columns(k_ref, taps_ref)
     weight = left_rows(exp_ref[...])
     for h in range(rows):
         doubled_ref[h] = dot_tn(weight, right_rows(normed_of(band_ref[h])[0]))
-
-    def group(g, carry):
-        at = pl.ds(pl.multiple_of(g * 8, 8), 8)
-        taps = kt_ref[at, :]
-        moved = [shifted(doubled_ref[h, at, :]) for h in range(rows)]
-        for h in range(rows):
-            total = None
-            for i in range(3):
-                src = h + i - 1
-                if 0 <= src < rows:
-                    for j in range(3):
-                        term = taps[:, 3 * i + j : 3 * i + j + 1] * moved[src][j]
-                        total = term if total is None else total + term
-            conv_ref[h, at, :] = total
-        return carry
-
-    lax.fori_loop(0, wide // 8, group, 0)
-    relayout(cot_ref, cband_ref)
-    view = view_ref[0]
-    for k in range(half):
-        keep_ref[k] = cband_ref[half * view + k]
-        send_ref[k] = cband_ref[half * (1 - view) + k]
-
-
-def conv_edge_kernel(
-    width, part_ref, doubled_ref, up_ref, down_ref, exp_ref, k_ref, conv_ref, edge_ref, gating_ref, pool_ref, kt_ref
-):
-    rows, wide, padded = part_ref.shape
-    ch = wide // 2
-    kernel_columns(k_ref, kt_ref)
-    weight = left_rows(exp_ref[...])
-    edge_ref[0] = dot_tn(weight, right_rows(normed_of(up_ref[...])[0]))
-    edge_ref[1] = dot_tn(weight, right_rows(normed_of(down_ref[...])[0]))
     keep = lane_mask((8, padded), width)
 
     def group(g, carry):
@@ -173,67 +187,97 @@
         halves = []
         for offset in (0, ch):
             at = pl.ds(pl.multiple_of(lower + offset, 8), 8)
-            taps = kt_ref[at, :]
-            above, below = shifted(edge_ref[0, at, :]), shifted(edge_ref[1, at, :])
+            taps = taps_ref[at, :]
+            moved = [shifted(doubled_ref[h, at, :]) for h in range(rows)]
             out = []
             for h in range(rows):
-                total = part_ref[h, at, :]
-                for j in range(3):
-                    if h == 0:
-                        total = total + taps[:, j : j + 1] * above[j]
-                    if h == rows - 1:
-                        total = total + taps[:, 6 + j : 7 + j] * below[j]
+                total = None
+                for i in range(3):
+                    src = h + i - 1
+                    if 0 <= src < rows:
+                        for j in range(3):
+                            term = taps[:, 3 * i + j : 3 * i + j + 1] * moved[src][j]
+                            total = term if total is None else total + term
                 total = jnp.where(keep, total, 0.0)
                 conv_ref[h, at, :] = total
                 out.append(total)
             halves.append(out)
+        at = pl.ds(lower, 8)
         pooled = jnp.zeros((8, padded), F32)
-        at = pl.ds(lower, 8)
-        for h in range(rows):
+        for h in range(1, rows - 1):
             gate = halves[0][h] * halves[1][h]
             gating_ref[h, at, :] = gate
             pooled = pooled + gate
-        kt_ref[at, :] = jnp.broadcast_to(jnp.sum(pooled, axis=1, keepdims=True), (8, kt_ref.shape[1]))
+        pool_ref[at, :] = pooled
         return carry
 
-    lax.fori_loop(0, ch // 8, group, 0)
-    sums = to_row(kt_ref[0:ch, 0:1])
+    lax.fori_loop(0, ch // 8, group, 0, unroll=UNROLL)
+
+
+def conv_edge_kernel(
+    width, conv_in, gating_in, pool_in, taps_ref, up_ref, down_ref, exp_ref, conv_ref, gating_ref, edge_ref, pool_ref, sums_ref
+):
+    rows, wide, padded = conv_ref.shape
+    ch = wide // 2
+    weight = left_rows(exp_ref[...])
+    edge_ref[0] = dot_tn(weight, right_rows(normed_of(up_ref[...])[0]))
+    edge_ref[1] = dot_tn(weight, right_rows(normed_of(down_ref[...])[0]))
+    keep = lane_mask((8, padded), width)
+
+    def group(g, carry):
+        lower = pl.multiple_of(g * 8, 8)
+        gates = [None, None]
+        for offset in (0, ch):
+            at = pl.ds(pl.multiple_of(lower + offset, 8), 8)
+            taps = taps_ref[at, :]
+            for side, (h, tap) in enumerate(((0, 0), (rows - 1, 6))):
+                moved = shifted(edge_ref[side, at, :])
+                total = conv_in[h, at, :]
+                for j in range(3):
+                    total = total + jnp.where(keep, taps[:, tap + j : tap + j + 1] * moved[j], 0.0)
+                conv_ref[h, at, :] = total
+                gates[side] = total if gates[side] is None else gates[side] * total
+        at = pl.ds(lower, 8)
+        gating_ref[0, at, :] = gates[0]
+        gating_ref[rows - 1, at, :] = gates[1]
+        pooled = pool_in[at, :] + gates[0] + gates[1]
+        sums_ref[at, :] = jnp.broadcast_to(jnp.sum(pooled, axis=1, keepdims=True), (8, sums_ref.shape[1]))
+        return carry
+
+    lax.fori_loop(0, ch // 8, group, 0, unroll=UNROLL)
     pool_ref[...] = jnp.zeros(pool_ref.shape, F32)
-    pool_ref[:, 0:ch] = jnp.broadcast_to(sums, (8, ch))
-
-
-def attention_of(pool_ref, proj_ref, bias_ref, area):
+    pool_ref[:, 0:ch] = jnp.broadcast_to(to_row(sums_ref[:, 0:1]), (8, ch))
+
+
+def total_of(refs):
+    total = refs[0][...]
+    for ref in refs[1:]:
+        total = total + ref[...]
+    return total
+
+
+def base_of(view_ref, half, kept):
+    return half * view_ref[0] if kept else half * (1 - view_ref[0])
+
+
+def attention_of(pool_refs, proj_ref, bias_ref, area):
     ch = proj_ref.shape[0]
-    pooled = pool_ref[:, 0:ch] * (1.0 / area)
+    pooled = total_of(pool_refs)[:, 0:ch] * (1.0 / area)
     ph, plow = split(pooled)
     wh, wl = split(proj_ref[...])
     product = dot_nt(ph, wh) + dot_nt(ph, wl) + dot_nt(plow, wh)
     return pooled[0:1], product[0:1] + bias_ref[...]
 
 
-def tail_kernel(
-    area,
-    base_ref,
-    band_ref,
-    gating_ref,
-    pool_ref,
-    proj_ref,
-    bias_ref,
-    squeeze_ref,
-    branch_ref,
-    up_ref,
-    down_ref,
-    scale_ref,
-    hidden_ref,
-    one_ref,
-    expanded_ref,
-):
+def tail_kernel(area, kept, parts, view_ref, band_ref, gating_ref, *refs):
+    pool_refs, refs = refs[:parts], refs[parts:]
+    proj_ref, bias_ref, squeeze_ref, branch_ref, up_ref, down_ref, scale_ref, hidden_ref, one_ref, expanded_ref = refs
     half, ch, _ = hidden_ref.shape
-    _, attention = attention_of(pool_ref, proj_ref, bias_ref, area)
+    _, attention = attention_of(pool_refs, proj_ref, bias_ref, area)
     squeeze = left_lanes(to_column(branch_ref[...]) * squeeze_ref[...] * attention)
     up = left_rows(up_ref[...])
     down = left_lanes(to_column(scale_ref[...]) * down_ref[...])
-    base = base_ref[0]
+    base = base_of(view_ref, half, kept)
     for k in range(half):
         one = band_ref[base + k] + dot_nn(squeeze, right_rows(gating_ref[base + k]))
         one_ref[k] = one
@@ -247,9 +291,10 @@
     hid0_ref,
     hid1_ref,
     cot0_ref,
-    cot1_ref,
-    pack0_ref,
-    pack1_ref,
+    q_ref,
+    v_ref,
+    s_ref,
+    other_ref,
     out0_ref,
     out1_ref,
     dh0_ref,
@@ -264,10 +309,10 @@
     block = 128
     inv = ch ** (-0.5)
     mask = lane_mask((1, padded), width)
-    hids, cots = (hid0_ref, hid1_ref), (cot0_ref, cot1_ref)
-    wq = [ref[0:ch, 0:ch] for ref in (pack0_ref, pack1_ref)]
-    wv = [ref[0:ch, ch : 2 * ch] for ref in (pack0_ref, pack1_ref)]
-    scale = [to_column(ref[ch : ch + 1, 0:ch]) for ref in (pack0_ref, pack1_ref)]
+    hids = (hid0_ref, hid1_ref)
+    q_other, v_other, s_other = unpack_square(other_ref, half * ch, ch)
+    wq, wv = (q_ref[...], q_other), (v_ref[...], v_other)
+    scale = [to_column(x) for x in (s_ref[...], s_other)]
     lq, lv = [left_lanes(w) for w in wq], [left_lanes(w) for w in wv]
     lqt, lvt = [left_rows(w) for w in wq], [left_rows(w) for w in wv]
     acc_q, acc_v, acc_s = [None, None], [None, None], [None, None]
@@ -277,7 +322,7 @@
 
     for k in range(half):
         h = [ref[k] for ref in hids]
-        u = [ref[k] for ref in cots]
+        u = [cot0_ref[k], other_ref[k * ch : (k + 1) * ch, :]]
         norms = [normed_of(x) for x in h]
         q = [dot_nn(lq[s], right_rows(norms[s][0])) for s in range(2)]
         v = [dot_nn(lv[s], right_rows(h[s])) for s in range(2)]
@@ -343,39 +388,24 @@
     for s, ref in enumerate((grad0_ref, grad1_ref)):
         ref[0:ch, 0:ch] = fold(acc_q[s])
         ref[0:ch, ch : 2 * ch] = fold(acc_v[s])
-        row = to_row(jnp.sum(acc_s[s], axis=1, keepdims=True))
-        ref[ch : ch + 8, 0:ch] = jnp.broadcast_to(row, (8, ch))
-        ref[ch : ch + 8, ch : 2 * ch] = jnp.zeros((8, ch), F32)
-
-
-def tail_back_kernel(
-    area,
-    final,
-    base_ref,
-    dh_ref,
-    one_ref,
-    expanded_ref,
-    gating_ref,
-    pool_ref,
-    proj_ref,
-    bias_ref,
-    squeeze_ref,
-    branch_ref,
-    up_ref,
-    down_ref,
-    scale_ref,
-    *refs,
-):
+        ref[ch : ref.shape[0], :] = jnp.zeros((ref.shape[0] - ch, 2 * ch), F32)
+        ref[ch : ch + 1, 0:ch] = to_row(jnp.sum(acc_s[s], axis=1, keepdims=True))
+
+
+def tail_back_kernel(area, final, parts, view_ref, dh_ref, one_ref, expanded_ref, gating_ref, *refs):
+    pool_refs, refs = refs[:parts], refs[parts:]
+    proj_ref, bias_ref, squeeze_ref, branch_ref, up_ref, down_ref, scale_ref = refs[:7]
+    refs = refs[7:]
     half, ch, _ = dh_ref.shape
-    base = base_ref[0]
-    pooled, attention = attention_of(pool_ref, proj_ref, bias_ref, area)
+    base = base_of(view_ref, half, not final)
+    pooled, attention = attention_of(pool_refs, proj_ref, bias_ref, area)
     branch, scale = to_column(branch_ref[...]), to_column(scale_ref[...])
     mixed = branch * squeeze_ref[...]
     squeeze = left_rows(mixed * attention)
     up = left_lanes(up_ref[...])
     down = left_rows(scale * down_ref[...])
     if final:
-        acc_in, dgate_in, done_in, (dgate_ref, done_ref, pg_ref, grad_ref) = refs[0], refs[1], refs[2], refs[3:]
+        acc_in, dgate_ref, done_ref, pg_ref, grad_ref = refs
     else:
         dgate_ref, done_ref, acc_ref = refs
     acc1 = acc2 = acc3 = None
@@ -420,12 +450,17 @@
     grad_ref[2 * ch : 3 * ch, ch : 2 * ch] = vectors
 
 
-def conv_back_kernel(
+def conv_back_kernel(width, parts, view_ref, core_ref, *refs):
+    conv_back_body(width, view_ref, core_ref, refs[:parts], *refs[parts:])
+
+
+def conv_back_body(
     width,
     view_ref,
+    core_ref,
+    pg_refs,
     dkeep_ref,
     dsend_ref,
-    pg_ref,
     conv_ref,
     doubled_ref,
     edge_ref,
@@ -433,12 +468,16 @@
     up_ref,
     down_ref,
     exp_ref,
-    k_ref,
+    kt_ref,
+    own_ref,
+    other_ref,
+    gradb_ref,
     dn_ref,
     dnup_ref,
     dndown_ref,
-    grad_ref,
-    kt_ref,
+    mine_ref,
+    theirs_ref,
+    all_ref,
     dgate_ref,
     bg_ref,
     gk_ref,
@@ -448,8 +487,7 @@
     ch = wide // 2
     half = rows // 2
     view = view_ref[0]
-    kernel_columns(k_ref, kt_ref)
-    pgcol_ref[...] = jnp.broadcast_to(to_column(pg_ref[0:1, 0:ch]), pgcol_ref.shape)
+    pgcol_ref[...] = jnp.broadcast_to(to_column(total_of(pg_refs)[0:1, 0:ch]), pgcol_ref.shape)
     for k in range(half):
         dgate_ref[half * view + k] = dkeep_ref[k]
         dgate_ref[half * (1 - view) + k] = dsend_ref[k]
@@ -499,7 +537,7 @@
             gk_ref[own, :] = packed
         return carry
 
-    lax.fori_loop(0, ch // 8, group, 0)
+    lax.fori_loop(0, ch // 8, group, 0, unroll=UNROLL)
     weight = left_lanes(exp_ref[...])
     acc = None
     for r in range(rows + 2):
@@ -514,8 +552,18 @@
             dndown_ref[...] = value
         else:
             dn_ref[r - 1] = value
-    grad_ref[0:ch, :] = fold(acc)
-    grad_ref[ch : ch + 16, :] = gk_ref[...].T[0:16, :]
+    at = gradb_ref.shape[0]
+    all_ref[0:at, :] = gradb_ref[...]
+    all_ref[at : at + ch, :] = fold(acc)
+    all_ref[at + ch : at + ch + 16, :] = gk_ref[...].T[0:16, :]
+    core = core_ref[0]
+    place = 0
+    for ref in (all_ref, own_ref, other_ref):
+        lines = ref.shape[0] // 2
+        at = slice(place, place + lines)
+        mine_ref[at, :] = ref[pl.ds(pl.multiple_of(lines * core, 8), lines), :]
+        theirs_ref[at, :] = ref[pl.ds(pl.multiple_of(lines * (1 - core), 8), lines), :]
+        place += lines
 
 
 def place_rows(o_ref, row, value):
@@ -549,36 +597,78 @@
         place_rows(o_ref, h, scratch_ref[h])
 
 
-def finish_kernel(factor, a_ref, b_ref, c_ref, up_ref, down_ref, squeeze_ref, pool_ref, bias_ref, branch_ref, scale_ref, q_ref, v_ref, s_ref, exp_ref, k_ref):
+def finish_kernel(
+    factor,
+    core_ref,
+    mine_ref,
+    theirs_ref,
+    up_ref,
+    down_ref,
+    squeeze_ref,
+    pool_ref,
+    bias_ref,
+    branch_ref,
+    scale_ref,
+    exp_ref,
+    k_ref,
+    q_ref,
+    v_ref,
+    s_ref,
+    all_ref,
+    own_ref,
+):
     ch = q_ref.shape[0]
-    q_ref[...] = a_ref[0:ch, 0:ch] * factor
-    v_ref[...] = a_ref[0:ch, ch : 2 * ch] * factor
-    s_ref[...] = a_ref[ch : ch + 1, 0:ch] * factor
-    up_ref[...] = b_ref[0:ch, :] * factor
-    down_ref[...] = b_ref[ch : 2 * ch, 0:ch] * factor
-    squeeze_ref[...] = b_ref[ch : 2 * ch, ch : 2 * ch] * factor
-    pool_ref[...] = b_ref[2 * ch : 3 * ch, 0:ch] * factor
-    bias_ref[...] = b_ref[2 * ch : 2 * ch + 1, ch : 2 * ch] * factor
-    branch_ref[...] = b_ref[2 * ch + 1 : 2 * ch + 2, ch : 2 * ch] * factor
-    scale_ref[...] = b_ref[2 * ch + 2 : 2 * ch + 3, ch : 2 * ch] * factor
-    exp_ref[...] = c_ref[0:ch, :] * factor
+    core = core_ref[0]
+    place = 0
+    for ref in (all_ref, own_ref):
+        lines = ref.shape[0] // 2
+        at = slice(place, place + lines)
+        ref[pl.ds(pl.multiple_of(lines * core, 8), lines), :] = mine_ref[at, :] * factor
+        ref[pl.ds(pl.multiple_of(lines * (1 - core), 8), lines), :] = theirs_ref[at, :] * factor
+        place += lines
+    up_ref[...] = all_ref[0:ch, :]
+    down_ref[...] = all_ref[ch : 2 * ch, 0:ch]
+    squeeze_ref[...] = all_ref[ch : 2 * ch, ch : 2 * ch]
+    at = 2 * ch
+    pool_ref[...] = all_ref[at : at + ch, 0:ch]
+    bias_ref[...] = all_ref[at : at + 1, ch : 2 * ch]
+    branch_ref[...] = all_ref[at + 1 : at + 2, ch : 2 * ch]
+    scale_ref[...] = all_ref[at + 2 : at + 3, ch : 2 * ch]
+    at = at + ch
+    exp_ref[...] = all_ref[at : at + ch, :]
+    at = at + ch
     for i in range(3):
-        k_ref[i] = c_ref[ch + 3 * i : ch + 3 * i + 3, :] * factor
-
-
-def call(kernel, outs, *args, scalars=0, scratch=(), name=None, cost=None):
+        k_ref[i] = all_ref[at + 3 * i : at + 3 * i + 3, :]
+    q_ref[...] = own_ref[0:ch, 0:ch]
+    v_ref[...] = own_ref[0:ch, ch : 2 * ch]
+    s_ref[...] = own_ref[ch : ch + 1, 0:ch]
+
+
+def add_kernel(mine_ref, other_ref, o_ref):
+    o_ref[...] = mine_ref[...] + other_ref[...]
+
+
+def add_split_kernel(mine_ref, other_ref, keep_ref, send_ref):
+    total, both = mine_ref.shape[0], keep_ref.shape[0]
+    owned = total - both
+    keep_ref[...] = mine_ref[0:both, :] + other_ref[0:both, :]
+    send_ref[0 : both - owned, :] = keep_ref[0 : both - owned, :]
+    send_ref[both - owned : both, :] = mine_ref[both:total, :] + other_ref[both:total, :]
+
+
+def call(kernel, outs, *args, scalars=0, far=0, scratch=(), aliases=None, limit=12 * MIB):
     smem = pl.BlockSpec(memory_space=pltpu.SMEM)
     vmem = pl.BlockSpec(memory_space=pltpu.VMEM)
+    hbm = pl.BlockSpec(memory_space=pltpu.HBM)
     shapes = tuple(jax.ShapeDtypeStruct(s, F32) for s in outs)
     return pl.pallas_call(
         kernel,
         out_shape=shapes,
-        in_specs=[smem] * scalars + [vmem] * (len(args) - scalars),
+        in_specs=[smem] * scalars + [hbm] * far + [vmem] * (len(args) - scalars - far),
         out_specs=(vmem,) * len(shapes),
         scratch_shapes=list(scratch),
-        compiler_params=pltpu.CompilerParams(vmem_limit_bytes=28 * MIB),
-        name=name,
-        cost_estimate=cost,
+        compiler_params=pltpu.CompilerParams(vmem_limit_bytes=limit),
+        input_output_aliases=aliases or {},
     )(*args)
 
 
@@ -586,17 +676,24 @@
     return lax.ppermute(x, axis, [(i, i ^ mask) for i in range(lax.axis_size(axis))])
 
 
-def sum_over(x, *axes):
-    for axis in axes:
-        size = lax.axis_size(axis)
-        if size & (size - 1):
-            x = lax.psum(x, axis)
-            continue
-        mask = 1
-        while mask < size:
-            x = x + swap(x, axis, mask)
-            mask *= 2
+def add(x, y):
+    return call(add_kernel, [x.shape], x, y)[0]
+
+
+def sum_over(x, axis, first=1):
+    size, mask = lax.axis_size(axis), first
+    if size & (size - 1):
+        raise ValueError("axis size")
+    while mask < size:
+        x = add(x, swap(x, axis, mask))
+        mask *= 2
     return x
+
+
+def parts_over(x, axis):
+    if lax.axis_size(axis) > 4:
+        return (sum_over(x, axis),)
+    return (x,) + tuple(swap(x, axis, mask) for mask in range(1, lax.axis_size(axis)))
 
 
 def per_device(
@@ -624,7 +721,7 @@
     area = rows * bands * width
     factor = (2 * frames * lax.axis_size("dp") * area) ** (-0.5)
     view = lax.axis_index("view").astype(jnp.int32).reshape(1)
-    keep_base, send_base = half * view, half * (1 - view)
+    core = (lax.axis_index("dp").astype(jnp.int32) & 1).reshape(1)
     part, full = (half, ch, padded), (rows, ch, padded)
     row = (ch, padded)
     exp_t, up_t = expand_in.T, ffn_expand.T
@@ -632,96 +729,96 @@
     bias, branch, scale = (x.reshape(1, ch) for x in (pool_bias, branch_scale, ffn_scale))
     vm = lambda *shape: pltpu.VMEM(shape, F32)
 
-    band, first, last, pack = call(
+    lines = half * ch + wide * ch // padded + 8
+    query, value = query_proj[0], value_proj[0]
+    image = vm(ch, rows, width)
+    band, first, last, cot_keep, pack = call(
         start_kernel,
-        [full, row, row, (ch + 8, wide)],
+        [full, row, row, part, (lines, padded)],
+        view,
+        core,
         frames_in[0, 0],
-        query_proj[0],
-        value_proj[0],
+        cotangent[0, 0],
+        query,
+        value,
         cross_scale,
-        name="start",
+        scalars=2,
+        far=5,
+        scratch=[image, image, vm(ch, ch), vm(ch, ch), vm(1, ch), vm(rows, ch, padded), pltpu.SemaphoreType.DMA((5,))],
+        limit=67043328 - 4 * padded * (rows * ch + 2 * ch + half * ch + lines) * 17 // 16,
     )
     up_pairs = [(i, i + 1) for i in range(bands - 1)]
     down_pairs = [(i + 1, i) for i in range(bands - 1)]
     above = lax.ppermute(last, "row", up_pairs)
     below = lax.ppermute(first, "row", down_pairs)
-    pack_other = swap(pack, "view", 1)
-    doubled, conv_part, cot_send, cot_keep = call(
-        conv_own_kernel,
-        [(rows, wide, padded)] * 2 + [part] * 2,
-        view,
+    other = swap(pack, "view", 1)
+    doubled, conv, gating, pool, taps = call(
+        functools.partial(conv_own_kernel, width),
+        [(rows, wide, padded)] * 2 + [full, row, (wide, wide)],
         band,
         exp_t,
         k_rows,
-        cotangent[0, 0],
-        scalars=1,
-        scratch=[vm(wide, wide), vm(rows, ch, padded)],
-        name="conv_own",
-    )
-    cot_other = swap(cot_send, "view", 1)
-    conv, edge, gating, pool = call(
+    )
+    conv, gating, edge, pool = call(
         functools.partial(conv_edge_kernel, width),
-        [(rows, wide, padded), (2, wide, padded), full, (8, wide)],
-        conv_part,
-        doubled,
+        [(rows, wide, padded), full, (2, wide, padded), (8, wide)],
+        conv,
+        gating,
+        pool,
+        taps,
         above,
         below,
         exp_t,
-        k_rows,
-        scratch=[vm(wide, wide)],
-        name="conv_edge",
-    )
-    pool = sum_over(pool, "row")
-    weights = (pool, pool_proj, bias, squeeze_out, branch, up_t, ffn_shrink, scale)
-
-    def tail(base, name):
+        scratch=[vm(ch, 128)],
+        aliases={0: 0, 1: 1},
+    )
+    pools = parts_over(pool, "row")
+    parts = len(pools)
+    weights = pools + (pool_proj, bias, squeeze_out, branch, up_t, ffn_shrink, scale)
+
+    def tail(kept):
         return call(
-            functools.partial(tail_kernel, area),
+            functools.partial(tail_kernel, area, kept, parts),
             [part, part, (half, wide, padded)],
-            base,
+            view,
             band,
             gating,
             *weights,
             scalars=1,
-            name=name,
         )
 
-    hid_send, one_send, expanded_send = tail(send_base, "tail_send")
+    hid_send, one_send, expanded_send = tail(False)
     hid_other = swap(hid_send, "view", 1)
-    hid_keep, one_keep, expanded_keep = tail(keep_base, "tail_keep")
+    hid_keep, one_keep, expanded_keep = tail(True)
     out_keep, out_send, dh_keep, dh_send, grad_own, grad_other = call(
         functools.partial(attend_kernel, width),
-        [part] * 4 + [(ch + 8, wide)] * 2,
+        [part, part, part, part, (ch + 16, wide), (ch + 16, wide)],
         hid_keep,
         hid_other,
         cot_keep,
-        cot_other,
-        pack,
-        pack_other,
+        query,
+        value,
+        cross_scale,
+        other,
         scratch=[vm(padded, padded), pltpu.VMEM((padded, padded), BF16), pltpu.VMEM((padded, padded), BF16)],
-        name="attend",
     )
     dh_back = swap(dh_send, "view", 1)
     out_back = swap(out_send, "view", 1)
-    grad_a = grad_own + swap(grad_other, "view", 1)
     dgate_keep, done_keep, acc = call(
-        functools.partial(tail_back_kernel, area, False),
+        functools.partial(tail_back_kernel, area, False, parts),
         [part, part, (wide, 8 * ch)],
-        keep_base,
+        view,
         dh_keep,
         one_keep,
         expanded_keep,
         gating,
         *weights,
         scalars=1,
-        name="tail_back_keep",
     )
     dgate_send, done_send, pool_grad, grad_b = call(
-        lambda base, dh, one, ex, gate, w0, w1, w2, w3, w4, w5, w6, w7, acc, dg, dn, pg, gr: tail_back_kernel(
-            area, True, base, dh, one, ex, gate, w0, w1, w2, w3, w4, w5, w6, w7, acc, None, None, dg, dn, pg, gr
-        ),
+        functools.partial(tail_back_kernel, area, True, parts),
         [part, part, (8, wide), (3 * ch, wide)],
-        send_base,
+        view,
         dh_back,
         one_send,
         expanded_send,
@@ -729,28 +826,21 @@
         *weights,
         acc,
         scalars=1,
-        name="tail_back_send",
-    )
-    pool_grad = sum_over(pool_grad, "row")
-    grad_a = sum_over(grad_a, "dp", "row")
-    grad_b = sum_over(grad_b, "dp", "view", "row")
+    )
+    pool_grads = parts_over(pool_grad, "row")
     (output,) = call(
-        assemble_kernel,
-        [(ch, rows, width)],
+        assemble_kernel, [(ch, rows, width)], view, out_keep, out_back, scalars=1, scratch=[vm(rows, ch, padded)]
+    )
+    shared_lines, owned_lines = 4 * ch + 16, ch + 16
+    piece = shared_lines // 2 + owned_lines
+    dn, dn_up, dn_down, mine, theirs = call(
+        functools.partial(conv_back_kernel, width, len(pool_grads)),
+        [full, row, row, (piece, wide), (piece, wide)],
         view,
-        out_keep,
-        out_back,
-        scalars=1,
-        scratch=[vm(rows, ch, padded)],
-        name="assemble",
-    )
-    dn, dn_up, dn_down, grad_c = call(
-        functools.partial(conv_back_kernel, width),
-        [full, row, row, (ch + 16, wide)],
-        view,
+        core,
+        *pool_grads,
         dgate_keep,
         dgate_send,
-        pool_grad,
         conv,
         doubled,
         edge,
@@ -758,14 +848,21 @@
         above,
         below,
         exp_t,
-        k_rows,
-        scalars=1,
-        scratch=[vm(wide, wide), vm(rows, ch, padded), vm(rows + 2, wide, padded), vm(wide, wide), vm(ch, wide)],
-        name="conv_back",
+        taps,
+        grad_own,
+        grad_other,
+        grad_b,
+        scalars=2,
+        scratch=[vm(shared_lines, wide), vm(rows, ch, padded), vm(rows + 2, wide, padded), vm(wide, wide), vm(ch, wide)],
     )
     from_above = lax.ppermute(dn_down, "row", up_pairs)
     from_below = lax.ppermute(dn_up, "row", down_pairs)
-    grad_c = sum_over(grad_c, "dp", "view", "row")
+    both = (shared_lines + owned_lines) // 2
+    mine, send = call(add_split_kernel, [(both, wide)] * 2, mine, swap(theirs, "dp", 1))
+    mine = add(mine, swap(send, "view", 1))
+    mine = sum_over(mine, "dp", 2)
+    mine = sum_over(mine, "row")
+    theirs = swap(mine, "dp", 1)
     (frames_grad,) = call(
         front_back_kernel,
         [(ch, rows, width)],
@@ -778,15 +875,16 @@
         done_send,
         scalars=1,
         scratch=[vm(rows, ch, padded)],
-        name="front_back",
-    )
-    g_up, g_down, g_squeeze, g_pool, g_bias, g_branch, g_scale, g_q, g_v, g_s, g_exp, g_k = call(
+    )
+    square, line = (ch, ch), (1, ch)
+    g_up, g_down, g_squeeze, g_pool, g_bias, g_branch, g_scale, g_exp, g_k, g_q, g_v, g_s = call(
         functools.partial(finish_kernel, factor),
-        [(ch, wide), (ch, ch), (ch, ch), (ch, ch), (1, ch), (1, ch), (1, ch), (ch, ch), (ch, ch), (1, ch), (ch, wide), (3, 3, wide)],
-        grad_a,
-        grad_b,
-        grad_c,
-        name="finish",
+        [(ch, wide), square, square, square, line, line, line, (ch, wide), (3, 3, wide), square, square, line],
+        core,
+        mine,
+        theirs,
+        scalars=1,
+        scratch=[vm(shared_lines, wide), vm(owned_lines, wide)],
     )
     return (
         output[None, None],
@@ -809,6 +907,7 @@
 def solution(mesh):
     image = P("view", "dp", None, "row", None)
     owned = (P("view", None, None), P("view", None, None), P("view", None))
+
     return jax.shard_map(
         per_device,
         mesh=mesh,

time: 104 us -> 86 us (0.83)
  starting transfers between devices: 39.9 us -> 29.9 us
  waiting for transfers between devices: 36.4 us -> 29.9 us
  local copies, waits for them, and re-layouts: 4.54 us -> 2.36 us
    ppermute x24 -> x16, waiting for transfers between devices: 34.1 us -> 24 us  [swap(): lax.ppermute(x, axis, [(i, i ^ mask) for i in range(lax.axis_size(axis))])]
    ppermute x24 -> x16, starting transfers between devices: 28.9 us -> 19.4 us  [swap(): lax.ppermute(x, axis, [(i, i ^ mask) for i in range(lax.axis_size(axis))])]
    ppermute x1, waiting for transfers between devices: 0.01 us -> 4.36 us  [per_device(): from_below = lax.ppermute(dn_up, 'row', down_pairs)]
    unnamed x28 -> x30, local copies, waits for them, and re-layouts: 4.54 us -> 2.36 us
    pallas_call x12 -> x17, Pallas kernels: 21.7 us -> 22.6 us  [call(): pl.pallas_call(kernel, out_shape=shapes, in_specs=[smem] * scalars + [hbm...]
  transfers between devices with their start and end apart: 28 -> 20, of which waited for: 15 -> 13; matrix products, arithmetic and copies ran while one was open for 0% -> 0% of each run, Pallas kernels for 12% -> 11%
where the time goes in v2:
time: 86 us; the launch traced here: 85.7 us
  starting transfers between devices  29.9 us (35%)
  waiting for transfers between devices  29.9 us (35%)
  Pallas kernels  22.6 us (26%)
  local copies, waits for them, and re-layouts  2.36 us (3%)
  between operations  0.9 us (1%)
    ppermute x16, waiting for transfers between devices, swap(): lax.ppermute(x, axis, [(i, i ^ mask) for i in range(lax.axis_size(axis))])  24 us
    pallas_call x17, Pallas kernels, call(): pl.pallas_call(kernel, out_shape=shapes, in_specs=[smem] * scalars + [hbm...  22.6 us
    ppermute x16, starting transfers between devices, swap(): lax.ppermute(x, axis, [(i, i ^ mask) for i in range(lax.axis_size(axis))])  19.4 us
    ppermute x1, starting transfers between devices, per_device(): above = lax.ppermute(last, 'row', up_pairs)  4.96 us
    ppermute x1, waiting for transfers between devices, per_device(): from_below = lax.ppermute(dn_up, 'row', down_pairs)  4.36 us
    ppermute x1, starting transfers between devices, per_device(): from_above = lax.ppermute(dn_down, 'row', up_pairs)  3.02 us
    unnamed x30, local copies, waits for them, and re-layouts  2.36 us
  transfers between devices with their start and end apart: 20, of which 13 were waited for; matrix products, arithmetic and copies ran while one was open for 0% of the time, Pallas kernels for 11%

profile of v2, /device:TPU:0, one launch (start us, length us, event | category | flops | bytes accessed | tf_op | source)
XLA Modules:
  0.0 85.7 jit_solution(13636674352622731576)
XLA Ops:
  0.7 2.3 %shard_map.245 = (f32[4,64,512]{2,1,0:T(8,128)}, f32[64,512]{1,0:T(8,128)}, f32[64,512]{1,0:T(8,128)}, f32[2,64,512]{2,1,0:T(8,128)}, f32[152,512]{1,0:T(8,128)}) custom-call(s32[1]{0:T(128)} %bitcast.view_ref, s32[1]{0:T(128)} %bitcast.1.core_ref, f32[64,4,480]{2,1,0:T(4,128)} %bitcast.47, f32[64,4,480]{2,1,0:T(4,128)} %bitcast.48, f32[64,64]{1,0:T(8,128)} %bitcast.29, ...), custom_call_target="tpu_custom_call" | custom-call | tf_op jit(solution)/shard_map/pallas_call | solution.py:664
  3.0 0.0 copy-start.13
  3.0 5.0 %collective-permute-start = (f32[64,512]{1,0:T(8,128)}, f32[64,512]{1,0:T(8,128)S(1)}, u32[]{:S(2)}, u32[]{:S(2)}) collective-permute-start(f32[64,512]{1,0:T(8,128)} %get-tuple-element.71), channel_id=1, source_target_pairs={{0,2},{2,4},{4,6},{1,3},{3,5},{5,7},{8,10},{10,12},{12,14},{9,11},... | collective-permute-start | bytes 393224 | tf_op jit(solution)/shard_map/ppermute | solution.py:752
  8.0 1.3 %collective-permute-start.1 = (f32[64,512]{1,0:T(8,128)}, f32[64,512]{1,0:T(8,128)S(1)}, u32[]{:S(2)}, u32[]{:S(2)}) collective-permute-start(f32[64,512]{1,0:T(8,128)} %get-tuple-element.72), channel_id=1, source_target_pairs={{2,0},{4,2},{6,4},{3,1},{5,3},{7,5},{10,8},{12,10},{14,12},{11,9},... | collective-permute-start | bytes 393224 | tf_op jit(solution)/shard_map/ppermute | solution.py:753
  9.3 1.6 %collective-permute-start.6 = (f32[152,512]{1,0:T(8,128)}, f32[152,512]{1,0:T(8,128)S(1)}, u32[]{:S(2)}, u32[]{:S(2)}) collective-permute-start(f32[152,512]{1,0:T(8,128)} %get-tuple-element.78), channel_id=1, source_target_pairs={{0,1},{1,0},{2,3},{3,2},{4,5},{5,4},{6,7},{7,6},{8,9},{9,8},{10,11... | collective-permute-start | bytes 933896 | tf_op jit(solution)/shard_map/ppermute | solution.py:676
  10.8 1.0 %copy-done = f32[4,64,512]{2,1,0:T(8,128)S(1)} copy-done((f32[4,64,512]{2,1,0:T(8,128)S(1)}, f32[4,64,512]{2,1,0:T(8,128)}, u32[]{:S(2)}) %copy-start) | copy-done | bytes 524312
  11.9 1.8 %shard_map.246 = (f32[4,128,512]{2,1,0:T(8,128)S(1)}, f32[4,128,512]{2,1,0:T(8,128)S(1)}, f32[4,64,512]{2,1,0:T(8,128)S(1)}, f32[64,512]{1,0:T(8,128)S(1)}, f32[128,128]{1,0:T(8,128)S(1)}) custom-call(f32[4,64,512]{2,1,0:T(8,128)S(1)} %copy-done, f32[64,128]{1,0:T(8,128)S(1)} %bitcast.26, f32[3,3,128]{2,1,0:T(4,128)S(1)} %bitcast.45), custom_call_target="tpu_custom_call" | custom-call | tf_op jit(solution)/shard_map/pallas_call | solution.py:664
  13.6 0.0 collective-permute-done.up_ref.refs_10_
  13.6 1.4 %collective-permute-done.1.down_ref.refs_11_ = f32[64,512]{1,0:T(8,128)S(1)} collective-permute-done((f32[64,512]{1,0:T(8,128)}, f32[64,512]{1,0:T(8,128)S(1)}, u32[]{:S(2)}, u32[]{:S(2)}) %collective-permute-start.1) | collective-permute-done | bytes 131104 | tf_op jit(solution)/shard_map/ppermute | solution.py:753
  15.1 0.0 copy-start.5
  15.1 1.5 %shard_map.247 = (f32[4,128,512]{2,1,0:T(8,128)S(1)}, f32[4,64,512]{2,1,0:T(8,128)S(1)}, f32[2,128,512]{2,1,0:T(8,128)S(1)}, f32[8,128]{1,0:T(8,128)S(1)}) custom-call(f32[4,128,512]{2,1,0:T(8,128)S(1)} %get-tuple-element.67.conv_in, f32[4,64,512]{2,1,0:T(8,128)S(1)} %get-tuple-element.68.gating_in, ...), custom_call_target="tpu_custom_call", output_to_operand_aliasing={{0}: (0, {}), {1}: (1, {})} | custom-call | tf_op jit(solution)/shard_map/pallas_call | solution.py:664
  16.5 3.4 %collective-permute-start.4 = (f32[8,128]{1,0:T(8,128)S(1)}, f32[8,128]{1,0:T(8,128)S(1)}, u32[]{:S(2)}, u32[]{:S(2)}) collective-permute-start(f32[8,128]{1,0:T(8,128)S(1)} %get-tuple-element.74.refs_0_), channel_id=1, source_target_pairs={{0,6},{2,4},{4,2},{6,0},{1,7},{3,5},{5,3},{7,1},{8,14},{10,12},{12... | collective-permute-start | bytes 12296 | tf_op jit(solution)/shard_map/ppermute | solution.py:676
  19.9 0.0 collective-permute-start.3
  19.9 1.1 %collective-permute-start.2 = (f32[8,128]{1,0:T(8,128)S(1)}, f32[8,128]{1,0:T(8,128)S(1)}, u32[]{:S(2)}, u32[]{:S(2)}) collective-permute-start(f32[8,128]{1,0:T(8,128)S(1)} %get-tuple-element.74.refs_0_), channel_id=1, source_target_pairs={{0,2},{2,0},{4,6},{6,4},{1,3},{3,1},{5,7},{7,5},{8,10},{10,8},{12,... | collective-permute-start | bytes 12296 | tf_op jit(solution)/shard_map/ppermute | solution.py:676
  21.0 1.0 %collective-permute-done.4.refs_3_ = f32[8,128]{1,0:T(8,128)S(1)} collective-permute-done((f32[8,128]{1,0:T(8,128)S(1)}, f32[8,128]{1,0:T(8,128)S(1)}, u32[]{:S(2)}, u32[]{:S(2)}) %collective-permute-start.4) | collective-permute-done | bytes 4128 | tf_op jit(solution)/shard_map/ppermute | solution.py:676
  22.0 2.4 %collective-permute-done.3.refs_2_ = f32[8,128]{1,0:T(8,128)S(1)} collective-permute-done((f32[8,128]{1,0:T(8,128)S(1)}, f32[8,128]{1,0:T(8,128)S(1)}, u32[]{:S(2)}, u32[]{:S(2)}) %collective-permute-start.3) | collective-permute-done | bytes 4128 | tf_op jit(solution)/shard_map/ppermute | solution.py:676
  24.4 0.0 collective-permute-done.2.refs_1_
  24.4 0.0 copy-done.1
  24.4 0.0 copy-done.2
  24.5 0.0 copy-done.3
  24.5 0.0 copy-done.4
  24.5 0.6 copy-done.10
  25.1 0.0 copy-done.11
  25.1 0.0 copy-done.12
  25.1 1.2 %shard_map.249 = (f32[2,64,512]{2,1,0:T(8,128)S(1)}, f32[2,64,512]{2,1,0:T(8,128)S(1)}, f32[2,128,512]{2,1,0:T(8,128)S(1)}) custom-call(s32[1]{0:T(128)} %bitcast.view_ref, f32[4,64,512]{2,1,0:T(8,128)S(1)} %copy-done.1, f32[4,64,512]{2,1,0:T(8,128)S(1)} %get-tuple-element.73.gating_ref, f32[8,128]{1,0:T(8,128)S(1)} %get-tuple-element.74.refs_0_, ...), custom_call_target="tpu_custom_call" | custom-call | tf_op jit(solution)/shard_map/pallas_call | solution.py:664
  26.3 0.0 copy-start.9
  26.3 0.6 collective-permute-start.5
  26.9 1.2 %shard_map.248 = (f32[2,64,512]{2,1,0:T(8,128)S(1)}, f32[2,64,512]{2,1,0:T(8,128)S(1)}, f32[2,128,512]{2,1,0:T(8,128)S(1)}) custom-call(s32[1]{0:T(128)} %bitcast.view_ref, f32[4,64,512]{2,1,0:T(8,128)S(1)} %copy-done.1, f32[4,64,512]{2,1,0:T(8,128)S(1)} %get-tuple-element.73.gating_ref, f32[8,128]{1,0:T(8,128)S(1)} %get-tuple-element.74.refs_0_, ...), custom_call_target="tpu_custom_call" | custom-call | tf_op jit(solution)/shard_map/pallas_call | solution.py:664
  28.1 0.0 collective-permute-done.6.other_ref
  28.1 4.7 %collective-permute-done.5.hid1_ref = f32[2,64,512]{2,1,0:T(8,128)S(1)} collective-permute-done((f32[2,64,512]{2,1,0:T(8,128)S(1)}, f32[2,64,512]{2,1,0:T(8,128)S(1)}, u32[]{:S(2)}, u32[]{:S(2)}) %collective-permute-start.5) | collective-permute-done | bytes 262176 | tf_op jit(solution)/shard_map/ppermute | solution.py:676
  32.8 0.6 copy-done.14
  33.4 4.7 %shard_map.250 = (f32[2,64,512]{2,1,0:T(8,128)S(1)}, f32[2,64,512]{2,1,0:T(8,128)S(1)}, f32[2,64,512]{2,1,0:T(8,128)S(1)}, f32[2,64,512]{2,1,0:T(8,128)S(1)}, f3...) custom-call(f32[2,64,512]{2,1,0:T(8,128)S(1)} %get-tuple-element.75.hid0_ref, ...), custom_call_target="tpu_custom_call" | custom-call | tf_op jit(solution)/shard_map/pallas_call | solution.py:664
  38.1 0.6 collective-permute-start.8
  38.7 1.3 %shard_map.252 = (f32[2,64,512]{2,1,0:T(8,128)S(1)}, f32[2,64,512]{2,1,0:T(8,128)S(1)}, f32[128,512]{1,0:T(8,128)S(1)}) custom-call(s32[1]{0:T(128)} %bitcast.view_ref, f32[2,64,512]{2,1,0:T(8,128)S(1)} %get-tuple-element.84.dh_ref, f32[2,64,512]{2,1,0:T(8,128)S(1)} %get-tuple-element.85.one_ref, f32[2,128,512]{2,1,0:T(8,128)S(1)} %get-tuple-element.86.expanded_ref, ...), custom_call_target="tpu_custom_call" | custom-call | tf_op jit(solution)/shard_map/pallas_call | solution.py:664
  40.0 4.5 %collective-permute-done.8.dh_ref = f32[2,64,512]{2,1,0:T(8,128)S(1)} collective-permute-done((f32[2,64,512]{2,1,0:T(8,128)S(1)}, f32[2,64,512]{2,1,0:T(8,128)S(1)}, u32[]{:S(2)}, u32[]{:S(2)}) %collective-permute-start.8) | collective-permute-done | bytes 262176 | tf_op jit(solution)/shard_map/ppermute | solution.py:676
  44.5 1.6 %shard_map.253 = (f32[2,64,512]{2,1,0:T(8,128)S(1)}, f32[2,64,512]{2,1,0:T(8,128)S(1)}, f32[8,128]{1,0:T(8,128)S(1)}, f32[192,128]{1,0:T(8,128)S(1)}) custom-call(s32[1]{0:T(128)} %bitcast.view_ref, f32[2,64,512]{2,1,0:T(8,128)S(1)} %collective-permute-done.8.dh_ref, f32[2,64,512]{2,1,0:T(8,128)S(1)} %get-tuple-element.82.one_ref, ...), custom_call_target="tpu_custom_call" | custom-call | tf_op jit(solution)/shard_map/pallas_call | solution.py:664
  46.1 1.5 %collective-permute-start.11 = (f32[8,128]{1,0:T(8,128)S(1)}, f32[8,128]{1,0:T(8,128)S(1)}, u32[]{:S(2)}, u32[]{:S(2)}) collective-permute-start(f32[8,128]{1,0:T(8,128)S(1)} %get-tuple-element.88.refs_0_), channel_id=1, source_target_pairs={{0,6},{2,4},{4,2},{6,0},{1,7},{3,5},{5,3},{7,1},{8,14},{10,12},{12... | collective-permute-start | bytes 12296 | tf_op jit(solution)/shard_map/ppermute | solution.py:676
  47.6 0.6 collective-permute-start.10
  48.2 2.3 %collective-permute-start.9 = (f32[8,128]{1,0:T(8,128)S(1)}, f32[8,128]{1,0:T(8,128)S(1)}, u32[]{:S(2)}, u32[]{:S(2)}) collective-permute-start(f32[8,128]{1,0:T(8,128)S(1)} %get-tuple-element.88.refs_0_), channel_id=1, source_target_pairs={{0,2},{2,0},{4,6},{6,4},{1,3},{3,1},{5,7},{7,5},{8,10},{10,8},{12,... | collective-permute-start | bytes 12296 | tf_op jit(solution)/shard_map/ppermute | solution.py:676
  50.5 1.0 %collective-permute-done.11.refs_3_ = f32[8,128]{1,0:T(8,128)S(1)} collective-permute-done((f32[8,128]{1,0:T(8,128)S(1)}, f32[8,128]{1,0:T(8,128)S(1)}, u32[]{:S(2)}, u32[]{:S(2)}) %collective-permute-start.11) | collective-permute-done | bytes 4128 | tf_op jit(solution)/shard_map/ppermute | solution.py:676
  51.6 0.6 collective-permute-done.10.refs_2_
  52.1 0.0 collective-permute-done.9.refs_1_
  52.2 4.1 %shard_map.254 = (f32[4,64,512]{2,1,0:T(8,128)S(1)}, f32[64,512]{1,0:T(8,128)S(1)}, f32[64,512]{1,0:T(8,128)S(1)}, f32[216,128]{1,0:T(8,128)S(1)}, f32[216,128]{1,0:T(8,128)S(1)}) custom-call(s32[1]{0:T(128)} %bitcast.view_ref, s32[1]{0:T(128)} %bitcast.1.core_ref, f32[8,128]{1,0:T(8,128)S(1)} %get-tuple-element.88.refs_0_, ...), custom_call_target="tpu_custom_call" | custom-call | tf_op jit(solution)/shard_map/pallas_call | solution.py:664
  56.3 0.1 collective-permute-start.14
  56.4 1.3 %collective-permute-done.14.other_ref = f32[216,128]{1,0:T(8,128)S(1)} collective-permute-done((f32[216,128]{1,0:T(8,128)S(1)}, f32[216,128]{1,0:T(8,128)S(1)}, u32[]{:S(2)}, u32[]{:S(2)}) %collective-permute-start.14) | collective-permute-done | bytes 110624 | tf_op jit(solution)/shard_map/ppermute | solution.py:676
  57.7 1.3 %collective-permute-start.15 = (f32[176,128]{1,0:T(8,128)S(1)}, f32[176,128]{1,0:T(8,128)S(1)}, u32[]{:S(2)}, u32[]{:S(2)}) collective-permute-start(f32[176,128]{1,0:T(8,128)S(1)} %get-tuple-element.105), channel_id=1, source_target_pairs={{0,1},{1,0},{2,3},{3,2},{4,5},{5,4},{6,7},{7,6},{8,9},{9,8},{10,11... | collective-permute-start | bytes 270344 | tf_op jit(solution)/shard_map/ppermute | solution.py:676
  59.1 3.4 %collective-permute-done.15.other_ref = f32[176,128]{1,0:T(8,128)S(1)} collective-permute-done((f32[176,128]{1,0:T(8,128)S(1)}, f32[176,128]{1,0:T(8,128)S(1)}, u32[]{:S(2)}, u32[]{:S(2)}) %collective-permute-start.15) | collective-permute-done | bytes 90144 | tf_op jit(solution)/shard_map/ppermute | solution.py:676
  62.5 1.6 %collective-permute-start.16 = (f32[176,128]{1,0:T(8,128)S(1)}, f32[176,128]{1,0:T(8,128)S(1)}, u32[]{:S(2)}, u32[]{:S(2)}) collective-permute-start(f32[176,128]{1,0:T(8,128)S(1)} %shard_map.257.mine_ref), channel_id=1, source_target_pairs={{0,16},{8,24},{16,0},{24,8},{1,17},{9,25},{17,1},{25,9},{2,18},{10... | collective-permute-start | bytes 270344 | tf_op jit(solution)/shard_map/ppermute | solution.py:676
  64.1 3.0 %collective-permute-done.16.other_ref = f32[176,128]{1,0:T(8,128)S(1)} collective-permute-done((f32[176,128]{1,0:T(8,128)S(1)}, f32[176,128]{1,0:T(8,128)S(1)}, u32[]{:S(2)}, u32[]{:S(2)}) %collective-permute-start.16) | collective-permute-done | bytes 90144 | tf_op jit(solution)/shard_map/ppermute | solution.py:676
  67.1 2.1 %collective-permute-start.17 = (f32[176,128]{1,0:T(8,128)S(1)}, f32[176,128]{1,0:T(8,128)S(1)}, u32[]{:S(2)}, u32[]{:S(2)}) collective-permute-start(f32[176,128]{1,0:T(8,128)S(1)} %shard_map.258.mine_ref), channel_id=1, source_target_pairs={{0,2},{2,0},{4,6},{6,4},{1,3},{3,1},{5,7},{7,5},{8,10},{10,8},{12,... | collective-permute-start | bytes 270344 | tf_op jit(solution)/shard_map/ppermute | solution.py:676
  69.1 0.5 collective-permute-start.7
  69.7 2.0 %collective-permute-done.17.other_ref = f32[176,128]{1,0:T(8,128)S(1)} collective-permute-done((f32[176,128]{1,0:T(8,128)S(1)}, f32[176,128]{1,0:T(8,128)S(1)}, u32[]{:S(2)}, u32[]{:S(2)}) %collective-permute-start.17) | collective-permute-done | bytes 90144 | tf_op jit(solution)/shard_map/ppermute | solution.py:676
  71.7 2.0 %collective-permute-start.18 = (f32[176,128]{1,0:T(8,128)S(1)}, f32[176,128]{1,0:T(8,128)S(1)}, u32[]{:S(2)}, u32[]{:S(2)}) collective-permute-start(f32[176,128]{1,0:T(8,128)S(1)} %shard_map.259.mine_ref), channel_id=1, source_target_pairs={{0,4},{2,6},{4,0},{6,2},{1,5},{3,7},{5,1},{7,3},{8,12},{10,14},{12... | collective-permute-start | bytes 270344 | tf_op jit(solution)/shard_map/ppermute | solution.py:676
  73.7 3.0 %collective-permute-start.12 = (f32[64,512]{1,0:T(8,128)S(1)}, f32[64,512]{1,0:T(8,128)S(1)}, u32[]{:S(2)}, u32[]{:S(2)}) collective-permute-start(f32[64,512]{1,0:T(8,128)S(1)} %get-tuple-element.98), channel_id=1, source_target_pairs={{0,2},{2,4},{4,6},{1,3},{3,5},{5,7},{8,10},{10,12},{12,14},{9,11},... | collective-permute-start | bytes 393224 | tf_op jit(solution)/shard_map/ppermute | solution.py:858
  76.8 1.3 %collective-permute-start.13 = (f32[64,512]{1,0:T(8,128)S(1)}, f32[64,512]{1,0:T(8,128)S(1)}, u32[]{:S(2)}, u32[]{:S(2)}) collective-permute-start(f32[64,512]{1,0:T(8,128)S(1)} %get-tuple-element.99), channel_id=1, source_target_pairs={{2,0},{4,2},{6,4},{3,1},{5,3},{7,5},{10,8},{12,10},{14,12},{11,9},... | collective-permute-start | bytes 393224 | tf_op jit(solution)/shard_map/ppermute | solution.py:859
  78.1 0.0 collective-permute-done.18.other_ref
  78.1 0.1 collective-permute-start.19
  78.2 0.0 collective-permute-done.7.send_ref
  78.2 0.9 %shard_map.251 = f32[64,4,480]{2,1,0:T(4,128)} custom-call(s32[1]{0:T(128)} %bitcast.view_ref, f32[2,64,512]{2,1,0:T(8,128)S(1)} %get-tuple-element.79.keep_ref, f32[2,64,512]{2,1,0:T(8,128)S(1)} %collective-permute-done.7.send_ref), custom_call_target="tpu_custom_call" | custom-call | tf_op jit(solution)/shard_map/pallas_call | solution.py:664
  79.1 0.2 collective-permute-done.12.above_ref
  79.3 4.4 %collective-permute-done.13.below_ref = f32[64,512]{1,0:T(8,128)S(1)} collective-permute-done((f32[64,512]{1,0:T(8,128)S(1)}, f32[64,512]{1,0:T(8,128)S(1)}, u32[]{:S(2)}, u32[]{:S(2)}) %collective-permute-start.13) | collective-permute-done | bytes 131104 | tf_op jit(solution)/shard_map/ppermute | solution.py:859
  83.6 1.3 %shard_map.255 = f32[64,4,480]{2,1,0:T(4,128)} custom-call(s32[1]{0:T(128)} %bitcast.view_ref, f32[4,64,512]{2,1,0:T(8,128)S(1)} %get-tuple-element.97.dn_ref, f32[64,512]{1,0:T(8,128)S(1)} %collective-permute-done.12.above_ref, f32[64,512]{1,0:T(8,128)S(1)} %collective-permute-done.13.below_ref, f32[4,64,512]{2,1,0:T(8,128)S(1)} %copy-done.1, ...), custom_call_target="tpu_custom_call" | custom-call | tf_op jit(solution)/shard_map/pallas_call | solution.py:664
  84.9 0.0 collective-permute-done.19.theirs_ref
  84.9 0.7 shard_map.261
  (23 shorter events, 0.1 us)
Async XLA Ops:
  0.7 10.2 %copy-start.6 = (f32[128,64]{0,1:T(8,128)S(1)}, f32[128,64]{0,1:T(8,128)}, u32[]{:S(2)}) copy-start(f32[128,64]{0,1:T(8,128)} %param.16) | copy-start | bytes 98308
  3.0 7.8 %copy-start.13 = (f32[128,3,3]{0,2,1:T(4,128)S(1)}, f32[128,3,3]{0,2,1:T(4,128)}, u32[]{:S(2)}) copy-start(f32[128,3,3]{0,2,1:T(4,128)} %param.17) | copy-start | bytes 13828
  3.0 10.6 %collective-permute-start = (f32[64,512]{1,0:T(8,128)}, f32[64,512]{1,0:T(8,128)S(1)}, u32[]{:S(2)}, u32[]{:S(2)}) collective-permute-start(f32[64,512]{1,0:T(8,128)} %get-tuple-element.71), channel_id=1, source_target_pairs={{0,2},{2,4},{4,6},{1,3},{3,5},{5,7},{8,10},{10,12},{12,14},{9,11},... | collective-permute-start | bytes 393224 | tf_op jit(solution)/shard_map/ppermute | solution.py:752
  8.0 7.1 %collective-permute-start.1 = (f32[64,512]{1,0:T(8,128)}, f32[64,512]{1,0:T(8,128)S(1)}, u32[]{:S(2)}, u32[]{:S(2)}) collective-permute-start(f32[64,512]{1,0:T(8,128)} %get-tuple-element.72), channel_id=1, source_target_pairs={{2,0},{4,2},{6,4},{3,1},{5,3},{7,5},{10,8},{12,10},{14,12},{11,9},... | collective-permute-start | bytes 393224 | tf_op jit(solution)/shard_map/ppermute | solution.py:753
  9.3 18.8 %collective-permute-start.6 = (f32[152,512]{1,0:T(8,128)}, f32[152,512]{1,0:T(8,128)S(1)}, u32[]{:S(2)}, u32[]{:S(2)}) collective-permute-start(f32[152,512]{1,0:T(8,128)} %get-tuple-element.78), channel_id=1, source_target_pairs={{0,1},{1,0},{2,3},{3,2},{4,5},{5,4},{6,7},{7,6},{8,9},{9,8},{10,11... | collective-permute-start | bytes 933896 | tf_op jit(solution)/shard_map/ppermute | solution.py:676
  10.8 1.0 %copy-start = (f32[4,64,512]{2,1,0:T(8,128)S(1)}, f32[4,64,512]{2,1,0:T(8,128)}, u32[]{:S(2)}) copy-start(f32[4,64,512]{2,1,0:T(8,128)} %get-tuple-element.66.band_ref.refs_9_) | copy-start | bytes 1572868
  15.0 9.4 %copy-start.1 = (f32[4,64,512]{2,1,0:T(8,128)S(1)}, f32[4,64,512]{2,1,0:T(8,128)}, u32[]{:S(2)}) copy-start(f32[4,64,512]{2,1,0:T(8,128)} %get-tuple-element.66.band_ref.refs_9_) | copy-start | bytes 1572868
  15.0 9.4 %copy-start.2 = (f32[64,64]{1,0:T(8,128)S(1)}, f32[64,64]{1,0:T(8,128)}, u32[]{:S(2)}) copy-start(f32[64,64]{1,0:T(8,128)} %refs_4_.7) | copy-start | bytes 49156
  15.0 9.4 %copy-start.3 = (f32[64,64]{1,0:T(8,128)S(1)}, f32[64,64]{1,0:T(8,128)}, u32[]{:S(2)}) copy-start(f32[64,64]{1,0:T(8,128)} %refs_6_.7) | copy-start | bytes 49156
  15.0 9.4 %copy-start.4 = (f32[128,64]{0,1:T(8,128)S(1)}, f32[128,64]{0,1:T(8,128)}, u32[]{:S(2)}) copy-start(f32[128,64]{0,1:T(8,128)} %param.22) | copy-start | bytes 98308
  15.1 9.4 %copy-start.5 = (f32[64,64]{1,0:T(8,128)S(1)}, f32[64,64]{1,0:T(8,128)}, u32[]{:S(2)}) copy-start(f32[64,64]{1,0:T(8,128)} %refs_9_.7) | copy-start | bytes 49156
  16.5 5.5 %collective-permute-start.4 = (f32[8,128]{1,0:T(8,128)S(1)}, f32[8,128]{1,0:T(8,128)S(1)}, u32[]{:S(2)}, u32[]{:S(2)}) collective-permute-start(f32[8,128]{1,0:T(8,128)S(1)} %get-tuple-element.74.refs_0_), channel_id=1, source_target_pairs={{0,6},{2,4},{4,2},{6,0},{1,7},{3,5},{5,3},{7,1},{8,14},{10,12},{12... | collective-permute-start | bytes 12296 | tf_op jit(solution)/shard_map/ppermute | solution.py:676
  19.9 4.5 %collective-permute-start.3 = (f32[8,128]{1,0:T(8,128)S(1)}, f32[8,128]{1,0:T(8,128)S(1)}, u32[]{:S(2)}, u32[]{:S(2)}) collective-permute-start(f32[8,128]{1,0:T(8,128)S(1)} %get-tuple-element.74.refs_0_), channel_id=1, source_target_pairs={{0,4},{2,6},{4,0},{6,2},{1,5},{3,7},{5,1},{7,3},{8,12},{10,14},{12... | collective-permute-start | bytes 12296 | tf_op jit(solution)/shard_map/ppermute | solution.py:676
  19.9 4.5 %collective-permute-start.2 = (f32[8,128]{1,0:T(8,128)S(1)}, f32[8,128]{1,0:T(8,128)S(1)}, u32[]{:S(2)}, u32[]{:S(2)}) collective-permute-start(f32[8,128]{1,0:T(8,128)S(1)} %get-tuple-element.74.refs_0_), channel_id=1, source_target_pairs={{0,2},{2,0},{4,6},{6,4},{1,3},{3,1},{5,7},{7,5},{8,10},{10,8},{12,... | collective-permute-start | bytes 12296 | tf_op jit(solution)/shard_map/ppermute | solution.py:676
  24.4 0.7 copy-start.10
  24.4 0.7 copy-start.11
  24.4 0.7 copy-start.12
  26.3 6.5 %copy-start.7 = (f32[2,64,512]{2,1,0:T(8,128)S(1)}, f32[2,64,512]{2,1,0:T(8,128)}, u32[]{:S(2)}) copy-start(f32[2,64,512]{2,1,0:T(8,128)} %get-tuple-element.77.cot0_ref) | copy-start | bytes 786436
  26.3 6.5 %copy-start.8 = (f32[1,64,64]{2,1,0:T(8,128)S(1)}, f32[1,64,64]{2,1,0:T(8,128)}, u32[]{:S(2)}) copy-start(f32[1,64,64]{2,1,0:T(8,128)} %param.25) | copy-start | bytes 49156
  26.3 6.5 %copy-start.9 = (f32[1,64,64]{2,1,0:T(8,128)S(1)}, f32[1,64,64]{2,1,0:T(8,128)}, u32[]{:S(2)}) copy-start(f32[1,64,64]{2,1,0:T(8,128)} %param.26) | copy-start | bytes 49156
  26.3 6.4 %collective-permute-start.5 = (f32[2,64,512]{2,1,0:T(8,128)S(1)}, f32[2,64,512]{2,1,0:T(8,128)S(1)}, u32[]{:S(2)}, u32[]{:S(2)}) collective-permute-start(f32[2,64,512]{2,1,0:T(8,128)S(1)} %get-tuple-element.76), channel_id=1, source_target_pairs={{0,1},{1,0},{2,3},{3,2},{4,5},{5,4},{6,7},{7,6},{8,9},{9,8},{10,11... | collective-permute-start | bytes 786440 | tf_op jit(solution)/shard_map/ppermute | solution.py:676
  32.7 0.7 copy-start.14
  38.1 6.4 %collective-permute-start.8 = (f32[2,64,512]{2,1,0:T(8,128)S(1)}, f32[2,64,512]{2,1,0:T(8,128)S(1)}, u32[]{:S(2)}, u32[]{:S(2)}) collective-permute-start(f32[2,64,512]{2,1,0:T(8,128)S(1)} %get-tuple-element.81), channel_id=1, source_target_pairs={{0,1},{1,0},{2,3},{3,2},{4,5},{5,4},{6,7},{7,6},{8,9},{9,8},{10,11... | collective-permute-start | bytes 786440 | tf_op jit(solution)/shard_map/ppermute | solution.py:676
  46.1 5.4 %collective-permute-start.11 = (f32[8,128]{1,0:T(8,128)S(1)}, f32[8,128]{1,0:T(8,128)S(1)}, u32[]{:S(2)}, u32[]{:S(2)}) collective-permute-start(f32[8,128]{1,0:T(8,128)S(1)} %get-tuple-element.88.refs_0_), channel_id=1, source_target_pairs={{0,6},{2,4},{4,2},{6,0},{1,7},{3,5},{5,3},{7,1},{8,14},{10,12},{12... | collective-permute-start | bytes 12296 | tf_op jit(solution)/shard_map/ppermute | solution.py:676
  47.6 4.5 %collective-permute-start.10 = (f32[8,128]{1,0:T(8,128)S(1)}, f32[8,128]{1,0:T(8,128)S(1)}, u32[]{:S(2)}, u32[]{:S(2)}) collective-permute-start(f32[8,128]{1,0:T(8,128)S(1)} %get-tuple-element.88.refs_0_), channel_id=1, source_target_pairs={{0,4},{2,6},{4,0},{6,2},{1,5},{3,7},{5,1},{7,3},{8,12},{10,14},{12... | collective-permute-start | bytes 12296 | tf_op jit(solution)/shard_map/ppermute | solution.py:676
  48.2 3.9 %collective-permute-start.9 = (f32[8,128]{1,0:T(8,128)S(1)}, f32[8,128]{1,0:T(8,128)S(1)}, u32[]{:S(2)}, u32[]{:S(2)}) collective-permute-start(f32[8,128]{1,0:T(8,128)S(1)} %get-tuple-element.88.refs_0_), channel_id=1, source_target_pairs={{0,2},{2,0},{4,6},{6,4},{1,3},{3,1},{5,7},{7,5},{8,10},{10,8},{12,... | collective-permute-start | bytes 12296 | tf_op jit(solution)/shard_map/ppermute | solution.py:676
  56.3 1.4 %collective-permute-start.14 = (f32[216,128]{1,0:T(8,128)S(1)}, f32[216,128]{1,0:T(8,128)S(1)}, u32[]{:S(2)}, u32[]{:S(2)}) collective-permute-start(f32[216,128]{1,0:T(8,128)S(1)} %get-tuple-element.103), channel_id=1, source_target_pairs={{0,8},{8,0},{16,24},{24,16},{1,9},{9,1},{17,25},{25,17},{2,10},{10... | collective-permute-start | bytes 331784 | tf_op jit(solution)/shard_map/ppermute | solution.py:676
  57.7 4.7 %collective-permute-start.15 = (f32[176,128]{1,0:T(8,128)S(1)}, f32[176,128]{1,0:T(8,128)S(1)}, u32[]{:S(2)}, u32[]{:S(2)}) collective-permute-start(f32[176,128]{1,0:T(8,128)S(1)} %get-tuple-element.105), channel_id=1, source_target_pairs={{0,1},{1,0},{2,3},{3,2},{4,5},{5,4},{6,7},{7,6},{8,9},{9,8},{10,11... | collective-permute-start | bytes 270344 | tf_op jit(solution)/shard_map/ppermute | solution.py:676
  62.5 4.6 %collective-permute-start.16 = (f32[176,128]{1,0:T(8,128)S(1)}, f32[176,128]{1,0:T(8,128)S(1)}, u32[]{:S(2)}, u32[]{:S(2)}) collective-permute-start(f32[176,128]{1,0:T(8,128)S(1)} %shard_map.257.mine_ref), channel_id=1, source_target_pairs={{0,16},{8,24},{16,0},{24,8},{1,17},{9,25},{17,1},{25,9},{2,18},{10... | collective-permute-start | bytes 270344 | tf_op jit(solution)/shard_map/ppermute | solution.py:676
  67.1 4.6 %collective-permute-start.17 = (f32[176,128]{1,0:T(8,128)S(1)}, f32[176,128]{1,0:T(8,128)S(1)}, u32[]{:S(2)}, u32[]{:S(2)}) collective-permute-start(f32[176,128]{1,0:T(8,128)S(1)} %shard_map.258.mine_ref), channel_id=1, source_target_pairs={{0,2},{2,0},{4,6},{6,4},{1,3},{3,1},{5,7},{7,5},{8,10},{10,8},{12,... | collective-permute-start | bytes 270344 | tf_op jit(solution)/shard_map/ppermute | solution.py:676
  69.1 9.0 %collective-permute-start.7 = (f32[2,64,512]{2,1,0:T(8,128)S(1)}, f32[2,64,512]{2,1,0:T(8,128)S(1)}, u32[]{:S(2)}, u32[]{:S(2)}) collective-permute-start(f32[2,64,512]{2,1,0:T(8,128)S(1)} %get-tuple-element.80), channel_id=1, source_target_pairs={{0,1},{1,0},{2,3},{3,2},{4,5},{5,4},{6,7},{7,6},{8,9},{9,8},{10,11... | collective-permute-start | bytes 786440 | tf_op jit(solution)/shard_map/ppermute | solution.py:676
  71.7 6.4 %collective-permute-start.18 = (f32[176,128]{1,0:T(8,128)S(1)}, f32[176,128]{1,0:T(8,128)S(1)}, u32[]{:S(2)}, u32[]{:S(2)}) collective-permute-start(f32[176,128]{1,0:T(8,128)S(1)} %shard_map.259.mine_ref), channel_id=1, source_target_pairs={{0,4},{2,6},{4,0},{6,2},{1,5},{3,7},{5,1},{7,3},{8,12},{10,14},{12... | collective-permute-start | bytes 270344 | tf_op jit(solution)/shard_map/ppermute | solution.py:676
  73.7 5.5 %collective-permute-start.12 = (f32[64,512]{1,0:T(8,128)S(1)}, f32[64,512]{1,0:T(8,128)S(1)}, u32[]{:S(2)}, u32[]{:S(2)}) collective-permute-start(f32[64,512]{1,0:T(8,128)S(1)} %get-tuple-element.98), channel_id=1, source_target_pairs={{0,2},{2,4},{4,6},{1,3},{3,5},{5,7},{8,10},{10,12},{12,14},{9,11},... | collective-permute-start | bytes 393224 | tf_op jit(solution)/shard_map/ppermute | solution.py:858
  76.8 6.9 %collective-permute-start.13 = (f32[64,512]{1,0:T(8,128)S(1)}, f32[64,512]{1,0:T(8,128)S(1)}, u32[]{:S(2)}, u32[]{:S(2)}) collective-permute-start(f32[64,512]{1,0:T(8,128)S(1)} %get-tuple-element.99), channel_id=1, source_target_pairs={{2,0},{4,2},{6,4},{3,1},{5,3},{7,5},{10,8},{12,10},{14,12},{11,9},... | collective-permute-start | bytes 393224 | tf_op jit(solution)/shard_map/ppermute | solution.py:859
  78.1 6.8 %collective-permute-start.19 = (f32[176,128]{1,0:T(8,128)S(1)}, f32[176,128]{1,0:T(8,128)S(1)}, u32[]{:S(2)}, u32[]{:S(2)}) collective-permute-start(f32[176,128]{1,0:T(8,128)S(1)} %shard_map.260.mine_ref), channel_id=1, source_target_pairs={{0,8},{8,0},{16,24},{24,16},{1,9},{9,1},{17,25},{25,17},{2,10},{10... | collective-permute-start | bytes 270344 | tf_op jit(solution)/shard_map/ppermute | solution.py:676

commit v3 on v2

--- a/solution.py
+++ b/solution.py
@@ -12,7 +12,6 @@
 F32 = jnp.float32
 BF16 = jnp.bfloat16
 MIB = 1 << 20
-UNROLL = 2
 
 
 def split(x):
@@ -119,43 +118,28 @@
     return wide[:, :ch], wide[:, ch:], x_ref[base + lines : base + lines + 1, 0:ch]
 
 
-def start_kernel(
-    view_ref,
-    core_ref,
-    x_hbm,
-    cot_hbm,
-    q_hbm,
-    v_hbm,
-    s_hbm,
-    band_ref,
-    first_ref,
-    last_ref,
-    keep_ref,
-    send_ref,
-    x_ref,
-    cot_ref,
-    q_ref,
-    v_ref,
-    s_ref,
-    scratch_ref,
-    sems,
-):
-    pairs = ((x_hbm, x_ref), (cot_hbm, cot_ref), (q_hbm, q_ref), (v_hbm, v_ref), (s_hbm, s_ref))
-    copies = [pltpu.make_async_copy(src, dst, sems.at[i]) for i, (src, dst) in enumerate(pairs)]
+def start_kernel(view_ref, core_ref, odd_ref, slot_ref, x_ref, band_ref, first_ref, second_ref):
+    relayout(x_ref, band_ref)
+    end = band_ref.shape[0] - 1
+    first_ref[...] = band_ref[end * (1 - odd_ref[0])]
+    second_ref[...] = band_ref[end * odd_ref[0]]
+
+
+def pack_kernel(count, view_ref, *refs):
+    fars, (cot_ref, keep_ref, send_ref), refs = refs[:count], refs[count : count + 3], refs[count + 3 :]
+    nears, (scratch_ref, sems) = refs[:count], refs[count:]
+    copies = [pltpu.make_async_copy(src, dst, sems.at[i]) for i, (src, dst) in enumerate(zip(fars, nears))]
     for copy in copies:
         copy.start()
     half, ch, _ = keep_ref.shape
     view = view_ref[0]
-    copies[0].wait()
-    relayout(x_ref, band_ref)
-    first_ref[...] = band_ref[0]
-    last_ref[...] = band_ref[2 * half - 1]
-    for copy in copies[1:]:
-        copy.wait()
     relayout(cot_ref, scratch_ref)
     for k in range(half):
         keep_ref[k] = scratch_ref[half * view + k]
         send_ref[k * ch : (k + 1) * ch, :] = scratch_ref[half * (1 - view) + k]
+    for copy in copies:
+        copy.wait()
+    q_ref, v_ref, s_ref = nears[:3]
     pack_square(send_ref, half * ch, q_ref[...], v_ref[...], s_ref[...])
 
 
@@ -211,17 +195,34 @@
         pool_ref[at, :] = pooled
         return carry
 
-    lax.fori_loop(0, ch // 8, group, 0, unroll=UNROLL)
+    lax.fori_loop(0, ch // 8, group, 0, unroll=True)
 
 
 def conv_edge_kernel(
-    width, conv_in, gating_in, pool_in, taps_ref, up_ref, down_ref, exp_ref, conv_ref, gating_ref, edge_ref, pool_ref, sums_ref
+    width,
+    odd_ref,
+    conv_in,
+    gating_in,
+    pool_in,
+    taps_ref,
+    first_ref,
+    second_ref,
+    exp_ref,
+    conv_ref,
+    gating_ref,
+    edge_ref,
+    halo_ref,
+    pool_ref,
+    sums_ref,
 ):
     rows, wide, padded = conv_ref.shape
     ch = wide // 2
     weight = left_rows(exp_ref[...])
-    edge_ref[0] = dot_tn(weight, right_rows(normed_of(up_ref[...])[0]))
-    edge_ref[1] = dot_tn(weight, right_rows(normed_of(down_ref[...])[0]))
+    odd = odd_ref[0]
+    for side, choice in enumerate((odd == 1, odd == 0)):
+        normed = normed_of(jnp.where(choice, first_ref[...], second_ref[...]))[0]
+        halo_ref[side] = normed
+        edge_ref[side] = dot_tn(weight, right_rows(normed))
     keep = lane_mask((8, padded), width)
 
     def group(g, carry):
@@ -244,7 +245,7 @@
         sums_ref[at, :] = jnp.broadcast_to(jnp.sum(pooled, axis=1, keepdims=True), (8, sums_ref.shape[1]))
         return carry
 
-    lax.fori_loop(0, ch // 8, group, 0, unroll=UNROLL)
+    lax.fori_loop(0, ch // 8, group, 0, unroll=True)
     pool_ref[...] = jnp.zeros(pool_ref.shape, F32)
     pool_ref[:, 0:ch] = jnp.broadcast_to(to_row(sums_ref[:, 0:1]), (8, ch))
 
@@ -269,43 +270,32 @@
     return pooled[0:1], product[0:1] + bias_ref[...]
 
 
-def tail_kernel(area, kept, parts, view_ref, band_ref, gating_ref, *refs):
+def tail_kernel(area, kept, picks, parts, view_ref, band_ref, gating_ref, *refs):
     pool_refs, refs = refs[:parts], refs[parts:]
-    proj_ref, bias_ref, squeeze_ref, branch_ref, up_ref, down_ref, scale_ref, hidden_ref, one_ref, expanded_ref = refs
-    half, ch, _ = hidden_ref.shape
+    proj_ref, bias_ref, squeeze_ref, branch_ref, up_ref, down_ref, scale_ref, one_ref, expanded_ref = refs[:9]
+    hidden_refs = refs[9:]
+    ch = squeeze_ref.shape[0]
     _, attention = attention_of(pool_refs, proj_ref, bias_ref, area)
     squeeze = left_lanes(to_column(branch_ref[...]) * squeeze_ref[...] * attention)
     up = left_rows(up_ref[...])
     down = left_lanes(to_column(scale_ref[...]) * down_ref[...])
-    base = base_of(view_ref, half, kept)
-    for k in range(half):
+    base = base_of(view_ref, band_ref.shape[0] // 2, kept)
+    for n, k in enumerate(picks):
         one = band_ref[base + k] + dot_nn(squeeze, right_rows(gating_ref[base + k]))
-        one_ref[k] = one
+        one_ref[n] = one
         expanded = dot_tn(up, right_rows(normed_of(one)[0]))
-        expanded_ref[k] = expanded
-        hidden_ref[k] = one + dot_nn(down, right_rows(expanded[:ch] * expanded[ch:]))
-
-
-def attend_kernel(
-    width,
-    hid0_ref,
-    hid1_ref,
-    cot0_ref,
-    q_ref,
-    v_ref,
-    s_ref,
-    other_ref,
-    out0_ref,
-    out1_ref,
-    dh0_ref,
-    dh1_ref,
-    grad0_ref,
-    grad1_ref,
-    e_ref,
-    eh_ref,
-    el_ref,
-):
-    half, ch, padded = hid0_ref.shape
+        expanded_ref[n] = expanded
+        hidden_refs[n][...] = one + dot_nn(down, right_rows(expanded[:ch] * expanded[ch:]))
+
+
+def attend_kernel(width, k, hid0_ref, hid1_ref, cot0_ref, q_ref, v_ref, s_ref, other_ref, *refs):
+    if k:
+        before_ref, refs = refs[0], refs[1:]
+    out0_ref, out1_ref, dh0_ref, dh1_ref, grad0_ref, grad1_ref, e_ref, eh_ref, el_ref = refs
+    ch, padded = hid0_ref.shape
+    half = cot0_ref.shape[0]
+    if k:
+        out1_ref[0:k] = before_ref[...]
     block = 128
     inv = ch ** (-0.5)
     mask = lane_mask((1, padded), width)
@@ -315,102 +305,97 @@
     scale = [to_column(x) for x in (s_ref[...], s_other)]
     lq, lv = [left_lanes(w) for w in wq], [left_lanes(w) for w in wv]
     lqt, lvt = [left_rows(w) for w in wq], [left_rows(w) for w in wv]
-    acc_q, acc_v, acc_s = [None, None], [None, None], [None, None]
-
-    def add(acc, s, value):
-        acc[s] = value if acc[s] is None else acc[s] + value
-
-    for k in range(half):
-        h = [ref[k] for ref in hids]
-        u = [cot0_ref[k], other_ref[k * ch : (k + 1) * ch, :]]
-        norms = [normed_of(x) for x in h]
-        q = [dot_nn(lq[s], right_rows(norms[s][0])) for s in range(2)]
-        v = [dot_nn(lv[s], right_rows(h[s])) for s in range(2)]
-        qh, ql = zip(*[split(q[0] * inv), split(q[1])])
-        vh, vl = zip(*[split(x) for x in v])
-        left = stack_rows(qh[0], qh[0], ql[0])
-        right = stack_rows(qh[1], ql[1], qh[1])
-        col_sum = jnp.zeros((1, padded), F32)
-        for b in range(0, padded, block):
-            scores = dot_tn(left[:, b : b + block], right)
-            weights = jnp.where(mask, jnp.exp(scores), 0.0)
-            if b + block > width:
-                rows_at = lax.broadcasted_iota(jnp.int32, (block, 1), 0) + b
-                weights = jnp.where(rows_at < width, weights, 0.0)
-            eh, el = split(weights)
-            e_ref[b : b + block, :] = weights
-            eh_ref[b : b + block, :] = eh
-            el_ref[b : b + block, :] = el
-            col_sum = col_sum + jnp.sum(weights, axis=0, keepdims=True)
-        b_inv = jnp.where(mask, 1.0 / jnp.where(mask, col_sum, 1.0), 0.0)
-        g = [scale[s] * u[s] for s in range(2)]
-        bg = g[1] * b_inv
-        bgh, bgl = split(bg)
-        ones = jnp.ones((16, padded), BF16)
-        first = dot_nt(stack_rows(vh[1], vl[1], bgh, bgl, ones), eh_ref[...])
-        second = dot_nt(stack_rows(vh[1], bgh, ones), el_ref[...])
-        row_sum = first[4 * ch : 4 * ch + 1] + second[2 * ch : 2 * ch + 1]
-        a_inv = jnp.where(mask, 1.0 / jnp.where(mask, row_sum, 1.0), 0.0)
-        carried0 = (first[0:ch] + first[ch : 2 * ch] + second[0:ch]) * a_inv
-        dv0 = first[2 * ch : 3 * ch] + first[3 * ch : 4 * ch] + second[ch : 2 * ch]
-        ag = g[0] * a_inv
-        agh, agl = split(ag)
-        first = dot_nn(stack_rows(vh[0], vl[0], agh, agl), eh_ref[...])
-        second = dot_nn(stack_rows(vh[0], agh), el_ref[...])
-        carried1 = (first[0:ch] + first[ch : 2 * ch] + second[0:ch]) * b_inv
-        dv1 = first[2 * ch : 3 * ch] + first[3 * ch : 4 * ch] + second[ch : 2 * ch]
-        out0_ref[k] = h[0] + scale[0] * carried0
-        out1_ref[k] = h[1] + scale[1] * carried1
-        d0 = jnp.sum(ag * carried0, axis=0, keepdims=True)
-        d1 = jnp.sum(bg * carried1, axis=0, keepdims=True)
-        d0h, d0l = split(d0)
-        row_at = lax.broadcasted_iota(jnp.int32, (16, padded), 0)
-        extra = jnp.where(row_at == 0, d0h.astype(F32), jnp.where(row_at == 1, d0l.astype(F32), 0.0)).astype(BF16)
-        left = stack_rows(agh, vh[0], agh, vh[0], agl, vl[0], extra)
-        right = stack_rows(vh[1], bgh, vl[1], bgl, vh[1], bgh, -ones)
-        for b in range(0, padded, block):
-            inner = dot_tn(left[:, b : b + block], right) - d1
-            dsh, dsl = split(e_ref[b : b + block, :] * inner)
-            eh_ref[b : b + block, :] = dsh
-            el_ref[b : b + block, :] = dsl
-        first = dot_nt(stack_rows(qh[1], ql[1]), eh_ref[...])
-        dq0 = (first[0:ch] + first[ch : 2 * ch] + dot_nt(qh[1], el_ref[...])) * inv
-        first = dot_nn(stack_rows(qh[0], ql[0]), eh_ref[...])
-        dq1 = first[0:ch] + first[ch : 2 * ch] + dot_nn(qh[0], el_ref[...])
-        dq, dv, carried = (dq0, dq1), (dv0, dv1), (carried0, carried1)
-        for s, ref in enumerate((dh0_ref, dh1_ref)):
-            normed, spread = norms[s]
-            dn = dot_tn(lqt[s], right_rows(dq[s]))
-            ref[k] = u[s] + norm_back(dn, normed, spread) + dot_tn(lvt[s], right_rows(dv[s]))
-            add(acc_q, s, outer_pixels(dq[s], normed))
-            add(acc_v, s, outer_pixels(dv[s], h[s]))
-            add(acc_s, s, u[s] * carried[s])
-    for s, ref in enumerate((grad0_ref, grad1_ref)):
-        ref[0:ch, 0:ch] = fold(acc_q[s])
-        ref[0:ch, ch : 2 * ch] = fold(acc_v[s])
-        ref[ch : ref.shape[0], :] = jnp.zeros((ref.shape[0] - ch, 2 * ch), F32)
-        ref[ch : ch + 1, 0:ch] = to_row(jnp.sum(acc_s[s], axis=1, keepdims=True))
-
-
-def tail_back_kernel(area, final, parts, view_ref, dh_ref, one_ref, expanded_ref, gating_ref, *refs):
+    h = [ref[...] for ref in hids]
+    u = [cot0_ref[k], other_ref[k * ch : (k + 1) * ch, :]]
+    norms = [normed_of(x) for x in h]
+    q = [dot_nn(lq[s], right_rows(norms[s][0])) for s in range(2)]
+    v = [dot_nn(lv[s], right_rows(h[s])) for s in range(2)]
+    qh, ql = zip(*[split(q[0] * inv), split(q[1])])
+    vh, vl = zip(*[split(x) for x in v])
+    left = stack_rows(qh[0], qh[0], ql[0])
+    right = stack_rows(qh[1], ql[1], qh[1])
+    col_sum = jnp.zeros((1, padded), F32)
+    for b in range(0, padded, block):
+        scores = dot_tn(left[:, b : b + block], right)
+        weights = jnp.where(mask, jnp.exp(scores), 0.0)
+        if b + block > width:
+            rows_at = lax.broadcasted_iota(jnp.int32, (block, 1), 0) + b
+            weights = jnp.where(rows_at < width, weights, 0.0)
+        eh, el = split(weights)
+        e_ref[b : b + block, :] = weights
+        eh_ref[b : b + block, :] = eh
+        el_ref[b : b + block, :] = el
+        col_sum = col_sum + jnp.sum(weights, axis=0, keepdims=True)
+    b_inv = jnp.where(mask, 1.0 / jnp.where(mask, col_sum, 1.0), 0.0)
+    g = [scale[s] * u[s] for s in range(2)]
+    bg = g[1] * b_inv
+    bgh, bgl = split(bg)
+    ones = jnp.ones((16, padded), BF16)
+    first = dot_nt(stack_rows(vh[1], vl[1], bgh, bgl, ones), eh_ref[...])
+    second = dot_nt(stack_rows(vh[1], bgh, ones), el_ref[...])
+    row_sum = first[4 * ch : 4 * ch + 1] + second[2 * ch : 2 * ch + 1]
+    a_inv = jnp.where(mask, 1.0 / jnp.where(mask, row_sum, 1.0), 0.0)
+    carried0 = (first[0:ch] + first[ch : 2 * ch] + second[0:ch]) * a_inv
+    dv0 = first[2 * ch : 3 * ch] + first[3 * ch : 4 * ch] + second[ch : 2 * ch]
+    ag = g[0] * a_inv
+    agh, agl = split(ag)
+    first = dot_nn(stack_rows(vh[0], vl[0], agh, agl), eh_ref[...])
+    second = dot_nn(stack_rows(vh[0], agh), el_ref[...])
+    carried1 = (first[0:ch] + first[ch : 2 * ch] + second[0:ch]) * b_inv
+    dv1 = first[2 * ch : 3 * ch] + first[3 * ch : 4 * ch] + second[ch : 2 * ch]
+    out0_ref[...] = h[0] + scale[0] * carried0
+    out1_ref[k] = h[1] + scale[1] * carried1
+    d0 = jnp.sum(ag * carried0, axis=0, keepdims=True)
+    d1 = jnp.sum(bg * carried1, axis=0, keepdims=True)
+    d0h, d0l = split(d0)
+    row_at = lax.broadcasted_iota(jnp.int32, (16, padded), 0)
+    extra = jnp.where(row_at == 0, d0h.astype(F32), jnp.where(row_at == 1, d0l.astype(F32), 0.0)).astype(BF16)
+    left = stack_rows(agh, vh[0], agh, vh[0], agl, vl[0], extra)
+    right = stack_rows(vh[1], bgh, vl[1], bgl, vh[1], bgh, -ones)
+    for b in range(0, padded, block):
+        inner = dot_tn(left[:, b : b + block], right) - d1
+        dsh, dsl = split(e_ref[b : b + block, :] * inner)
+        eh_ref[b : b + block, :] = dsh
+        el_ref[b : b + block, :] = dsl
+    first = dot_nt(stack_rows(qh[1], ql[1]), eh_ref[...])
+    dq0 = (first[0:ch] + first[ch : 2 * ch] + dot_nt(qh[1], el_ref[...])) * inv
+    first = dot_nn(stack_rows(qh[0], ql[0]), eh_ref[...])
+    dq1 = first[0:ch] + first[ch : 2 * ch] + dot_nn(qh[0], el_ref[...])
+    dq, dv, carried = (dq0, dq1), (dv0, dv1), (carried0, carried1)
+    for s, (ref, grad_ref) in enumerate(((dh0_ref, grad0_ref), (dh1_ref, grad1_ref))):
+        normed, spread = norms[s]
+        dn = dot_tn(lqt[s], right_rows(dq[s]))
+        ref[...] = u[s] + norm_back(dn, normed, spread) + dot_tn(lvt[s], right_rows(dv[s]))
+        grad_ref[0:ch, 0:ch] = fold(outer_pixels(dq[s], normed))
+        grad_ref[0:ch, ch : 2 * ch] = fold(outer_pixels(dv[s], h[s]))
+        grad_ref[ch : grad_ref.shape[0], :] = jnp.zeros((grad_ref.shape[0] - ch, 2 * ch), F32)
+        grad_ref[ch : ch + 1, 0:ch] = to_row(jnp.sum(u[s] * carried[s], axis=1, keepdims=True))
+
+
+def tail_back_kernel(area, kept, picks, first, final, parts, view_ref, slot_ref, gating_ref, one_ref, expanded_ref, *refs):
+    dh_refs, refs = refs[: len(picks)], refs[len(picks) :]
     pool_refs, refs = refs[:parts], refs[parts:]
     proj_ref, bias_ref, squeeze_ref, branch_ref, up_ref, down_ref, scale_ref = refs[:7]
     refs = refs[7:]
-    half, ch, _ = dh_ref.shape
-    base = base_of(view_ref, half, not final)
-    pooled, attention = attention_of(pool_refs, proj_ref, bias_ref, area)
+    if not first:
+        acc_in, refs = refs[0], refs[1:]
+    if final:
+        own_ref, dgate_ref, done_ref, pg_ref, grad_ref = refs
+    else:
+        dgate_ref, done_ref, acc_ref = refs
+    ch = squeeze_ref.shape[0]
+    base = base_of(view_ref, gating_ref.shape[0] // 2, kept)
+    _, attention = attention_of(pool_refs, proj_ref, bias_ref, area)
     branch, scale = to_column(branch_ref[...]), to_column(scale_ref[...])
     mixed = branch * squeeze_ref[...]
     squeeze = left_rows(mixed * attention)
     up = left_lanes(up_ref[...])
     down = left_rows(scale * down_ref[...])
-    if final:
-        acc_in, dgate_ref, done_ref, pg_ref, grad_ref = refs
-    else:
-        dgate_ref, done_ref, acc_ref = refs
     acc1 = acc2 = acc3 = None
-    for k in range(half):
-        dh, one, expanded = dh_ref[k], one_ref[k], expanded_ref[k]
+    if not first:
+        acc1, acc2, acc3 = acc_in[:, 0 : 2 * ch], acc_in[:, 2 * ch : 6 * ch], acc_in[:, 6 * ch : 8 * ch]
+    for n, k in enumerate(picks):
+        dh, one, expanded = dh_refs[n][...], one_ref[n], expanded_ref[n]
         lower, upper = expanded[:ch], expanded[ch:]
         normed, spread = normed_of(one)
         term1 = outer_pixels(dh, lower * upper)
@@ -419,9 +404,9 @@
         term2 = outer_pixels(normed, dexp)
         dn = dot_nn(up, right_rows(dexp))
         done = dh + norm_back(dn, normed, spread)
-        done_ref[k] = done
+        done_ref[n] = done
         term3 = outer_pixels(done, gating_ref[base + k])
-        dgate_ref[k] = dot_tn(squeeze, right_rows(done))
+        dgate_ref[n] = dot_tn(squeeze, right_rows(done))
         acc1 = term1 if acc1 is None else acc1 + term1
         acc2 = term2 if acc2 is None else acc2 + term2
         acc3 = term3 if acc3 is None else acc3 + term3
@@ -430,11 +415,8 @@
         acc_ref[:, 2 * ch : 6 * ch] = acc2
         acc_ref[:, 6 * ch : 8 * ch] = acc3
         return
-    m1 = fold(acc1 + acc_in[:, 0 : 2 * ch])
-    m2 = fold(acc2 + acc_in[:, 2 * ch : 6 * ch])
-    m3 = fold(acc3 + acc_in[:, 6 * ch : 8 * ch])
+    m1, m2, m3 = fold(acc1), fold(acc2), fold(acc3)
     datt = jnp.sum(mixed * m3, axis=0, keepdims=True)
-    dcol = to_column(datt)
     dh8, dl8 = split(jnp.broadcast_to(datt, (8, ch)))
     ph, plow = split(proj_ref[...])
     pg_ref[...] = jnp.zeros(pg_ref.shape, F32)
@@ -442,39 +424,46 @@
     grad_ref[0:ch, :] = m2
     grad_ref[ch : 2 * ch, 0:ch] = scale * m1
     grad_ref[ch : 2 * ch, ch : 2 * ch] = branch * m3 * attention
-    grad_ref[2 * ch : 3 * ch, 0:ch] = dcol * pooled
+    slots = grad_ref.shape[0] - 2 * ch - 8
+    here = lax.broadcasted_iota(jnp.int32, (slots, ch), 0) == slot_ref[0]
+    at = slice(2 * ch, 2 * ch + slots)
+    grad_ref[at, 0:ch] = jnp.where(here, datt, 0.0)
+    grad_ref[at, ch : 2 * ch] = jnp.where(here, own_ref[0:1, 0:ch] * (1.0 / area), 0.0)
+    at = slice(2 * ch + slots, 2 * ch + slots + 8)
     dscale = jnp.sum(down_ref[...] * m1, axis=1, keepdims=True)
     dbranch = jnp.sum(squeeze_ref[...] * attention * m3, axis=1, keepdims=True)
-    row_at = lax.broadcasted_iota(jnp.int32, (ch, ch), 0)
-    vectors = jnp.where(row_at == 0, datt, jnp.where(row_at == 1, to_row(dbranch), jnp.where(row_at == 2, to_row(dscale), 0.0)))
-    grad_ref[2 * ch : 3 * ch, ch : 2 * ch] = vectors
-
-
-def conv_back_kernel(width, parts, view_ref, core_ref, *refs):
-    conv_back_body(width, view_ref, core_ref, refs[:parts], *refs[parts:])
+    grad_ref[at, 0:ch] = jnp.broadcast_to(to_row(dbranch), (8, ch))
+    grad_ref[at, ch : 2 * ch] = jnp.broadcast_to(to_row(dscale), (8, ch))
+
+
+def conv_back_kernel(width, parts, half, view_ref, core_ref, odd_ref, *refs):
+    pools, refs = refs[:parts], refs[parts:]
+    sends, refs = refs[:half], refs[half:]
+    owns, others, refs = refs[:half], refs[half : 2 * half], refs[2 * half :]
+    conv_back_body(width, view_ref, core_ref, odd_ref, pools, sends, owns, others, *refs)
 
 
 def conv_back_body(
     width,
     view_ref,
     core_ref,
+    odd_ref,
     pg_refs,
+    dsend_refs,
+    own_refs,
+    other_refs,
     dkeep_ref,
-    dsend_ref,
     conv_ref,
     doubled_ref,
     edge_ref,
     band_ref,
-    up_ref,
-    down_ref,
+    halo_ref,
     exp_ref,
     kt_ref,
-    own_ref,
-    other_ref,
     gradb_ref,
     dn_ref,
-    dnup_ref,
-    dndown_ref,
+    first_ref,
+    second_ref,
     mine_ref,
     theirs_ref,
     all_ref,
@@ -482,6 +471,8 @@
     bg_ref,
     gk_ref,
     pgcol_ref,
+    own_ref,
+    other_ref,
 ):
     rows, wide, padded = conv_ref.shape
     ch = wide // 2
@@ -490,7 +481,7 @@
     pgcol_ref[...] = jnp.broadcast_to(to_column(total_of(pg_refs)[0:1, 0:ch]), pgcol_ref.shape)
     for k in range(half):
         dgate_ref[half * view + k] = dkeep_ref[k]
-        dgate_ref[half * (1 - view) + k] = dsend_ref[k]
+        dgate_ref[half * (1 - view) + k] = dsend_refs[k][0]
     keep = lane_mask((8, padded), width)
     lanes = lax.broadcasted_iota(jnp.int32, (8, 128), 1)
 
@@ -537,25 +528,33 @@
             gk_ref[own, :] = packed
         return carry
 
-    lax.fori_loop(0, ch // 8, group, 0, unroll=UNROLL)
+    lax.fori_loop(0, ch // 8, group, 0, unroll=True)
     weight = left_lanes(exp_ref[...])
     acc = None
     for r in range(rows + 2):
-        source = up_ref[...] if r == 0 else down_ref[...] if r == rows + 1 else band_ref[r - 1]
+        normed = halo_ref[0] if r == 0 else halo_ref[1] if r == rows + 1 else normed_of(band_ref[r - 1])[0]
         back = bg_ref[r]
-        term = outer_pixels(normed_of(source)[0], back)
+        term = outer_pixels(normed, back)
         acc = term if acc is None else acc + term
         value = dot_nn(weight, right_rows(back))
         if r == 0:
-            dnup_ref[...] = value
+            above = value
         elif r == rows + 1:
-            dndown_ref[...] = value
+            below = value
         else:
             dn_ref[r - 1] = value
+    odd = odd_ref[0] == 1
+    first_ref[...] = jnp.where(odd, above, below)
+    second_ref[...] = jnp.where(odd, below, above)
     at = gradb_ref.shape[0]
     all_ref[0:at, :] = gradb_ref[...]
     all_ref[at : at + ch, :] = fold(acc)
     all_ref[at + ch : at + ch + 16, :] = gk_ref[...].T[0:16, :]
+    at = at + ch + 16
+    if at < all_ref.shape[0]:
+        all_ref[at : all_ref.shape[0], :] = jnp.zeros((all_ref.shape[0] - at, wide), F32)
+    own_ref[...] = total_of(own_refs)
+    other_ref[...] = total_of(other_refs)
     core = core_ref[0]
     place = 0
     for ref in (all_ref, own_ref, other_ref):
@@ -570,35 +569,37 @@
     o_ref[:, row, :] = value[:, 0 : o_ref.shape[2]]
 
 
-def front_back_kernel(view_ref, dn_ref, above_ref, below_ref, band_ref, keep_ref, send_ref, o_ref, scratch_ref):
+def collect(view_ref, scratch_ref, kept, sent):
+    half = scratch_ref.shape[0] // 2
+    for k in range(half):
+        scratch_ref[base_of(view_ref, half, True) + k] = kept[k]
+        scratch_ref[base_of(view_ref, half, False) + k] = sent[k]
+
+
+def front_back_kernel(half, view_ref, odd_ref, dn_ref, first_ref, second_ref, band_ref, keep_ref, *refs):
+    sends, (o_ref, scratch_ref) = refs[:half], refs[half:]
     rows = dn_ref.shape[0]
-    half = rows // 2
-    view = view_ref[0]
-    for k in range(half):
-        scratch_ref[half * view + k] = keep_ref[k]
-        scratch_ref[half * (1 - view) + k] = send_ref[k]
+    collect(view_ref, scratch_ref, keep_ref, [ref[0] for ref in sends])
     for h in range(rows):
         dn = dn_ref[h]
         if h == 0:
-            dn = dn + above_ref[...]
+            dn = dn + jnp.where(odd_ref[0] == 1, first_ref[...], second_ref[...])
         if h == rows - 1:
-            dn = dn + below_ref[...]
+            dn = dn + jnp.where(odd_ref[0] == 1, second_ref[...], first_ref[...])
         normed, spread = normed_of(band_ref[h])
         place_rows(o_ref, h, scratch_ref[h] + norm_back(dn, normed, spread))
 
 
-def assemble_kernel(view_ref, keep_ref, send_ref, o_ref, scratch_ref):
-    half = keep_ref.shape[0]
-    view = view_ref[0]
-    for k in range(half):
-        scratch_ref[half * view + k] = keep_ref[k]
-        scratch_ref[half * (1 - view) + k] = send_ref[k]
+def assemble_kernel(half, view_ref, sent_ref, *refs):
+    keeps, (o_ref, scratch_ref) = refs[:half], refs[half:]
+    collect(view_ref, scratch_ref, [ref[...] for ref in keeps], sent_ref)
     for h in range(2 * half):
         place_rows(o_ref, h, scratch_ref[h])
 
 
 def finish_kernel(
     factor,
+    slots,
     core_ref,
     mine_ref,
     theirs_ref,
@@ -630,11 +631,19 @@
     down_ref[...] = all_ref[ch : 2 * ch, 0:ch]
     squeeze_ref[...] = all_ref[ch : 2 * ch, ch : 2 * ch]
     at = 2 * ch
-    pool_ref[...] = all_ref[at : at + ch, 0:ch]
-    bias_ref[...] = all_ref[at : at + 1, ch : 2 * ch]
-    branch_ref[...] = all_ref[at + 1 : at + 2, ch : 2 * ch]
-    scale_ref[...] = all_ref[at + 2 : at + 3, ch : 2 * ch]
-    at = at + ch
+    slots = all_ref[at : at + slots, :]
+    pool_ref[...] = lax.dot_general(
+        slots[:, 0:ch],
+        slots[:, ch : 2 * ch] * (1.0 / factor),
+        (((0,), (0,)), ((), ())),
+        precision=lax.Precision.HIGHEST,
+        preferred_element_type=F32,
+    )
+    bias_ref[...] = jnp.sum(slots[:, 0:ch], axis=0, keepdims=True)
+    at = at + slots.shape[0]
+    branch_ref[...] = all_ref[at : at + 1, 0:ch]
+    scale_ref[...] = all_ref[at : at + 1, ch : 2 * ch]
+    at = at + 8
     exp_ref[...] = all_ref[at : at + ch, :]
     at = at + ch
     for i in range(3):
@@ -722,6 +731,9 @@
     factor = (2 * frames * lax.axis_size("dp") * area) ** (-0.5)
     view = lax.axis_index("view").astype(jnp.int32).reshape(1)
     core = (lax.axis_index("dp").astype(jnp.int32) & 1).reshape(1)
+    odd = (lax.axis_index("row").astype(jnp.int32) & 1).reshape(1)
+    slot = (2 * lax.axis_index("dp") + lax.axis_index("view")).astype(jnp.int32).reshape(1)
+    slots = -(-2 * lax.axis_size("dp") // 8) * 8
     part, full = (half, ch, padded), (rows, ch, padded)
     row = (ch, padded)
     exp_t, up_t = expand_in.T, ffn_expand.T
@@ -731,26 +743,29 @@
 
     lines = half * ch + wide * ch // padded + 8
     query, value = query_proj[0], value_proj[0]
-    image = vm(ch, rows, width)
-    band, first, last, cot_keep, pack = call(
-        start_kernel,
-        [full, row, row, part, (lines, padded)],
+    band, border0, border1 = call(start_kernel, [full, row, row], view, core, odd, slot, frames_in[0, 0], scalars=4)
+    pairs = [
+        [pair for i in range(begin, bands - 1, 2) for pair in ((i, i + 1), (i + 1, i))] for begin in range(2)
+    ]
+
+    def meet(x, turn):
+        return lax.ppermute(x, "row", pairs[turn])
+
+    border0 = meet(border0, 0)
+    border1 = meet(border1, 1)
+    square, line = (ch, ch), (1, ch)
+    fars = (query, value, cross_scale, pool_proj, bias, squeeze_out, branch, up_t, ffn_shrink, scale)
+    cot_keep, pack, *nears = call(
+        functools.partial(pack_kernel, len(fars)),
+        [part, (lines, padded)] + [x.shape for x in fars],
         view,
-        core,
-        frames_in[0, 0],
+        *(pltpu.with_memory_space_constraint(x, pltpu.HBM) for x in fars),
         cotangent[0, 0],
-        query,
-        value,
-        cross_scale,
-        scalars=2,
-        far=5,
-        scratch=[image, image, vm(ch, ch), vm(ch, ch), vm(1, ch), vm(rows, ch, padded), pltpu.SemaphoreType.DMA((5,))],
-        limit=67043328 - 4 * padded * (rows * ch + 2 * ch + half * ch + lines) * 17 // 16,
+        scalars=1,
+        far=len(fars),
+        scratch=[vm(rows, ch, padded), pltpu.SemaphoreType.DMA((len(fars),))],
     )
-    up_pairs = [(i, i + 1) for i in range(bands - 1)]
-    down_pairs = [(i + 1, i) for i in range(bands - 1)]
-    above = lax.ppermute(last, "row", up_pairs)
-    below = lax.ppermute(first, "row", down_pairs)
+    query, value, cross, pool_proj, bias, squeeze_out, branch, up_t, ffn_shrink, scale = nears
     other = swap(pack, "view", 1)
     doubled, conv, gating, pool, taps = call(
         functools.partial(conv_own_kernel, width),
@@ -759,104 +774,134 @@
         exp_t,
         k_rows,
     )
-    conv, gating, edge, pool = call(
+    conv, gating, edge, halo, pool = call(
         functools.partial(conv_edge_kernel, width),
-        [(rows, wide, padded), full, (2, wide, padded), (8, wide)],
+        [(rows, wide, padded), full, (2, wide, padded), (2, ch, padded), (8, wide)],
+        odd,
         conv,
         gating,
         pool,
         taps,
-        above,
-        below,
+        border0,
+        border1,
         exp_t,
+        scalars=1,
         scratch=[vm(ch, 128)],
-        aliases={0: 0, 1: 1},
+        aliases={1: 0, 2: 1},
     )
     pools = parts_over(pool, "row")
     parts = len(pools)
     weights = pools + (pool_proj, bias, squeeze_out, branch, up_t, ffn_shrink, scale)
 
-    def tail(kept):
-        return call(
-            functools.partial(tail_kernel, area, kept, parts),
-            [part, part, (half, wide, padded)],
+    every = range(half)
+
+    def tail(kept, picks):
+        count = len(picks)
+        one, expanded, *hidden = call(
+            functools.partial(tail_kernel, area, kept, picks, parts),
+            [(count, ch, padded), (count, wide, padded)] + [row] * count,
             view,
             band,
             gating,
             *weights,
             scalars=1,
         )
-
-    hid_send, one_send, expanded_send = tail(False)
-    hid_other = swap(hid_send, "view", 1)
-    hid_keep, one_keep, expanded_keep = tail(True)
-    out_keep, out_send, dh_keep, dh_send, grad_own, grad_other = call(
-        functools.partial(attend_kernel, width),
-        [part, part, part, part, (ch + 16, wide), (ch + 16, wide)],
-        hid_keep,
-        hid_other,
-        cot_keep,
-        query,
-        value,
-        cross_scale,
-        other,
-        scratch=[vm(padded, padded), pltpu.VMEM((padded, padded), BF16), pltpu.VMEM((padded, padded), BF16)],
-    )
-    dh_back = swap(dh_send, "view", 1)
+        return one, expanded, hidden
+
+    sent, hid_other = [], []
+    for k in every:
+        one, expanded, (hidden,) = tail(False, (k,))
+        sent.append((one, expanded))
+        hid_other.append(swap(hidden, "view", 1))
+    one_keep, expanded_keep, hid_keep = tail(True, tuple(every))
+    out_keep, dh_keep, dh_back, own_grads, other_grads = [], [], [], [], []
+    out_send = ()
+    for k in every:
+        out, out_send, dh, dh_send, own, other_grad = call(
+            functools.partial(attend_kernel, width, k),
+            [row, (k + 1, ch, padded), row, row, (ch + 16, wide), (ch + 16, wide)],
+            hid_keep[k],
+            hid_other[k],
+            cot_keep,
+            query,
+            value,
+            cross,
+            other,
+            *((out_send,) if k else ()),
+            scratch=[vm(padded, padded), pltpu.VMEM((padded, padded), BF16), pltpu.VMEM((padded, padded), BF16)],
+        )
+        out_keep.append(out)
+        dh_keep.append(dh)
+        own_grads.append(own)
+        other_grads.append(other_grad)
+        dh_back.append(swap(dh_send, "view", 1))
     out_back = swap(out_send, "view", 1)
-    dgate_keep, done_keep, acc = call(
-        functools.partial(tail_back_kernel, area, False, parts),
-        [part, part, (wide, 8 * ch)],
-        view,
-        dh_keep,
-        one_keep,
-        expanded_keep,
-        gating,
-        *weights,
-        scalars=1,
-    )
-    dgate_send, done_send, pool_grad, grad_b = call(
-        functools.partial(tail_back_kernel, area, True, parts),
-        [part, part, (8, wide), (3 * ch, wide)],
-        view,
-        dh_back,
-        one_send,
-        expanded_send,
-        gating,
-        *weights,
-        acc,
-        scalars=1,
-    )
+
+    def tail_back(kept, picks, final, one, expanded, dh, acc):
+        count = len(picks)
+        ends = [(8, wide), (2 * ch + slots + 8, wide)] if final else [(wide, 8 * ch)]
+        return call(
+            functools.partial(tail_back_kernel, area, kept, picks, acc is None, final, parts),
+            [(count, ch, padded)] * 2 + ends,
+            view,
+            slot,
+            gating,
+            one,
+            expanded,
+            *dh,
+            *weights,
+            *(() if acc is None else (acc,)),
+            *((pool,) if final else ()),
+            scalars=2,
+        )
+
+    dgate_keep, done_keep, acc = tail_back(True, tuple(every), False, one_keep, expanded_keep, dh_keep, None)
+    dgate_send, done_send = [], []
+    for k in every:
+        final = k == half - 1
+        dgate, done, *rest = tail_back(False, (k,), final, *sent[k], [dh_back[k]], acc)
+        acc = rest[0]
+        dgate_send.append(dgate)
+        done_send.append(done)
+    pool_grad, grad_b = rest
     pool_grads = parts_over(pool_grad, "row")
     (output,) = call(
-        assemble_kernel, [(ch, rows, width)], view, out_keep, out_back, scalars=1, scratch=[vm(rows, ch, padded)]
+        functools.partial(assemble_kernel, half),
+        [(ch, rows, width)],
+        view,
+        out_back,
+        *out_keep,
+        scalars=1,
+        scratch=[vm(rows, ch, padded)],
     )
-    shared_lines, owned_lines = 4 * ch + 16, ch + 16
+    shared_lines = -(-(2 * ch + slots + 8 + ch + 16) // 16) * 16
+    owned_lines = ch + 16
     piece = shared_lines // 2 + owned_lines
-    dn, dn_up, dn_down, mine, theirs = call(
-        functools.partial(conv_back_kernel, width, len(pool_grads)),
+    dn, border0, border1, mine, theirs = call(
+        functools.partial(conv_back_kernel, width, len(pool_grads), half),
         [full, row, row, (piece, wide), (piece, wide)],
         view,
         core,
+        odd,
         *pool_grads,
+        *dgate_send,
+        *own_grads,
+        *other_grads,
         dgate_keep,
-        dgate_send,
         conv,
         doubled,
         edge,
         band,
-        above,
-        below,
+        halo,
         exp_t,
         taps,
-        grad_own,
-        grad_other,
         grad_b,
-        scalars=2,
-        scratch=[vm(shared_lines, wide), vm(rows, ch, padded), vm(rows + 2, wide, padded), vm(wide, wide), vm(ch, wide)],
+        scalars=3,
+        scratch=[vm(shared_lines, wide), vm(rows, ch, padded), vm(rows + 2, wide, padded), vm(wide, wide), vm(ch, wide)]
+        + [vm(owned_lines, wide)] * 2,
     )
-    from_above = lax.ppermute(dn_down, "row", up_pairs)
-    from_below = lax.ppermute(dn_up, "row", down_pairs)
+    border0 = meet(border0, 0)
+    border1 = meet(border1, 1)
     both = (shared_lines + owned_lines) // 2
     mine, send = call(add_split_kernel, [(both, wide)] * 2, mine, swap(theirs, "dp", 1))
     mine = add(mine, swap(send, "view", 1))
@@ -864,21 +909,21 @@
     mine = sum_over(mine, "row")
     theirs = swap(mine, "dp", 1)
     (frames_grad,) = call(
-        front_back_kernel,
+        functools.partial(front_back_kernel, half),
         [(ch, rows, width)],
         view,
+        odd,
         dn,
-        from_above,
-        from_below,
+        border0,
+        border1,
         band,
         done_keep,
-        done_send,
-        scalars=1,
+        *done_send,
+        scalars=2,
         scratch=[vm(rows, ch, padded)],
     )
-    square, line = (ch, ch), (1, ch)
     g_up, g_down, g_squeeze, g_pool, g_bias, g_branch, g_scale, g_exp, g_k, g_q, g_v, g_s = call(
-        functools.partial(finish_kernel, factor),
+        functools.partial(finish_kernel, factor, slots),
         [(ch, wide), square, square, square, line, line, line, (ch, wide), (3, 3, wide), square, square, line],
         core,
         mine,

time: 86 us -> 75.8 us (0.88)
  waiting for transfers between devices: 29.9 us -> 22.8 us
  Pallas kernels: 22.6 us -> 20.9 us
  local copies, waits for them, and re-layouts: 2.36 us -> 1.05 us
    ppermute x4, starting transfers between devices: 10.6 us -> 2.96 us  [meet(): return lax.ppermute(x, 'row', pairs[turn])]
    ppermute x16 -> x18, starting transfers between devices: 19.4 us -> 26.5 us  [swap(): lax.ppermute(x, axis, [(i, i ^ mask) for i in range(lax.axis_size(axis))])]
    ppermute x4, waiting for transfers between devices: 5.91 us -> 1.3 us  [meet(): return lax.ppermute(x, 'row', pairs[turn])]
    ppermute x16 -> x18, waiting for transfers between devices: 24 us -> 21.5 us  [swap(): lax.ppermute(x, axis, [(i, i ^ mask) for i in range(lax.axis_size(axis))])]
    pallas_call x17 -> x21, Pallas kernels: 22.6 us -> 20.9 us  [call(): pl.pallas_call(kernel, out_shape=shapes, in_specs=[smem] * scalars + [hbm...]
    unnamed x30 -> x8, local copies, waits for them, and re-layouts: 2.36 us -> 1.05 us
  transfers between devices with their start and end apart: 20 -> 22, of which waited for: 13 -> 12; matrix products, arithmetic and copies ran while one was open for 0% -> 0% of each run, Pallas kernels for 11% -> 19%
where the time goes in v3:
time: 75.8 us; the launch traced here: 75 us
  starting transfers between devices  29.4 us (39%)
  waiting for transfers between devices  22.8 us (30%)
  Pallas kernels  20.9 us (28%)
  local copies, waits for them, and re-layouts  1.05 us (1%)
  between operations  0.91 us (1%)
    ppermute x18, starting transfers between devices, swap(): lax.ppermute(x, axis, [(i, i ^ mask) for i in range(lax.axis_size(axis))])  26.5 us
    ppermute x18, waiting for transfers between devices, swap(): lax.ppermute(x, axis, [(i, i ^ mask) for i in range(lax.axis_size(axis))])  21.5 us
    pallas_call x21, Pallas kernels, call(): pl.pallas_call(kernel, out_shape=shapes, in_specs=[smem] * scalars + [hbm...  20.9 us
    ppermute x4, starting transfers between devices, meet(): return lax.ppermute(x, 'row', pairs[turn])  2.96 us
  transfers between devices with their start and end apart: 22, of which 12 were waited for; matrix products, arithmetic and copies ran while one was open for 0% of the time, Pallas kernels for 19%

profile of v3, /device:TPU:0, one launch (start us, length us, event | category | flops | bytes accessed | tf_op | source)
XLA Modules:
  0.0 75.0 jit_solution(17524032751130357350)
XLA Ops:
  0.7 0.0 copy-start
  0.7 1.0 %copy-done = f32[1,1,64,4,480]{4,3,2,1,0:T(4,128)S(1)} copy-done((f32[1,1,64,4,480]{4,3,2,1,0:T(4,128)S(1)}, f32[1,1,64,4,480]{4,3,2,1,0:T(4,128)}, u32[]{:S(2)}) %copy-start) | copy-done | bytes 491544
  1.7 1.1 %shard_map.248 = (f32[2,64,512]{2,1,0:T(8,128)S(1)}, f32[152,512]{1,0:T(8,128)S(1)}, f32[64,64]{1,0:T(8,128)S(1)}, f32[64,64]{1,0:T(8,128)S(1)}, f32[1,64]{1,0:T...) custom-call(s32[1]{0:T(128)} %bitcast.view_ref, ...), custom_call_target="tpu_custom_call" | custom-call | tf_op jit(solution)/shard_map/pallas_call | solution.py:673
  2.8 3.0 %collective-permute-start.6 = (f32[152,512]{1,0:T(8,128)S(1)}, f32[152,512]{1,0:T(8,128)S(1)}, u32[]{:S(2)}, u32[]{:S(2)}) collective-permute-start(f32[152,512]{1,0:T(8,128)S(1)} %get-tuple-element.112), channel_id=1, source_target_pairs={{0,1},{1,0},{2,3},{3,2},{4,5},{5,4},{6,7},{7,6},{8,9},{9,8},{10,11... | collective-permute-start | bytes 933896 | tf_op jit(solution)/shard_map/ppermute | solution.py:685
  5.9 0.0 copy-done.1
  5.9 0.1 shard_map.245
  6.0 0.0 copy-start.3
  6.0 1.6 %collective-permute-start = (f32[64,512]{1,0:T(8,128)S(1)}, f32[64,512]{1,0:T(8,128)S(1)}, u32[]{:S(2)}, u32[]{:S(2)}) collective-permute-start(f32[64,512]{1,0:T(8,128)S(1)} %get-tuple-element.95), channel_id=1, source_target_pairs={{0,2},{2,0},{4,6},{6,4},{1,3},{3,1},{5,7},{7,5},{8,10},{10,8},{12,... | collective-permute-start | bytes 393224 | tf_op jit(solution)/shard_map/ppermute | solution.py:752
  7.6 0.7 collective-permute-start.1
  8.3 1.4 %shard_map.246 = (f32[4,128,512]{2,1,0:T(8,128)S(1)}, f32[4,128,512]{2,1,0:T(8,128)S(1)}, f32[4,64,512]{2,1,0:T(8,128)S(1)}, f32[64,512]{1,0:T(8,128)S(1)}, f32[128,128]{1,0:T(8,128)S(1)}) custom-call(f32[4,64,512]{2,1,0:T(8,128)S(1)} %get-tuple-element.90.band_ref.refs_14_, f32[64,128]{1,0:T(8,128)S(1)} %bitcast.26, f32[3,3,128]{2,1,0:T(4,128)S(1)} %bitcast.29), custom_call_target="tpu_custom_call" | custom-call | tf_op jit(solution)/shard_map/pallas_call | solution.py:673
  9.8 1.3 %collective-permute-done.first_ref = f32[64,512]{1,0:T(8,128)S(1)} collective-permute-done((f32[64,512]{1,0:T(8,128)S(1)}, f32[64,512]{1,0:T(8,128)S(1)}, u32[]{:S(2)}, u32[]{:S(2)}) %collective-permute-start) | collective-permute-done | bytes 131104 | tf_op jit(solution)/shard_map/ppermute | solution.py:752
  11.0 0.0 collective-permute-done.1.second_ref
  11.0 1.0 %shard_map.247 = (f32[4,128,512]{2,1,0:T(8,128)S(1)}, f32[4,64,512]{2,1,0:T(8,128)S(1)}, f32[2,128,512]{2,1,0:T(8,128)S(1)}, f32[2,64,512]{2,1,0:T(8,128)S(1)}, f32[8,128]{1,0:T(8,128)S(1)}) custom-call(s32[1]{0:T(128)} %bitcast.2.odd_ref, f32[4,128,512]{2,1,0:T(8,128)S(1)} %get-tuple-element.91.conv_in, ...), custom_call_target="tpu_custom_call", output_to_operand_aliasing={{0}: (1, {}), {1}: (2, {})} | custom-call | tf_op jit(solution)/shard_map/pallas_call | solution.py:673
  12.1 3.6 %collective-permute-start.4 = (f32[8,128]{1,0:T(8,128)S(1)}, f32[8,128]{1,0:T(8,128)S(1)}, u32[]{:S(2)}, u32[]{:S(2)}) collective-permute-start(f32[8,128]{1,0:T(8,128)S(1)} %get-tuple-element.98.refs_0_.refs_2_.refs_1_.refs_13_), channel_id=1, source_target_pairs={{0,6},{2,4},{4,2},{6,0},{1,7},{3,5},{5,3},{7,1},{8,14},{10,12},{12... | collective-permute-start | bytes 12296 | tf_op jit(solution)/shard_map/ppermute | solution.py:685
  15.7 2.5 %collective-permute-start.3 = (f32[8,128]{1,0:T(8,128)S(1)}, f32[8,128]{1,0:T(8,128)S(1)}, u32[]{:S(2)}, u32[]{:S(2)}) collective-permute-start(f32[8,128]{1,0:T(8,128)S(1)} %get-tuple-element.98.refs_0_.refs_2_.refs_1_.refs_13_), channel_id=1, source_target_pairs={{0,4},{2,6},{4,0},{6,2},{1,5},{3,7},{5,1},{7,3},{8,12},{10,14},{12... | collective-permute-start | bytes 12296 | tf_op jit(solution)/shard_map/ppermute | solution.py:685
  18.2 0.5 collective-permute-start.2
  18.7 0.0 collective-permute-done.4.refs_3_.refs_5_.refs_4_
  18.7 1.5 %collective-permute-done.3.refs_2_.refs_4_.refs_3_ = f32[8,128]{1,0:T(8,128)S(1)} collective-permute-done((f32[8,128]{1,0:T(8,128)S(1)}, f32[8,128]{1,0:T(8,128)S(1)}, u32[]{:S(2)}, u32[]{:S(2)}) %collective-permute-start.3) | collective-permute-done | bytes 4128 | tf_op jit(solution)/shard_map/ppermute | solution.py:685
  20.2 1.6 %collective-permute-done.2.refs_1_.refs_3_.refs_2_ = f32[8,128]{1,0:T(8,128)S(1)} collective-permute-done((f32[8,128]{1,0:T(8,128)S(1)}, f32[8,128]{1,0:T(8,128)S(1)}, u32[]{:S(2)}, u32[]{:S(2)}) %collective-permute-start.2) | collective-permute-done | bytes 4128 | tf_op jit(solution)/shard_map/ppermute | solution.py:685
  21.8 0.8 %shard_map.251 = (f32[1,64,512]{2,1,0:T(8,128)S(1)}, f32[1,128,512]{2,1,0:T(8,128)S(1)}, f32[64,512]{1,0:T(8,128)S(1)}) custom-call(s32[1]{0:T(128)} %bitcast.view_ref, f32[4,64,512]{2,1,0:T(8,128)S(1)} %get-tuple-element.90.band_ref.refs_14_, f32[4,64,512]{2,1,0:T(8,128)S(1)} %get-tuple-element.97.gating_ref, ...), custom_call_target="tpu_custom_call" | custom-call | tf_op jit(solution)/shard_map/pallas_call | solution.py:673
  22.6 0.6 collective-permute-start.7
  23.2 0.8 %shard_map.250 = (f32[1,64,512]{2,1,0:T(8,128)S(1)}, f32[1,128,512]{2,1,0:T(8,128)S(1)}, f32[64,512]{1,0:T(8,128)S(1)}) custom-call(s32[1]{0:T(128)} %bitcast.view_ref, f32[4,64,512]{2,1,0:T(8,128)S(1)} %get-tuple-element.90.band_ref.refs_14_, f32[4,64,512]{2,1,0:T(8,128)S(1)} %get-tuple-element.97.gating_ref, ...), custom_call_target="tpu_custom_call" | custom-call | tf_op jit(solution)/shard_map/pallas_call | solution.py:673
  23.9 1.5 %collective-permute-start.5 = (f32[64,512]{1,0:T(8,128)S(1)}, f32[64,512]{1,0:T(8,128)S(1)}, u32[]{:S(2)}, u32[]{:S(2)}) collective-permute-start(f32[64,512]{1,0:T(8,128)S(1)} %get-tuple-element.107), channel_id=1, source_target_pairs={{0,1},{1,0},{2,3},{3,2},{4,5},{5,4},{6,7},{7,6},{8,9},{9,8},{10,11... | collective-permute-start | bytes 393224 | tf_op jit(solution)/shard_map/ppermute | solution.py:685
  25.5 1.2 %shard_map.249 = (f32[2,64,512]{2,1,0:T(8,128)S(1)}, f32[2,128,512]{2,1,0:T(8,128)S(1)}, f32[64,512]{1,0:T(8,128)S(1)}, f32[64,512]{1,0:T(8,128)S(1)}) custom-call(s32[1]{0:T(128)} %bitcast.view_ref, f32[4,64,512]{2,1,0:T(8,128)S(1)} %get-tuple-element.90.band_ref.refs_14_, f32[4,64,512]{2,1,0:T(8,128)S(1)} %get-tuple-element.97.gating_ref, ...), custom_call_target="tpu_custom_call" | custom-call | tf_op jit(solution)/shard_map/pallas_call | solution.py:673
  26.6 1.0 %collective-permute-done.7.hid1_ref = f32[64,512]{1,0:T(8,128)S(1)} collective-permute-done((f32[64,512]{1,0:T(8,128)S(1)}, f32[64,512]{1,0:T(8,128)S(1)}, u32[]{:S(2)}, u32[]{:S(2)}) %collective-permute-start.7) | collective-permute-done | bytes 131104 | tf_op jit(solution)/shard_map/ppermute | solution.py:685
  27.6 0.0 collective-permute-done.6.other_ref
  27.6 2.5 %shard_map.252 = (f32[64,512]{1,0:T(8,128)S(1)}, f32[1,64,512]{2,1,0:T(8,128)S(1)}, f32[64,512]{1,0:T(8,128)S(1)}, f32[64,512]{1,0:T(8,128)S(1)}, f32[80,128]{1,0:T(8,128)S(1)}, /*index=5*/f32[80,128]{1,0:T(8,128)S(1)}) custom-call(f32[64,512]{1,0:T(8,128)S(1)} %get-tuple-element.113.hid0_ref, f32[64,512]{1,0:T(8,128)S(1)} %collective-permute-done.7.hid1_ref, ...), custom_call_target="tpu_custom_call" | custom-call | tf_op jit(solution)/shard_map/pallas_call | solution.py:673
  30.1 0.6 collective-permute-start.10
  30.7 0.0 collective-permute-done.5.hid1_ref
  30.7 2.5 %shard_map.253 = (f32[64,512]{1,0:T(8,128)S(1)}, f32[2,64,512]{2,1,0:T(8,128)S(1)}, f32[64,512]{1,0:T(8,128)S(1)}, f32[64,512]{1,0:T(8,128)S(1)}, f32[80,128]{1,0:T(8,128)S(1)}, /*index=5*/f32[80,128]{1,0:T(8,128)S(1)}) custom-call(f32[64,512]{1,0:T(8,128)S(1)} %get-tuple-element.106.hid0_ref, f32[64,512]{1,0:T(8,128)S(1)} %collective-permute-done.5.hid1_ref, ...), custom_call_target="tpu_custom_call" | custom-call | tf_op jit(solution)/shard_map/pallas_call | solution.py:673
  33.3 1.5 %collective-permute-start.9 = (f32[64,512]{1,0:T(8,128)S(1)}, f32[64,512]{1,0:T(8,128)S(1)}, u32[]{:S(2)}, u32[]{:S(2)}) collective-permute-start(f32[64,512]{1,0:T(8,128)S(1)} %get-tuple-element.121), channel_id=1, source_target_pairs={{0,1},{1,0},{2,3},{3,2},{4,5},{5,4},{6,7},{7,6},{8,9},{9,8},{10,11... | collective-permute-start | bytes 393224 | tf_op jit(solution)/shard_map/ppermute | solution.py:685
  34.8 1.3 %shard_map.255 = (f32[2,64,512]{2,1,0:T(8,128)S(1)}, f32[2,64,512]{2,1,0:T(8,128)S(1)}, f32[128,512]{1,0:T(8,128)S(1)}) custom-call(s32[1]{0:T(128)} %bitcast.view_ref, s32[1]{0:T(128)} %bitcast.3.slot_ref, f32[4,64,512]{2,1,0:T(8,128)S(1)} %get-tuple-element.97.gating_ref, f32[2,64,512]{2,1,0:T(8,128)S(1)} %get-tuple-element.125.one_ref, ...), custom_call_target="tpu_custom_call" | custom-call | tf_op jit(solution)/shard_map/pallas_call | solution.py:673
  36.1 0.0 collective-permute-done.10.refs_0_
  36.1 0.7 shard_map.256
  36.8 1.5 %collective-permute-done.9.refs_0_ = f32[64,512]{1,0:T(8,128)S(1)} collective-permute-done((f32[64,512]{1,0:T(8,128)S(1)}, f32[64,512]{1,0:T(8,128)S(1)}, u32[]{:S(2)}, u32[]{:S(2)}) %collective-permute-start.9) | collective-permute-done | bytes 131104 | tf_op jit(solution)/shard_map/ppermute | solution.py:685
  38.3 0.9 %shard_map.257 = (f32[1,64,512]{2,1,0:T(8,128)S(1)}, f32[1,64,512]{2,1,0:T(8,128)S(1)}, f32[8,128]{1,0:T(8,128)S(1)}, f32[144,128]{1,0:T(8,128)S(1)}) custom-call(s32[1]{0:T(128)} %bitcast.view_ref, s32[1]{0:T(128)} %bitcast.3.slot_ref, f32[4,64,512]{2,1,0:T(8,128)S(1)} %get-tuple-element.97.gating_ref, f32[1,64,512]{2,1,0:T(8,128)S(1)} %get-tuple-element.119.one_ref, ...), custom_call_target="tpu_custom_call" | custom-call | tf_op jit(solution)/shard_map/pallas_call | solution.py:673
  39.2 2.9 %collective-permute-start.13 = (f32[8,128]{1,0:T(8,128)S(1)}, f32[8,128]{1,0:T(8,128)S(1)}, u32[]{:S(2)}, u32[]{:S(2)}) collective-permute-start(f32[8,128]{1,0:T(8,128)S(1)} %get-tuple-element.131.refs_0_), channel_id=1, source_target_pairs={{0,6},{2,4},{4,2},{6,0},{1,7},{3,5},{5,3},{7,1},{8,14},{10,12},{12... | collective-permute-start | bytes 12296 | tf_op jit(solution)/shard_map/ppermute | solution.py:685
  42.1 0.0 collective-permute-start.12
  42.1 1.5 %collective-permute-start.11 = (f32[8,128]{1,0:T(8,128)S(1)}, f32[8,128]{1,0:T(8,128)S(1)}, u32[]{:S(2)}, u32[]{:S(2)}) collective-permute-start(f32[8,128]{1,0:T(8,128)S(1)} %get-tuple-element.131.refs_0_), channel_id=1, source_target_pairs={{0,2},{2,0},{4,6},{6,4},{1,3},{3,1},{5,7},{7,5},{8,10},{10,8},{12,... | collective-permute-start | bytes 12296 | tf_op jit(solution)/shard_map/ppermute | solution.py:685
  43.7 1.0 %collective-permute-done.13.refs_3_ = f32[8,128]{1,0:T(8,128)S(1)} collective-permute-done((f32[8,128]{1,0:T(8,128)S(1)}, f32[8,128]{1,0:T(8,128)S(1)}, u32[]{:S(2)}, u32[]{:S(2)}) %collective-permute-start.13) | collective-permute-done | bytes 4128 | tf_op jit(solution)/shard_map/ppermute | solution.py:685
  44.7 1.9 %collective-permute-done.12.refs_2_ = f32[8,128]{1,0:T(8,128)S(1)} collective-permute-done((f32[8,128]{1,0:T(8,128)S(1)}, f32[8,128]{1,0:T(8,128)S(1)}, u32[]{:S(2)}, u32[]{:S(2)}) %collective-permute-start.12) | collective-permute-done | bytes 4128 | tf_op jit(solution)/shard_map/ppermute | solution.py:685
  46.6 0.0 collective-permute-done.11.refs_1_
  46.6 3.3 %shard_map.258 = (f32[4,64,512]{2,1,0:T(8,128)S(1)}, f32[64,512]{1,0:T(8,128)S(1)}, f32[64,512]{1,0:T(8,128)S(1)}, f32[192,128]{1,0:T(8,128)S(1)}, f32[192,128]{1,0:T(8,128)S(1)}) custom-call(s32[1]{0:T(128)} %bitcast.view_ref, s32[1]{0:T(128)} %bitcast.1.core_ref, s32[1]{0:T(128)} %bitcast.2.odd_ref, f32[8,128]{1,0:T(8,128)S(1)} %get-tuple-element.131.refs_0_, ...), custom_call_target="tpu_custom_call" | custom-call | tf_op jit(solution)/shard_map/pallas_call | solution.py:673
  50.0 0.1 collective-permute-start.16
  50.0 1.3 %collective-permute-done.16.other_ref = f32[192,128]{1,0:T(8,128)S(1)} collective-permute-done((f32[192,128]{1,0:T(8,128)S(1)}, f32[192,128]{1,0:T(8,128)S(1)}, u32[]{:S(2)}, u32[]{:S(2)}) %collective-permute-start.16) | collective-permute-done | bytes 98336 | tf_op jit(solution)/shard_map/ppermute | solution.py:685
  51.3 1.6 %collective-permute-start.17 = (f32[152,128]{1,0:T(8,128)S(1)}, f32[152,128]{1,0:T(8,128)S(1)}, u32[]{:S(2)}, u32[]{:S(2)}) collective-permute-start(f32[152,128]{1,0:T(8,128)S(1)} %get-tuple-element.153), channel_id=1, source_target_pairs={{0,1},{1,0},{2,3},{3,2},{4,5},{5,4},{6,7},{7,6},{8,9},{9,8},{10,11... | collective-permute-start | bytes 233480 | tf_op jit(solution)/shard_map/ppermute | solution.py:685
  52.9 2.9 %collective-permute-done.17.other_ref = f32[152,128]{1,0:T(8,128)S(1)} collective-permute-done((f32[152,128]{1,0:T(8,128)S(1)}, f32[152,128]{1,0:T(8,128)S(1)}, u32[]{:S(2)}, u32[]{:S(2)}) %collective-permute-start.17) | collective-permute-done | bytes 77856 | tf_op jit(solution)/shard_map/ppermute | solution.py:685
  55.8 1.6 %collective-permute-start.18 = (f32[152,128]{1,0:T(8,128)S(1)}, f32[152,128]{1,0:T(8,128)S(1)}, u32[]{:S(2)}, u32[]{:S(2)}) collective-permute-start(f32[152,128]{1,0:T(8,128)S(1)} %shard_map.261.mine_ref), channel_id=1, source_target_pairs={{0,16},{8,24},{16,0},{24,8},{1,17},{9,25},{17,1},{25,9},{2,18},{10... | collective-permute-start | bytes 233480 | tf_op jit(solution)/shard_map/ppermute | solution.py:685
  57.4 1.5 %collective-permute-start.8 = (f32[2,64,512]{2,1,0:T(8,128)S(1)}, f32[2,64,512]{2,1,0:T(8,128)S(1)}, u32[]{:S(2)}, u32[]{:S(2)}) collective-permute-start(f32[2,64,512]{2,1,0:T(8,128)S(1)} %get-tuple-element.116), channel_id=1, source_target_pairs={{0,1},{1,0},{2,3},{3,2},{4,5},{5,4},{6,7},{7,6},{8,9},{9,8},{10,11... | collective-permute-start | bytes 786440 | tf_op jit(solution)/shard_map/ppermute | solution.py:685
  58.9 1.4 %collective-permute-done.18.other_ref = f32[152,128]{1,0:T(8,128)S(1)} collective-permute-done((f32[152,128]{1,0:T(8,128)S(1)}, f32[152,128]{1,0:T(8,128)S(1)}, u32[]{:S(2)}, u32[]{:S(2)}) %collective-permute-start.18) | collective-permute-done | bytes 77856 | tf_op jit(solution)/shard_map/ppermute | solution.py:685
  60.3 0.7 collective-permute-start.19
  61.0 3.8 %collective-permute-done.19.other_ref = f32[152,128]{1,0:T(8,128)S(1)} collective-permute-done((f32[152,128]{1,0:T(8,128)S(1)}, f32[152,128]{1,0:T(8,128)S(1)}, u32[]{:S(2)}, u32[]{:S(2)}) %collective-permute-start.19) | collective-permute-done | bytes 77856 | tf_op jit(solution)/shard_map/ppermute | solution.py:685
  64.8 2.6 %collective-permute-start.20 = (f32[152,128]{1,0:T(8,128)S(1)}, f32[152,128]{1,0:T(8,128)S(1)}, u32[]{:S(2)}, u32[]{:S(2)}) collective-permute-start(f32[152,128]{1,0:T(8,128)S(1)} %shard_map.263.mine_ref), channel_id=1, source_target_pairs={{0,4},{2,6},{4,0},{6,2},{1,5},{3,7},{5,1},{7,3},{8,12},{10,14},{12... | collective-permute-start | bytes 233480 | tf_op jit(solution)/shard_map/ppermute | solution.py:685
  67.4 0.0 collective-permute-start.14
  67.4 0.7 collective-permute-start.15
  68.1 3.6 %collective-permute-done.20.other_ref = f32[152,128]{1,0:T(8,128)S(1)} collective-permute-done((f32[152,128]{1,0:T(8,128)S(1)}, f32[152,128]{1,0:T(8,128)S(1)}, u32[]{:S(2)}, u32[]{:S(2)}) %collective-permute-start.20) | collective-permute-done | bytes 77856 | tf_op jit(solution)/shard_map/ppermute | solution.py:685
  71.7 0.1 collective-permute-start.21
  71.7 0.0 collective-permute-done.8.sent_ref
  71.8 0.9 %shard_map.254 = f32[64,4,480]{2,1,0:T(4,128)} custom-call(s32[1]{0:T(128)} %bitcast.view_ref, f32[2,64,512]{2,1,0:T(8,128)S(1)} %collective-permute-done.8.sent_ref, f32[64,512]{1,0:T(8,128)S(1)} %get-tuple-element.117.refs_0_, f32[64,512]{1,0:T(8,128)S(1)} %get-tuple-element.118.refs_1_), custom_call_target="tpu_custom_call" | custom-call | tf_op jit(solution)/shard_map/pallas_call | solution.py:673
  72.7 0.0 collective-permute-done.14.first_ref
  72.7 0.0 collective-permute-done.15.second_ref
  72.7 1.3 %shard_map.259 = f32[64,4,480]{2,1,0:T(4,128)} custom-call(s32[1]{0:T(128)} %bitcast.view_ref, s32[1]{0:T(128)} %bitcast.2.odd_ref, f32[4,64,512]{2,1,0:T(8,128)S(1)} %get-tuple-element.144.dn_ref, f32[64,512]{1,0:T(8,128)S(1)} %collective-permute-done.14.first_ref, f32[64,512]{1,0:T(8,128)S(1)} %collective-permute-done.15.second_ref, ...), custom_call_target="tpu_custom_call" | custom-call | tf_op jit(solution)/shard_map/pallas_call | solution.py:673
  74.1 0.0 collective-permute-done.21.theirs_ref
  74.1 0.9 %shard_map.265 = (f32[64,128]{1,0:T(8,128)}, f32[64,64]{1,0:T(8,128)}, f32[64,64]{1,0:T(8,128)}, f32[64,64]{1,0:T(8,128)}, f32[1,64]{1,0:T(1,128)}, /*index=5*/f...) custom-call(s32[1]{0:T(128)} %bitcast.1.core_ref, ...), custom_call_target="tpu_custom_call" | custom-call | tf_op jit(solution)/shard_map/pallas_call | solution.py:673
  (9 shorter events, 0.1 us)
Async XLA Ops:
  0.7 1.0 %copy-start = (f32[1,1,64,4,480]{4,3,2,1,0:T(4,128)S(1)}, f32[1,1,64,4,480]{4,3,2,1,0:T(4,128)}, u32[]{:S(2)}) copy-start(f32[1,1,64,4,480]{4,3,2,1,0:T(4,128)} %param.15) | copy-start | bytes 1474564
  1.7 4.2 %copy-start.1 = (f32[1,1,64,4,480]{4,3,2,1,0:T(4,128)S(1)}, f32[1,1,64,4,480]{4,3,2,1,0:T(4,128)}, u32[]{:S(2)}) copy-start(f32[1,1,64,4,480]{4,3,2,1,0:T(4,128)} %param.14) | copy-start | bytes 1474564
  2.8 24.8 %collective-permute-start.6 = (f32[152,512]{1,0:T(8,128)S(1)}, f32[152,512]{1,0:T(8,128)S(1)}, u32[]{:S(2)}, u32[]{:S(2)}) collective-permute-start(f32[152,512]{1,0:T(8,128)S(1)} %get-tuple-element.112), channel_id=1, source_target_pairs={{0,1},{1,0},{2,3},{3,2},{4,5},{5,4},{6,7},{7,6},{8,9},{9,8},{10,11... | collective-permute-start | bytes 933896 | tf_op jit(solution)/shard_map/ppermute | solution.py:685
  5.9 2.5 %copy-start.2 = (f32[128,64]{0,1:T(8,128)S(1)}, f32[128,64]{0,1:T(8,128)}, u32[]{:S(2)}) copy-start(f32[128,64]{0,1:T(8,128)} %param.16) | copy-start | bytes 98308
  6.0 2.3 %copy-start.3 = (f32[128,3,3]{0,2,1:T(4,128)S(1)}, f32[128,3,3]{0,2,1:T(4,128)}, u32[]{:S(2)}) copy-start(f32[128,3,3]{0,2,1:T(4,128)} %param.17) | copy-start | bytes 13828
  6.0 5.0 %collective-permute-start = (f32[64,512]{1,0:T(8,128)S(1)}, f32[64,512]{1,0:T(8,128)S(1)}, u32[]{:S(2)}, u32[]{:S(2)}) collective-permute-start(f32[64,512]{1,0:T(8,128)S(1)} %get-tuple-element.95), channel_id=1, source_target_pairs={{0,2},{2,0},{4,6},{6,4},{1,3},{3,1},{5,7},{7,5},{8,10},{10,8},{12,... | collective-permute-start | bytes 393224 | tf_op jit(solution)/shard_map/ppermute | solution.py:752
  7.6 3.4 %collective-permute-start.1 = (f32[64,512]{1,0:T(8,128)S(1)}, f32[64,512]{1,0:T(8,128)S(1)}, u32[]{:S(2)}, u32[]{:S(2)}) collective-permute-start(f32[64,512]{1,0:T(8,128)S(1)} %get-tuple-element.96), channel_id=1, source_target_pairs={{2,4},{4,2},{3,5},{5,3},{10,12},{12,10},{11,13},{13,11},{18,20},{2... | collective-permute-start | bytes 393224 | tf_op jit(solution)/shard_map/ppermute | solution.py:752
  12.1 6.6 %collective-permute-start.4 = (f32[8,128]{1,0:T(8,128)S(1)}, f32[8,128]{1,0:T(8,128)S(1)}, u32[]{:S(2)}, u32[]{:S(2)}) collective-permute-start(f32[8,128]{1,0:T(8,128)S(1)} %get-tuple-element.98.refs_0_.refs_2_.refs_1_.refs_13_), channel_id=1, source_target_pairs={{0,6},{2,4},{4,2},{6,0},{1,7},{3,5},{5,3},{7,1},{8,14},{10,12},{12... | collective-permute-start | bytes 12296 | tf_op jit(solution)/shard_map/ppermute | solution.py:685
  15.7 4.5 %collective-permute-start.3 = (f32[8,128]{1,0:T(8,128)S(1)}, f32[8,128]{1,0:T(8,128)S(1)}, u32[]{:S(2)}, u32[]{:S(2)}) collective-permute-start(f32[8,128]{1,0:T(8,128)S(1)} %get-tuple-element.98.refs_0_.refs_2_.refs_1_.refs_13_), channel_id=1, source_target_pairs={{0,4},{2,6},{4,0},{6,2},{1,5},{3,7},{5,1},{7,3},{8,12},{10,14},{12... | collective-permute-start | bytes 12296 | tf_op jit(solution)/shard_map/ppermute | solution.py:685
  18.2 3.6 %collective-permute-start.2 = (f32[8,128]{1,0:T(8,128)S(1)}, f32[8,128]{1,0:T(8,128)S(1)}, u32[]{:S(2)}, u32[]{:S(2)}) collective-permute-start(f32[8,128]{1,0:T(8,128)S(1)} %get-tuple-element.98.refs_0_.refs_2_.refs_1_.refs_13_), channel_id=1, source_target_pairs={{0,2},{2,0},{4,6},{6,4},{1,3},{3,1},{5,7},{7,5},{8,10},{10,8},{12,... | collective-permute-start | bytes 12296 | tf_op jit(solution)/shard_map/ppermute | solution.py:685
  22.6 5.0 %collective-permute-start.7 = (f32[64,512]{1,0:T(8,128)S(1)}, f32[64,512]{1,0:T(8,128)S(1)}, u32[]{:S(2)}, u32[]{:S(2)}) collective-permute-start(f32[64,512]{1,0:T(8,128)S(1)} %get-tuple-element.114), channel_id=1, source_target_pairs={{0,1},{1,0},{2,3},{3,2},{4,5},{5,4},{6,7},{7,6},{8,9},{9,8},{10,11... | collective-permute-start | bytes 393224 | tf_op jit(solution)/shard_map/ppermute | solution.py:685
  23.9 6.8 %collective-permute-start.5 = (f32[64,512]{1,0:T(8,128)S(1)}, f32[64,512]{1,0:T(8,128)S(1)}, u32[]{:S(2)}, u32[]{:S(2)}) collective-permute-start(f32[64,512]{1,0:T(8,128)S(1)} %get-tuple-element.107), channel_id=1, source_target_pairs={{0,1},{1,0},{2,3},{3,2},{4,5},{5,4},{6,7},{7,6},{8,9},{9,8},{10,11... | collective-permute-start | bytes 393224 | tf_op jit(solution)/shard_map/ppermute | solution.py:685
  30.1 6.0 %collective-permute-start.10 = (f32[64,512]{1,0:T(8,128)S(1)}, f32[64,512]{1,0:T(8,128)S(1)}, u32[]{:S(2)}, u32[]{:S(2)}) collective-permute-start(f32[64,512]{1,0:T(8,128)S(1)} %get-tuple-element.124), channel_id=1, source_target_pairs={{0,1},{1,0},{2,3},{3,2},{4,5},{5,4},{6,7},{7,6},{8,9},{9,8},{10,11... | collective-permute-start | bytes 393224 | tf_op jit(solution)/shard_map/ppermute | solution.py:685
  33.3 5.0 %collective-permute-start.9 = (f32[64,512]{1,0:T(8,128)S(1)}, f32[64,512]{1,0:T(8,128)S(1)}, u32[]{:S(2)}, u32[]{:S(2)}) collective-permute-start(f32[64,512]{1,0:T(8,128)S(1)} %get-tuple-element.121), channel_id=1, source_target_pairs={{0,1},{1,0},{2,3},{3,2},{4,5},{5,4},{6,7},{7,6},{8,9},{9,8},{10,11... | collective-permute-start | bytes 393224 | tf_op jit(solution)/shard_map/ppermute | solution.py:685
  39.2 5.5 %collective-permute-start.13 = (f32[8,128]{1,0:T(8,128)S(1)}, f32[8,128]{1,0:T(8,128)S(1)}, u32[]{:S(2)}, u32[]{:S(2)}) collective-permute-start(f32[8,128]{1,0:T(8,128)S(1)} %get-tuple-element.131.refs_0_), channel_id=1, source_target_pairs={{0,6},{2,4},{4,2},{6,0},{1,7},{3,5},{5,3},{7,1},{8,14},{10,12},{12... | collective-permute-start | bytes 12296 | tf_op jit(solution)/shard_map/ppermute | solution.py:685
  42.1 4.5 %collective-permute-start.12 = (f32[8,128]{1,0:T(8,128)S(1)}, f32[8,128]{1,0:T(8,128)S(1)}, u32[]{:S(2)}, u32[]{:S(2)}) collective-permute-start(f32[8,128]{1,0:T(8,128)S(1)} %get-tuple-element.131.refs_0_), channel_id=1, source_target_pairs={{0,4},{2,6},{4,0},{6,2},{1,5},{3,7},{5,1},{7,3},{8,12},{10,14},{12... | collective-permute-start | bytes 12296 | tf_op jit(solution)/shard_map/ppermute | solution.py:685
  42.1 4.5 %collective-permute-start.11 = (f32[8,128]{1,0:T(8,128)S(1)}, f32[8,128]{1,0:T(8,128)S(1)}, u32[]{:S(2)}, u32[]{:S(2)}) collective-permute-start(f32[8,128]{1,0:T(8,128)S(1)} %get-tuple-element.131.refs_0_), channel_id=1, source_target_pairs={{0,2},{2,0},{4,6},{6,4},{1,3},{3,1},{5,7},{7,5},{8,10},{10,8},{12,... | collective-permute-start | bytes 12296 | tf_op jit(solution)/shard_map/ppermute | solution.py:685
  50.0 1.4 %collective-permute-start.16 = (f32[192,128]{1,0:T(8,128)S(1)}, f32[192,128]{1,0:T(8,128)S(1)}, u32[]{:S(2)}, u32[]{:S(2)}) collective-permute-start(f32[192,128]{1,0:T(8,128)S(1)} %get-tuple-element.151), channel_id=1, source_target_pairs={{0,8},{8,0},{16,24},{24,16},{1,9},{9,1},{17,25},{25,17},{2,10},{10... | collective-permute-start | bytes 294920 | tf_op jit(solution)/shard_map/ppermute | solution.py:685
  51.3 4.5 %collective-permute-start.17 = (f32[152,128]{1,0:T(8,128)S(1)}, f32[152,128]{1,0:T(8,128)S(1)}, u32[]{:S(2)}, u32[]{:S(2)}) collective-permute-start(f32[152,128]{1,0:T(8,128)S(1)} %get-tuple-element.153), channel_id=1, source_target_pairs={{0,1},{1,0},{2,3},{3,2},{4,5},{5,4},{6,7},{7,6},{8,9},{9,8},{10,11... | collective-permute-start | bytes 233480 | tf_op jit(solution)/shard_map/ppermute | solution.py:685
  55.8 4.5 %collective-permute-start.18 = (f32[152,128]{1,0:T(8,128)S(1)}, f32[152,128]{1,0:T(8,128)S(1)}, u32[]{:S(2)}, u32[]{:S(2)}) collective-permute-start(f32[152,128]{1,0:T(8,128)S(1)} %shard_map.261.mine_ref), channel_id=1, source_target_pairs={{0,16},{8,24},{16,0},{24,8},{1,17},{9,25},{17,1},{25,9},{2,18},{10... | collective-permute-start | bytes 233480 | tf_op jit(solution)/shard_map/ppermute | solution.py:685
  57.4 14.3 %collective-permute-start.8 = (f32[2,64,512]{2,1,0:T(8,128)S(1)}, f32[2,64,512]{2,1,0:T(8,128)S(1)}, u32[]{:S(2)}, u32[]{:S(2)}) collective-permute-start(f32[2,64,512]{2,1,0:T(8,128)S(1)} %get-tuple-element.116), channel_id=1, source_target_pairs={{0,1},{1,0},{2,3},{3,2},{4,5},{5,4},{6,7},{7,6},{8,9},{9,8},{10,11... | collective-permute-start | bytes 786440 | tf_op jit(solution)/shard_map/ppermute | solution.py:685
  60.3 4.5 %collective-permute-start.19 = (f32[152,128]{1,0:T(8,128)S(1)}, f32[152,128]{1,0:T(8,128)S(1)}, u32[]{:S(2)}, u32[]{:S(2)}) collective-permute-start(f32[152,128]{1,0:T(8,128)S(1)} %shard_map.262.mine_ref), channel_id=1, source_target_pairs={{0,2},{2,0},{4,6},{6,4},{1,3},{3,1},{5,7},{7,5},{8,10},{10,8},{12,... | collective-permute-start | bytes 233480 | tf_op jit(solution)/shard_map/ppermute | solution.py:685
  64.8 6.9 %collective-permute-start.20 = (f32[152,128]{1,0:T(8,128)S(1)}, f32[152,128]{1,0:T(8,128)S(1)}, u32[]{:S(2)}, u32[]{:S(2)}) collective-permute-start(f32[152,128]{1,0:T(8,128)S(1)} %shard_map.263.mine_ref), channel_id=1, source_target_pairs={{0,4},{2,6},{4,0},{6,2},{1,5},{3,7},{5,1},{7,3},{8,12},{10,14},{12... | collective-permute-start | bytes 233480 | tf_op jit(solution)/shard_map/ppermute | solution.py:685
  67.4 5.3 %collective-permute-start.14 = (f32[64,512]{1,0:T(8,128)S(1)}, f32[64,512]{1,0:T(8,128)S(1)}, u32[]{:S(2)}, u32[]{:S(2)}) collective-permute-start(f32[64,512]{1,0:T(8,128)S(1)} %get-tuple-element.145), channel_id=1, source_target_pairs={{0,2},{2,0},{4,6},{6,4},{1,3},{3,1},{5,7},{7,5},{8,10},{10,8},{12,... | collective-permute-start | bytes 393224 | tf_op jit(solution)/shard_map/ppermute | solution.py:752
  67.4 5.3 %collective-permute-start.15 = (f32[64,512]{1,0:T(8,128)S(1)}, f32[64,512]{1,0:T(8,128)S(1)}, u32[]{:S(2)}, u32[]{:S(2)}) collective-permute-start(f32[64,512]{1,0:T(8,128)S(1)} %get-tuple-element.146), channel_id=1, source_target_pairs={{2,4},{4,2},{3,5},{5,3},{10,12},{12,10},{11,13},{13,11},{18,20},{2... | collective-permute-start | bytes 393224 | tf_op jit(solution)/shard_map/ppermute | solution.py:752
  71.7 2.4 %collective-permute-start.21 = (f32[152,128]{1,0:T(8,128)S(1)}, f32[152,128]{1,0:T(8,128)S(1)}, u32[]{:S(2)}, u32[]{:S(2)}) collective-permute-start(f32[152,128]{1,0:T(8,128)S(1)} %shard_map.264.mine_ref), channel_id=1, source_target_pairs={{0,8},{8,0},{16,24},{24,16},{1,9},{9,1},{17,25},{25,17},{2,10},{10... | collective-permute-start | bytes 233480 | tf_op jit(solution)/shard_map/ppermute | solution.py:685
